TPU v7x, 512 devices: a whole 4x8x8 slice. The times are simulated.
512 devices in a mesh: prow: 32 (over y, x), pcol: 16 (over z, core).
Axes of the slice: x: 4, y: 8, z: 8, core: 2. Of those that a mesh axis runs over, the one named last changes fastest.
Arguments:
- matrix: bfloat16 [4, 8192, 4, 4096], P(None, 'prow', None, 'pcol'), may hold values from -6 to 6
- pivots: int32 [2, 256], replicated, may hold values from 0 to 32767, as said below
- lower_inverse: bfloat16 [2, 256, 256], replicated, as said below
- upper_inverse: bfloat16 [2, 256, 256], replicated, as said below
Outputs:
- factored: bfloat16 [4, 8192, 4, 4096], P(None, 'prow', None, 'pcol')
Inputs may be any that keep to these rules, and one draw needn't show every extreme that they name: For each panel k and each i, pivots[k, i] is either k * 256 + i or a row at or after (k + 1) * 256; entry 0 of each list is k * 256; the rows of one panel's list are distinct, and each list names row 32767. Each lower_inverse[k] is unit lower triangular. Each upper_inverse[k] is upper triangular with positive diagonal.
All inputs are finite; a program needn't handle non-finite values.
Results may differ from a plain program's by a relative error of at most 0.0079.
Values may be sent and summed in bfloat16 or wider, within the bound.
A program may use at most 64 MiB of HBM per device.

v0:
```python
import jax
import jax.numpy as jnp
from jax import lax
from jax.sharding import PartitionSpec as P


def spread(block, axis, source):
    block = jnp.where(lax.axis_index(axis) == source, block, jnp.zeros_like(block))
    return lax.psum(block, axis)


def local(matrix, pivots, lower_inverse, upper_inverse):
    row_count = lax.axis_size("prow")
    col_count = lax.axis_size("pcol")
    my_row = lax.axis_index("prow")
    my_col = lax.axis_index("pcol")
    blocks_down, block, blocks_across, _ = matrix.shape
    local_rows = blocks_down * block
    local_cols = blocks_across * block
    current = matrix.reshape(local_rows, local_cols)
    row_place = jnp.arange(local_rows)
    col_place = jnp.arange(local_cols)
    global_rows = (row_place // block * row_count + my_row) * block + row_place % block
    global_cols = (col_place // block * col_count + my_col) * block + col_place % block
    for panel in range(pivots.shape[0]):
        start = panel * block
        chosen = pivots[panel]
        block_row = chosen // block
        is_mine = block_row % row_count == my_row
        local_index = block_row // row_count * block + chosen % block
        safe_index = jnp.where(is_mine, local_index, 0)
        picked = jnp.where(is_mine[:, None], current[safe_index], jnp.zeros((), jnp.bfloat16))
        top_holder = panel % row_count
        top_first = panel // row_count * block
        is_top = my_row == top_holder
        top_local = current[top_first : top_first + block]
        incoming = lax.psum(picked, "prow").astype(jnp.float32)
        old_top = spread(top_local, "prow", top_holder)
        incoming = incoming.astype(jnp.bfloat16)
        target = jnp.where(is_mine, local_index, local_rows)
        current = current.at[target].set(old_top, mode="drop")
        top_now = current[top_first : top_first + block]
        current = current.at[top_first : top_first + block].set(
            jnp.where(is_top, incoming, top_now)
        )
        panel_holder = panel % col_count
        panel_first = panel // col_count * block
        panel_cols = current[:, panel_first : panel_first + block]
        factor = jnp.dot(
            panel_cols, upper_inverse[panel], preferred_element_type=jnp.float32
        ).astype(jnp.bfloat16)
        lower = spread(factor, "pcol", panel_holder)
        top_rows_now = current[top_first : top_first + block]
        upper_local = jnp.dot(
            lower_inverse[panel], top_rows_now, preferred_element_type=jnp.float32
        ).astype(jnp.bfloat16)
        upper = spread(upper_local, "prow", top_holder)
        row_mask = global_rows >= start + block
        col_mask = global_cols >= start + block
        product = jnp.dot(lower, upper, preferred_element_type=jnp.float32)
        changed = (current.astype(jnp.float32) - product).astype(jnp.bfloat16)
        current = jnp.where(row_mask[:, None] & col_mask[None, :], changed, current)
        panel_now = current[:, panel_first : panel_first + block]
        is_panel = my_col == panel_holder
        current = current.at[:, panel_first : panel_first + block].set(
            jnp.where(is_panel & row_mask[:, None], lower, panel_now)
        )
        top_now = current[top_first : top_first + block]
        current = current.at[top_first : top_first + block].set(
            jnp.where(is_top & col_mask[None, :], upper, top_now)
        )
    return current.reshape(matrix.shape)


def solution(mesh):
    in_specs = (P(None, "prow", None, "pcol"), P(), P(), P())
    out_specs = P(None, "prow", None, "pcol")
    return jax.shard_map(local, mesh=mesh, in_specs=in_specs, out_specs=out_specs, check_vma=False)
```

profile of v0, /device:TPU:1, one launch (start us, length us, event | category | flops | bytes accessed | tf_op | source)
XLA Modules:
  0.0 932.4 jit_solution(9245979962297047601)
XLA Ops:
  6.5 0.0 all-reduce.19.cloned.1.call-start
  6.5 0.8 and_select_fusion.5
  7.3 0.8 fusion.48
  8.1 2.1 copy.23
  10.2 1.3 slice_select_fusion.4
  11.5 0.9 copy.24
  12.4 1.2 gather_fusion
  13.5 0.9 broadcast_select_fusion.1
  14.5 0.0 all-reduce.19.cloned.1.call-update
  14.5 0.0 all-reduce.9.cloned.1.call-start
  14.6 161.5 %all-reduce.19.cloned.1.call-done = (bf16[256,1024]{1,0:T(8,128)(2,1)}, bf16[256,1024]{1,0:T(8,128)(2,1)}) async-done(((bf16[256,1024]{1,0:T(8,128)(2,1)}, bf16[256,1024]{1,0:T(8,128)(2,1)}), (bf16[256,1024]{1,0:T(8,128)(2,1)}, bf16[256,1024]{1,0:T(8,128)(2,1)})) %all-reduce.19.cloned.1.call-update) | async-done | bytes 1048592 | tf_op jit(solution)/shard_map/psum | solution.py:9
  176.1 0.0 copy-start.1
  176.1 0.0 copy-start.4
  176.1 3.3 scatter_fusion
  179.5 0.0 copy-start.5
  179.5 0.0 copy-done.1
  179.5 0.0 copy-done.4
  179.5 1.1 fusion.3
  180.6 0.2 fusion.10
  180.8 0.0 copy-done.5
  180.8 1.1 fusion
  181.9 0.0 all-reduce.9.cloned.1.call-update
  182.0 0.0 all-reduce.11.cloned.1.call-start
  182.0 0.7 compare_reduce_fusion
  182.7 0.0 all-reduce.11.cloned.1.call-update
  182.8 0.0 all-reduce.17.cloned.1.call-start
  182.9 117.1 %all-reduce.9.cloned.1.call-done = bf16[1024,256]{1,0:T(8,128)(2,1)} async-done(((bf16[1024,256]{1,0:T(8,128)(2,1)}), bf16[1024,256]{1,0:T(8,128)(2,1)}) %all-reduce.9.cloned.1.call-update) | async-done | bytes 524304 | tf_op jit(solution)/shard_map/psum | solution.py:9
  300.0 157.3 %all-reduce.11.cloned.1.call-done = bf16[256,1024]{1,0:T(8,128)(2,1)} async-done(((bf16[256,1024]{1,0:T(8,128)(2,1)}), bf16[256,1024]{1,0:T(8,128)(2,1)}) %all-reduce.11.cloned.1.call-update) | async-done | bytes 524304 | tf_op jit(solution)/shard_map/psum | solution.py:9
  457.3 0.0 copy-start
  457.3 0.0 copy-start.3
  457.3 3.6 and_select_fusion
  460.9 0.0 copy-done
  460.9 2.9 fusion.6
  463.8 0.0 copy-done.3
  463.8 2.3 broadcast_select_fusion.2
  466.1 3.4 gather_fusion.1
  469.6 0.9 broadcast_select_fusion
  470.5 0.0 all-reduce.17.cloned.1.call-update
  470.5 0.0 all-reduce.13.cloned.1.call-start
  470.6 157.9 %all-reduce.17.cloned.1.call-done = (bf16[256,1024]{1,0:T(8,128)(2,1)}, bf16[256,1024]{1,0:T(8,128)(2,1)}) async-done(((bf16[256,1024]{1,0:T(8,128)(2,1)}, bf16[256,1024]{1,0:T(8,128)(2,1)}), (bf16[256,1024]{1,0:T(8,128)(2,1)}, bf16[256,1024]{1,0:T(8,128)(2,1)})) %all-reduce.17.cloned.1.call-update) | async-done | bytes 1048592 | tf_op jit(solution)/shard_map/psum | solution.py:9
  628.5 0.0 copy-start.2
  628.5 5.4 scatter_fusion.1
  633.9 0.0 copy-done.2
  633.9 2.2 fusion.5
  636.1 2.0 fusion.11
  638.1 2.2 fusion.1
  640.3 0.0 all-reduce.13.cloned.1.call-update
  640.3 0.2 all-reduce.15.cloned.1.call-start
  640.5 0.3 all-reduce.15.cloned.1.call-update
  640.9 117.4 %all-reduce.13.cloned.1.call-done = bf16[1024,256]{0,1:T(8,128)(2,1)} async-done(((bf16[1024,256]{0,1:T(8,128)(2,1)}), bf16[1024,256]{0,1:T(8,128)(2,1)}) %all-reduce.13.cloned.1.call-update) | async-done | bytes 524304 | tf_op jit(solution)/shard_map/psum | solution.py:9
  758.3 157.2 %all-reduce.15.cloned.1.call-done = bf16[256,1024]{1,0:T(8,128)(2,1)} async-done(((bf16[256,1024]{1,0:T(8,128)(2,1)}), bf16[256,1024]{1,0:T(8,128)(2,1)}) %all-reduce.15.cloned.1.call-update) | async-done | bytes 524304 | tf_op jit(solution)/shard_map/psum | solution.py:9
  915.5 3.7 and_select_fusion.1
  919.2 0.1 slice.176
  919.3 0.2 copy.22
  919.5 1.8 select_select_fusion
  921.3 0.2 copy.18
  921.5 0.1 constant_dynamic-update-slice_fusion
  921.6 1.3 fusion.7
  922.8 2.8 reshape.658
  (14 shorter events, 0.2 us)
Async XLA Ops:
  6.5 169.6 %all-reduce.19.cloned.1.call-start = ((), (), s32[]{:S(2)}) async-start(), calls=%async_computation.5 | async-start | bytes 2097152 | tf_op jit(solution)/shard_map/psum | solution.py:9
  14.5 285.5 %all-reduce.9.cloned.1.call-start = ((), (), s32[]{:S(2)}) async-start(), calls=%async_computation | async-start | bytes 1048576 | tf_op jit(solution)/shard_map/psum | solution.py:9
  176.1 3.4 copy-start.1
  176.1 3.4 copy-start.4
  179.5 1.4 copy-start.5
  182.0 275.4 %all-reduce.11.cloned.1.call-start = ((), (), s32[]{:S(2)}) async-start(), calls=%async_computation.1 | async-start | bytes 1048576 | tf_op jit(solution)/shard_map/psum | solution.py:9
  182.8 445.7 %all-reduce.17.cloned.1.call-start = ((), (), s32[]{:S(2)}) async-start(), calls=%async_computation.4 | async-start | bytes 2097152 | tf_op jit(solution)/shard_map/psum | solution.py:9
  457.3 3.6 copy-start
  457.3 6.5 copy-start.3
  470.5 287.8 %all-reduce.13.cloned.1.call-start = ((), (), s32[]{:S(2)}) async-start(), calls=%async_computation.2 | async-start | bytes 1048576 | tf_op jit(solution)/shard_map/psum | solution.py:9
  628.5 5.4 copy-start.2
  640.3 275.2 %all-reduce.15.cloned.1.call-start = ((), (), s32[]{:S(2)}) async-start(), calls=%async_computation.3 | async-start | bytes 1048576 | tf_op jit(solution)/shard_map/psum | solution.py:9
Sparse Core Ops, SparseCore 0:
  14.6 161.4 all-reduce.18
  182.1 117.8 all-reduce.8
  303.8 153.5 all-reduce.10
  470.6 157.8 all-reduce.16
  640.4 117.8 all-reduce.12
  761.9 153.5 all-reduce.14
where the time goes:
time: 936 us; the launch traced here: 932 us
  waiting for transfers between devices  869 us (93%)
  local copies, waits for them, and re-layouts  20.3 us (2%)
  other arithmetic  15.3 us (2%)
  matrix products  13.9 us (1%)
  between operations  13.7 us (1%)
    psum x6, waiting for transfers between devices, spread(): return lax.psum(block, axis)  868 us
  transfers between devices with their start and end apart: 6, of which 6 were waited for; matrix products, arithmetic and copies ran while one was open for 0% of the time, Pallas kernels for 0%

commit v1 on v0

--- a/solution.py
+++ b/solution.py
@@ -50,11 +50,9 @@
             panel_cols, upper_inverse[panel], preferred_element_type=jnp.float32
         ).astype(jnp.bfloat16)
         lower = spread(factor, "pcol", panel_holder)
-        top_rows_now = current[top_first : top_first + block]
-        upper_local = jnp.dot(
-            lower_inverse[panel], top_rows_now, preferred_element_type=jnp.float32
+        upper = jnp.dot(
+            lower_inverse[panel], incoming, preferred_element_type=jnp.float32
         ).astype(jnp.bfloat16)
-        upper = spread(upper_local, "prow", top_holder)
         row_mask = global_rows >= start + block
         col_mask = global_cols >= start + block
         product = jnp.dot(lower, upper, preferred_element_type=jnp.float32)

time: 936 us -> 610 us (0.65)
  waiting for transfers between devices: 869 us -> 552 us
    psum x6 -> x4, waiting for transfers between devices: 868 us -> 552 us  [spread(): return lax.psum(block, axis)]
  transfers between devices with their start and end apart: 6 -> 4, of which waited for: 6 -> 4; matrix products, arithmetic and copies ran while one was open for 0% -> 0% of each run, Pallas kernels for 0% -> 0%
where the time goes in v1:
time: 610 us
  waiting for transfers between devices  552 us (90%)
  local copies, waits for them, and re-layouts  19.8 us (3%)
  other arithmetic  13.5 us (2%)
  between operations  13.3 us (2%)
  matrix products  10.8 us (2%)
    psum x4, waiting for transfers between devices, spread(): return lax.psum(block, axis)  552 us
  transfers between devices with their start and end apart: 4, of which 4 were waited for; matrix products, arithmetic and copies ran while one was open for 0% of the time, Pallas kernels for 0%

profile of v1, /device:TPU:1, one launch (start us, length us, event | category | flops | bytes accessed | tf_op | source)
XLA Modules:
  0.0 609.7 jit_solution(5548198204034712789)
XLA Ops:
  6.5 0.0 all-reduce.13.cloned.1.call-start
  6.5 0.8 and_select_fusion.5
  7.3 0.8 fusion.45
  8.1 2.1 copy.11
  10.2 1.3 slice_select_fusion.4
  11.5 0.9 copy.12
  12.4 1.2 gather_fusion
  13.5 0.9 broadcast_select_fusion.1
  14.5 0.0 all-reduce.13.cloned.1.call-update
  14.5 0.0 all-reduce.7.cloned.1.call-start
  14.6 161.5 %all-reduce.13.cloned.1.call-done = (bf16[256,1024]{1,0:T(8,128)(2,1)}, bf16[256,1024]{1,0:T(8,128)(2,1)}) async-done(((bf16[256,1024]{1,0:T(8,128)(2,1)}, bf16[256,1024]{1,0:T(8,128)(2,1)}), (bf16[256,1024]{1,0:T(8,128)(2,1)}, bf16[256,1024]{1,0:T(8,128)(2,1)})) %all-reduce.13.cloned.1.call-update) | async-done | bytes 1048592 | tf_op jit(solution)/shard_map/psum | solution.py:9
  176.1 0.0 copy-start
  176.1 0.0 copy-start.5
  176.1 3.3 scatter_fusion
  179.5 0.0 copy-start.4
  179.5 0.0 copy-done
  179.5 0.2 fusion.8
  179.7 0.0 copy-done.5
  179.7 1.1 fusion
  180.8 0.0 all-reduce.7.cloned.1.call-update
  180.8 0.0 all-reduce.11.cloned.1.call-start
  180.9 0.7 compare_reduce_fusion
  181.6 0.0 copy-done.4
  181.6 0.3 convolution_convert_fusion.1
  181.9 116.9 %all-reduce.7.cloned.1.call-done = bf16[1024,256]{1,0:T(8,128)(2,1)} async-done(((bf16[1024,256]{1,0:T(8,128)(2,1)}), bf16[1024,256]{1,0:T(8,128)(2,1)}) %all-reduce.7.cloned.1.call-update) | async-done | bytes 524304 | tf_op jit(solution)/shard_map/psum | solution.py:9
  298.9 0.0 copy-start.2
  298.9 3.4 and_select_fusion
  302.2 0.0 copy-done.2
  302.2 2.9 fusion.2
  305.2 2.3 broadcast_select_fusion.2
  307.5 3.4 gather_fusion.1
  310.9 0.9 broadcast_select_fusion
  311.8 0.0 all-reduce.11.cloned.1.call-update
  311.8 0.0 all-reduce.9.cloned.1.call-start
  311.9 155.8 %all-reduce.11.cloned.1.call-done = (bf16[256,1024]{1,0:T(8,128)(2,1)}, bf16[256,1024]{1,0:T(8,128)(2,1)}) async-done(((bf16[256,1024]{1,0:T(8,128)(2,1)}, bf16[256,1024]{1,0:T(8,128)(2,1)}), (bf16[256,1024]{1,0:T(8,128)(2,1)}, bf16[256,1024]{1,0:T(8,128)(2,1)})) %all-reduce.11.cloned.1.call-update) | async-done | bytes 1048592 | tf_op jit(solution)/shard_map/psum | solution.py:9
  467.7 0.0 copy-start.1
  467.7 0.0 copy-start.6
  467.7 5.4 scatter_fusion.1
  473.1 0.0 copy-done.1
  473.1 2.0 fusion.6
  475.1 0.0 copy-done.6
  475.1 2.1 fusion.1
  477.3 0.0 all-reduce.9.cloned.1.call-update
  477.3 0.3 convolution_convert_fusion
  477.6 117.9 %all-reduce.9.cloned.1.call-done = bf16[1024,256]{1,0:T(8,128)(2,1)} async-done(((bf16[1024,256]{1,0:T(8,128)(2,1)}), bf16[1024,256]{1,0:T(8,128)(2,1)}) %all-reduce.9.cloned.1.call-update) | async-done | bytes 524304 | tf_op jit(solution)/shard_map/psum | solution.py:9
  595.5 0.0 copy-start.3
  595.5 3.5 and_select_fusion.1
  599.0 0.0 copy-done.3
  599.1 1.1 fusion.3
  600.2 0.2 fusion.4
  600.4 2.8 reshape.658
  (13 shorter events, 0.2 us)
Async XLA Ops:
  6.5 169.6 %all-reduce.13.cloned.1.call-start = ((), (), s32[]{:S(2)}) async-start(), calls=%async_computation.3 | async-start | bytes 2097152 | tf_op jit(solution)/shard_map/psum | solution.py:9
  14.5 284.4 %all-reduce.7.cloned.1.call-start = ((), (), s32[]{:S(2)}) async-start(), calls=%async_computation | async-start | bytes 1048576 | tf_op jit(solution)/shard_map/psum | solution.py:9
  176.1 3.4 copy-start
  176.1 3.6 copy-start.5
  179.5 2.2 copy-start.4
  180.8 286.9 %all-reduce.11.cloned.1.call-start = ((), (), s32[]{:S(2)}) async-start(), calls=%async_computation.2 | async-start | bytes 2097152 | tf_op jit(solution)/shard_map/psum | solution.py:9
  298.9 3.4 copy-start.2
  311.8 283.7 %all-reduce.9.cloned.1.call-start = ((), (), s32[]{:S(2)}) async-start(), calls=%async_computation.1 | async-start | bytes 1048576 | tf_op jit(solution)/shard_map/psum | solution.py:9
  467.7 5.4 copy-start.1
  467.7 7.4 %copy-start.6 = (bf16[2,256,256]{2,1,0:T(8,128)(2,1)S(1)}, bf16[2,256,256]{2,1,0:T(8,128)(2,1)}, u32[]{:S(2)}) copy-start(bf16[2,256,256]{2,1,0:T(8,128)(2,1)} %param.19) | copy-start | bytes 786436
  595.5 3.5 copy-start.3
Sparse Core Ops, SparseCore 0:
  14.6 161.4 all-reduce.12
  181.0 117.8 all-reduce.6
  311.9 155.7 all-reduce.10
  477.4 118.0 all-reduce.8

commit v2 on v1

--- a/solution.py
+++ b/solution.py
@@ -1,12 +1,107 @@
+import functools
+
 import jax
 import jax.numpy as jnp
 from jax import lax
+from jax.experimental import pallas as pl
+from jax.experimental.pallas import tpu as pltpu
 from jax.sharding import PartitionSpec as P
 
+MESH = pl.DeviceIdType.MESH
 
-def spread(block, axis, source):
-    block = jnp.where(lax.axis_index(axis) == source, block, jnp.zeros_like(block))
-    return lax.psum(block, axis)
+
+def sum_kernel(axis, other, n, x_ref, o_ref, recv, gath, ssend, srecv, gsend, grecv):
+    me = lax.axis_index(axis)
+    them = lax.axis_index(other)
+
+    def dev(j):
+        return (j, them) if axis == "prow" else (them, j)
+
+    barrier = pltpu.get_barrier_semaphore()
+
+    def greet(i, c):
+        j = lax.rem(me + i, n)
+        pl.semaphore_signal(barrier, 1, device_id=dev(j), device_id_type=MESH)
+        return c
+
+    lax.fori_loop(1, n, greet, 0)
+    pl.semaphore_wait(barrier, n - 1)
+
+    def scatter(j, s):
+        return pltpu.make_async_remote_copy(
+            src_ref=x_ref.at[j],
+            dst_ref=recv.at[s],
+            send_sem=ssend.at[j],
+            recv_sem=srecv.at[s],
+            device_id=dev(j),
+            device_id_type=MESH,
+        )
+
+    def start_scatter(i, c):
+        scatter(lax.rem(me + i, n), me).start()
+        return c
+
+    lax.fori_loop(1, n, start_scatter, 0)
+    recv[me] = x_ref[me]
+
+    def wait_scatter(i, c):
+        scatter(lax.rem(me + n - i, n), lax.rem(me + n - i, n)).wait_recv()
+        scatter(lax.rem(me + i, n), me).wait_send()
+        return c
+
+    lax.fori_loop(1, n, wait_scatter, 0)
+
+    total = recv[0].astype(jnp.float32)
+    for s in range(1, n):
+        total = total + recv[s].astype(jnp.float32)
+    gath[me] = total.astype(gath.dtype)
+
+    def gather(j, s):
+        return pltpu.make_async_remote_copy(
+            src_ref=gath.at[s],
+            dst_ref=gath.at[s],
+            send_sem=gsend.at[j],
+            recv_sem=grecv.at[s],
+            device_id=dev(j),
+            device_id_type=MESH,
+        )
+
+    def start_gather(i, c):
+        gather(lax.rem(me + i, n), me).start()
+        return c
+
+    lax.fori_loop(1, n, start_gather, 0)
+
+    def wait_gather(i, c):
+        gather(lax.rem(me + n - i, n), lax.rem(me + n - i, n)).wait_recv()
+        gather(lax.rem(me + i, n), me).wait_send()
+        return c
+
+    lax.fori_loop(1, n, wait_gather, 0)
+    o_ref[...] = gath[...]
+
+
+def axis_sum(x, axis, other, collective_id):
+    n = lax.axis_size(axis)
+    chunks = x.reshape(n, x.shape[0] // n, x.shape[1])
+    out = pl.pallas_call(
+        functools.partial(sum_kernel, axis, other, n),
+        out_shape=jax.ShapeDtypeStruct(chunks.shape, chunks.dtype),
+        in_specs=[pl.BlockSpec(memory_space=pltpu.VMEM)],
+        out_specs=pl.BlockSpec(memory_space=pltpu.VMEM),
+        scratch_shapes=[
+            pltpu.VMEM(chunks.shape, chunks.dtype),
+            pltpu.VMEM(chunks.shape, chunks.dtype),
+            pltpu.SemaphoreType.DMA((n,)),
+            pltpu.SemaphoreType.DMA((n,)),
+            pltpu.SemaphoreType.DMA((n,)),
+            pltpu.SemaphoreType.DMA((n,)),
+        ],
+        compiler_params=pltpu.CompilerParams(
+            collective_id=collective_id, has_side_effects=True
+        ),
+    )(chunks)
+    return out.reshape(x.shape)
 
 
 def local(matrix, pivots, lower_inverse, upper_inverse):
@@ -34,9 +129,10 @@
         top_first = panel // row_count * block
         is_top = my_row == top_holder
         top_local = current[top_first : top_first + block]
-        incoming = lax.psum(picked, "prow").astype(jnp.float32)
-        old_top = spread(top_local, "prow", top_holder)
-        incoming = incoming.astype(jnp.bfloat16)
+        top_part = jnp.where(is_top, top_local, jnp.zeros((), jnp.bfloat16))
+        both = axis_sum(jnp.concatenate([picked, top_part], axis=0), "prow", "pcol", 0)
+        incoming = both[:block]
+        old_top = both[block:]
         target = jnp.where(is_mine, local_index, local_rows)
         current = current.at[target].set(old_top, mode="drop")
         top_now = current[top_first : top_first + block]
@@ -49,7 +145,9 @@
         factor = jnp.dot(
             panel_cols, upper_inverse[panel], preferred_element_type=jnp.float32
         ).astype(jnp.bfloat16)
-        lower = spread(factor, "pcol", panel_holder)
+        is_panel = my_col == panel_holder
+        factor = jnp.where(is_panel, factor, jnp.zeros((), jnp.bfloat16))
+        lower = axis_sum(factor, "pcol", "prow", 1)
         upper = jnp.dot(
             lower_inverse[panel], incoming, preferred_element_type=jnp.float32
         ).astype(jnp.bfloat16)
@@ -59,7 +157,6 @@
         changed = (current.astype(jnp.float32) - product).astype(jnp.bfloat16)
         current = jnp.where(row_mask[:, None] & col_mask[None, :], changed, current)
         panel_now = current[:, panel_first : panel_first + block]
-        is_panel = my_col == panel_holder
         current = current.at[:, panel_first : panel_first + block].set(
             jnp.where(is_panel & row_mask[:, None], lower, panel_now)
         )

time: 610 us -> 248 us (0.41)
  waiting for transfers between devices: 552 us -> 0 us
  Pallas kernels: 0 us -> 199 us
  between operations: 13.3 us -> 0.27 us
    psum x4 -> x0, waiting for transfers between devices: 552 us -> none  [spread(): return lax.psum(block, axis)]
    pallas_call x0 -> x4, Pallas kernels: none -> 199 us  [axis_sum(): pl.pallas_call(functools.partial(sum_kernel, axis, other, n), out_shape=j...]
  transfers between devices with their start and end apart: 4 -> 0, of which waited for: 4 -> 0; matrix products, arithmetic and copies ran while one was open for 0% -> 0% of each run, Pallas kernels for 0% -> 0%
where the time goes in v2:
time: 248 us; the launch traced here: 246 us
  Pallas kernels  199 us (80%)
  local copies, waits for them, and re-layouts  19.7 us (8%)
  other arithmetic  15.7 us (6%)
  matrix products  11.4 us (5%)
    pallas_call x4, Pallas kernels, axis_sum(): pl.pallas_call(functools.partial(sum_kernel, axis, other, n), out_shape=j...  199 us
    dot_general x2, matrix products, local(): product = jnp.dot(lower, upper, preferred_element_type=jnp.float32)  6.78 us
    scatter x2, other arithmetic, local(): current.at[:, panel_first:panel_first + block]  5.99 us
    scatter x2, local copies, waits for them, and re-layouts, local(): current = current.at[target].set(old_top, mode='drop')  5.86 us

profile of v2, /device:TPU:1, one launch (start us, length us, event | category | flops | bytes accessed | tf_op | source)
XLA Modules:
  0.0 246.2 jit_solution(2892556860387603482)
XLA Ops:
  0.0 0.8 and_select_fusion.5
  0.8 2.1 copy.8
  2.9 0.0 copy-start.4
  2.9 1.2 gather_fusion
  4.1 0.0 copy-done.4
  4.2 0.1 broadcast_select_fusion.1
  4.3 1.3 slice_select_fusion.4
  5.5 0.1 copy.9
  5.6 1.0 pad_maximum_fusion
  6.7 60.1 %shard_map.46 = bf16[32,16,1024]{2,1,0:T(8,128)(2,1)} custom-call(bf16[32,16,1024]{2,1,0:T(8,128)(2,1)} %bitcast.78), custom_call_target="tpu_custom_call" | custom-call | tf_op jit(solution)/shard_map/pallas_call | solution.py:87
  66.8 1.3 fusion.46
  68.0 2.8 %scatter_fusion = bf16[1024,1024]{1,0:T(8,128)(2,1)S(1)} fusion(bf16[1024,1024]{1,0:T(8,128)(2,1)S(1)} %bitcast.73, s32[256]{0:T(256)S(1)} %bitcast.91, bf16[256,1024]{1,0:T(8,128)(2,1)S(1)} %bitcast.86), kind=kCustom, calls=%fused_computation.2 | custom fusion | bytes 1573888 | tf_op jit(solution)/shard_map/scatter | solution.py:137
  70.9 0.0 copy-start.3
  70.9 0.2 fusion.8
  71.1 2.0 fusion
  73.1 40.6 %shard_map.47 = bf16[16,64,256]{2,1,0:T(8,128)(2,1)} custom-call(bf16[16,64,256]{2,1,0:T(8,128)(2,1)} %bitcast.90), custom_call_target="tpu_custom_call" | custom-call | tf_op jit(solution)/shard_map/pallas_call | solution.py:87
  113.8 0.0 copy-done.3
  113.8 0.3 convolution_convert_fusion.1
  114.1 0.0 copy-start.1
  114.1 3.4 %and_select_fusion = bf16[1024,1024]{1,0:T(8,128)(2,1)} fusion(bf16[1024,1024]{1,0:T(8,128)(2,1)S(1)} %fusion.8, bf16[1024,256]{1,0:T(8,128)(2,1)} %bitcast.81, bf16[1024,256]{0,1:T(8,128)(2,1)S(1)} %convolution_convert_fusion.1, pred[1024]{0:T(1024)(128)(4,1)S(1)} %get-tuple-element.106, pred[1024]{0:T(1024)(128)(4,1)S(1)} %get-tuple-element.100), kind=kOutput, calls=%fused_computation.6 | convolution fusion | flops 542113792 | bytes 5244928 | tf_op jit(solution)/shard_map/dot_general | solution.py:156
  117.5 0.7 compare_reduce_fusion
  118.2 0.0 copy-done.1
  118.2 3.0 %fusion.2 = bf16[1024,1024]{1,0:T(8,128)(2,1)} fusion(bf16[1024,1024]{1,0:T(8,128)(2,1)} %and_select_fusion, bf16[1024,256]{1,0:T(8,128)(2,1)S(1)} %bitcast.82, pred[1024]{0:T(1024)(128)(4,1)S(1)} %get-tuple-element.103, pred[]{:T(512)} %compare_reduce_fusion), kind=kLoop, calls=%fused_computation.18 | loop fusion | flops 524288 | bytes 1574400 | tf_op jit(solution)/shard_map/scatter | solution.py:160
  121.2 2.1 broadcast_select_fusion.2
  123.3 3.4 %gather_fusion.1 = bf16[256,1024]{1,0:T(8,128)(2,1)S(1)} fusion(bf16[1024,1024]{1,0:T(8,128)(2,1)} %get-tuple-element.88, s32[1024]{0:T(1024)S(1)} %pad_clamp_fusion), kind=kCustom, calls=%fused_computation.1 | custom fusion | bytes 1049600 | tf_op jit(solution)/shard_map/gather | solution.py:127
  126.7 0.1 broadcast_select_fusion
  126.8 1.0 pad_maximum_fusion.1
  127.9 0.0 copy-start
  127.9 62.1 %shard_map.48 = bf16[32,16,1024]{2,1,0:T(8,128)(2,1)} custom-call(bf16[32,16,1024]{2,1,0:T(8,128)(2,1)} %bitcast.79), custom_call_target="tpu_custom_call" | custom-call | tf_op jit(solution)/shard_map/pallas_call | solution.py:87
  189.9 1.3 fusion.45
  191.2 0.0 copy-done
  191.2 3.0 %scatter_fusion.1 = bf16[1024,1024]{1,0:T(8,128)(2,1)S(1)} fusion(bf16[1024,1024]{1,0:T(8,128)(2,1)S(1)} %copy-done, s32[256]{0:T(256)S(1)} %bitcast.92, bf16[256,1024]{1,0:T(8,128)(2,1)S(1)} %bitcast.85), kind=kCustom, calls=%fused_computation.3 | custom fusion | bytes 1573888 | tf_op jit(solution)/shard_map/scatter | solution.py:137
  194.3 0.2 fusion.6
  194.5 2.0 fusion.1
  196.5 36.4 %shard_map.49 = bf16[16,64,256]{2,1,0:T(8,128)(2,1)} custom-call(bf16[16,64,256]{2,1,0:T(8,128)(2,1)} %bitcast.89), custom_call_target="tpu_custom_call" | custom-call | tf_op jit(solution)/shard_map/pallas_call | solution.py:87
  232.9 0.3 convolution_convert_fusion
  233.2 0.0 copy-start.2
  233.2 3.4 %and_select_fusion.1 = bf16[1024,1024]{1,0:T(8,128)(2,1)} fusion(bf16[1024,1024]{1,0:T(8,128)(2,1)S(1)} %fusion.6, bf16[1024,256]{1,0:T(8,128)(2,1)} %bitcast.83, bf16[1024,256]{0,1:T(8,128)(2,1)S(1)} %convolution_convert_fusion, pred[1024]{0:T(1024)(128)(4,1)S(1)} %get-tuple-element.107, pred[1024]{0:T(1024)(128)(4,1)S(1)} %get-tuple-element.101), kind=kOutput, calls=%fused_computation.7 | convolution fusion | flops 542113792 | bytes 5244928 | tf_op jit(solution)/shard_map/dot_general | solution.py:156
  236.6 0.0 copy-done.2
  236.6 3.0 %fusion.3 = bf16[1024,1024]{1,0:T(8,128)(2,1)} fusion(bf16[1024,1024]{1,0:T(8,128)(2,1)} %and_select_fusion.1, bf16[1024,256]{1,0:T(8,128)(2,1)S(1)} %bitcast.84, pred[1024]{0:T(1024)(128)(4,1)S(1)} %get-tuple-element.102, pred[]{:T(512)} %compare_reduce_fusion), kind=kLoop, calls=%fused_computation.19 | loop fusion | flops 524288 | bytes 1574400 | tf_op jit(solution)/shard_map/scatter | solution.py:160
  239.7 2.0 fusion.4
  241.7 4.5 %reshape.688 = bf16[4,256,4,256]{3,2,1,0:T(4,128)(2,1)} reshape(bf16[1024,1024]{1,0:T(8,128)(2,1)} %fusion.4) | data formatting | bytes 4194304 | tf_op jit(solution)/shard_map/reshape | solution.py:167
  (11 shorter events, 0.1 us)
Async XLA Ops:
  2.9 1.2 copy-start.4
  70.9 42.9 %copy-start.3 = (bf16[2,256,256]{2,1,0:T(8,128)(2,1)S(1)}, bf16[2,256,256]{2,1,0:T(8,128)(2,1)}, u32[]{:S(2)}) copy-start(bf16[2,256,256]{2,1,0:T(8,128)(2,1)} %param.18) | copy-start | bytes 786436
  114.1 4.1 %copy-start.1 = (bf16[16,64,256]{2,1,0:T(8,128)(2,1)S(1)}, bf16[16,64,256]{2,1,0:T(8,128)(2,1)}, u32[]{:S(2)}) copy-start(bf16[16,64,256]{2,1,0:T(8,128)(2,1)} %shard_map.47) | copy-start | bytes 1572868
  127.9 63.4 %copy-start = (bf16[1024,1024]{1,0:T(8,128)(2,1)S(1)}, bf16[1024,1024]{1,0:T(8,128)(2,1)}, u32[]{:S(2)}) copy-start(bf16[1024,1024]{1,0:T(8,128)(2,1)} %get-tuple-element.88) | copy-start | bytes 6291460
  233.2 3.4 %copy-start.2 = (bf16[16,64,256]{2,1,0:T(8,128)(2,1)S(1)}, bf16[16,64,256]{2,1,0:T(8,128)(2,1)}, u32[]{:S(2)}) copy-start(bf16[16,64,256]{2,1,0:T(8,128)(2,1)} %shard_map.49) | copy-start | bytes 1572868

commit v3 on v2

--- a/solution.py
+++ b/solution.py
@@ -10,7 +10,8 @@
 MESH = pl.DeviceIdType.MESH
 
 
-def sum_kernel(axis, other, n, x_ref, o_ref, recv, gath, ssend, srecv, gsend, grecv):
+def sum_kernel(axis, other, n, summed, source, x_ref, o_ref, recv, gath, ssend, srecv,
+               bsend, brecv, gsend, grecv):
     me = lax.axis_index(axis)
     them = lax.axis_index(other)
 
@@ -37,24 +38,88 @@
             device_id_type=MESH,
         )
 
-    def start_scatter(i, c):
-        scatter(lax.rem(me + i, n), me).start()
-        return c
-
-    lax.fori_loop(1, n, start_scatter, 0)
-    recv[me] = x_ref[me]
-
-    def wait_scatter(i, c):
-        scatter(lax.rem(me + n - i, n), lax.rem(me + n - i, n)).wait_recv()
-        scatter(lax.rem(me + i, n), me).wait_send()
-        return c
-
-    lax.fori_loop(1, n, wait_scatter, 0)
-
-    total = recv[0].astype(jnp.float32)
-    for s in range(1, n):
-        total = total + recv[s].astype(jnp.float32)
-    gath[me] = total.astype(gath.dtype)
+    def spread(j):
+        return pltpu.make_async_remote_copy(
+            src_ref=x_ref.at[j],
+            dst_ref=gath.at[j],
+            send_sem=bsend.at[j],
+            recv_sem=brecv.at[0],
+            device_id=dev(j),
+            device_id_type=MESH,
+        )
+
+    if summed > 0:
+        def start_scatter(i, c):
+            j = lax.rem(me + i, n)
+
+            @pl.when(j < summed)
+            def _():
+                scatter(j, me).start()
+
+            return c
+
+        lax.fori_loop(1, n, start_scatter, 0)
+
+    if summed < n:
+        @pl.when(me == source)
+        def _():
+            def start_spread(i, c):
+                j = lax.rem(me + i, n)
+
+                @pl.when(j >= summed)
+                def _():
+                    spread(j).start()
+
+                return c
+
+            lax.fori_loop(1, n, start_spread, 0)
+            if source >= summed:
+                gath[source] = x_ref[source]
+
+    if summed > 0:
+        @pl.when(me < summed)
+        def _():
+            recv[me] = x_ref[me]
+
+            def wait_scatter(i, c):
+                s = lax.rem(me + n - i, n)
+                scatter(s, s).wait_recv()
+                return c
+
+            lax.fori_loop(1, n, wait_scatter, 0)
+            total = recv[0].astype(jnp.float32)
+            for s in range(1, n):
+                total = total + recv[s].astype(jnp.float32)
+            gath[me] = total.astype(gath.dtype)
+
+        def wait_scatter_sent(i, c):
+            j = lax.rem(me + i, n)
+
+            @pl.when(j < summed)
+            def _():
+                scatter(j, me).wait_send()
+
+            return c
+
+        lax.fori_loop(1, n, wait_scatter_sent, 0)
+
+    if summed < n:
+        @pl.when((me >= summed) & (me != source))
+        def _():
+            spread(me).wait_recv()
+
+        @pl.when(me == source)
+        def _():
+            def wait_spread_sent(i, c):
+                j = lax.rem(me + i, n)
+
+                @pl.when(j >= summed)
+                def _():
+                    spread(j).wait_send()
+
+                return c
+
+            lax.fori_loop(1, n, wait_spread_sent, 0)
 
     def gather(j, s):
         return pltpu.make_async_remote_copy(
@@ -81,11 +146,12 @@
     o_ref[...] = gath[...]
 
 
-def axis_sum(x, axis, other, collective_id):
+def axis_sum(x, axis, other, collective_id, summed_rows, source):
     n = lax.axis_size(axis)
     chunks = x.reshape(n, x.shape[0] // n, x.shape[1])
+    summed = summed_rows // chunks.shape[1]
     out = pl.pallas_call(
-        functools.partial(sum_kernel, axis, other, n),
+        functools.partial(sum_kernel, axis, other, n, summed, source),
         out_shape=jax.ShapeDtypeStruct(chunks.shape, chunks.dtype),
         in_specs=[pl.BlockSpec(memory_space=pltpu.VMEM)],
         out_specs=pl.BlockSpec(memory_space=pltpu.VMEM),
@@ -94,6 +160,8 @@
             pltpu.VMEM(chunks.shape, chunks.dtype),
             pltpu.SemaphoreType.DMA((n,)),
             pltpu.SemaphoreType.DMA((n,)),
+            pltpu.SemaphoreType.DMA((n,)),
+            pltpu.SemaphoreType.DMA((1,)),
             pltpu.SemaphoreType.DMA((n,)),
             pltpu.SemaphoreType.DMA((n,)),
         ],
@@ -130,7 +198,9 @@
         is_top = my_row == top_holder
         top_local = current[top_first : top_first + block]
         top_part = jnp.where(is_top, top_local, jnp.zeros((), jnp.bfloat16))
-        both = axis_sum(jnp.concatenate([picked, top_part], axis=0), "prow", "pcol", 0)
+        both = axis_sum(
+            jnp.concatenate([picked, top_part], axis=0), "prow", "pcol", 2 * panel, block, top_holder
+        )
         incoming = both[:block]
         old_top = both[block:]
         target = jnp.where(is_mine, local_index, local_rows)
@@ -147,7 +217,7 @@
         ).astype(jnp.bfloat16)
         is_panel = my_col == panel_holder
         factor = jnp.where(is_panel, factor, jnp.zeros((), jnp.bfloat16))
-        lower = axis_sum(factor, "pcol", "prow", 1)
+        lower = axis_sum(factor, "pcol", "prow", 2 * panel + 1, 0, panel_holder)
         upper = jnp.dot(
             lower_inverse[panel], incoming, preferred_element_type=jnp.float32
         ).astype(jnp.bfloat16)

time: 248 us -> 255 us (1.028)
  the two profiles are of different devices: /device:TPU:1 before, /device:TPU:49 now
where the time goes in v3:
time: 255 us; the launch traced here: 254 us
  Pallas kernels  207 us (81%)
  local copies, waits for them, and re-layouts  19.7 us (8%)
  other arithmetic  15.7 us (6%)
  matrix products  11.4 us (4%)
    pallas_call x4, Pallas kernels, axis_sum(): pl.pallas_call(functools.partial(sum_kernel, axis, other, n, summed, sour...  207 us
    dot_general x2, matrix products, local(): product = jnp.dot(lower, upper, preferred_element_type=jnp.float32)  6.78 us
    scatter x2, other arithmetic, local(): current.at[:, panel_first:panel_first + block]  5.99 us
    scatter x2, local copies, waits for them, and re-layouts, local(): current = current.at[target].set(old_top, mode='drop')  5.86 us

profile of v3, /device:TPU:49, one launch (start us, length us, event | category | flops | bytes accessed | tf_op | source)
XLA Modules:
  0.0 254.3 jit_solution(15867783009825413644)
XLA Ops:
  0.0 0.8 and_select_fusion.5
  0.8 2.1 copy.8
  2.9 0.0 copy-start.4
  2.9 1.2 gather_fusion
  4.1 0.0 copy-done.4
  4.2 0.1 broadcast_select_fusion.1
  4.3 1.3 slice_select_fusion.4
  5.5 0.1 copy.9
  5.6 1.0 pad_maximum_fusion
  6.7 71.3 %shard_map.46 = bf16[32,16,1024]{2,1,0:T(8,128)(2,1)} custom-call(bf16[32,16,1024]{2,1,0:T(8,128)(2,1)} %bitcast.78), custom_call_target="tpu_custom_call" | custom-call | tf_op jit(solution)/shard_map/pallas_call | solution.py:153
  78.0 1.3 fusion.46
  79.3 2.8 %scatter_fusion = bf16[1024,1024]{1,0:T(8,128)(2,1)S(1)} fusion(bf16[1024,1024]{1,0:T(8,128)(2,1)S(1)} %bitcast.73, s32[256]{0:T(256)S(1)} %bitcast.91, bf16[256,1024]{1,0:T(8,128)(2,1)S(1)} %bitcast.86), kind=kCustom, calls=%fused_computation.2 | custom fusion | bytes 1573888 | tf_op jit(solution)/shard_map/scatter | solution.py:207
  82.2 0.0 copy-start.3
  82.2 0.2 fusion.8
  82.4 2.0 fusion
  84.4 37.5 %shard_map.47 = bf16[16,64,256]{2,1,0:T(8,128)(2,1)} custom-call(bf16[16,64,256]{2,1,0:T(8,128)(2,1)} %bitcast.90), custom_call_target="tpu_custom_call" | custom-call | tf_op jit(solution)/shard_map/pallas_call | solution.py:153
  121.9 0.0 copy-done.3
  121.9 0.3 convolution_convert_fusion.1
  122.2 0.0 copy-start.1
  122.2 3.4 %and_select_fusion = bf16[1024,1024]{1,0:T(8,128)(2,1)} fusion(bf16[1024,1024]{1,0:T(8,128)(2,1)S(1)} %fusion.8, bf16[1024,256]{1,0:T(8,128)(2,1)} %bitcast.81, bf16[1024,256]{0,1:T(8,128)(2,1)S(1)} %convolution_convert_fusion.1, pred[1024]{0:T(1024)(128)(4,1)S(1)} %get-tuple-element.106, pred[1024]{0:T(1024)(128)(4,1)S(1)} %get-tuple-element.100), kind=kOutput, calls=%fused_computation.6 | convolution fusion | flops 542113792 | bytes 5244928 | tf_op jit(solution)/shard_map/dot_general | solution.py:226
  125.6 0.7 compare_reduce_fusion
  126.4 0.0 copy-done.1
  126.4 3.0 %fusion.2 = bf16[1024,1024]{1,0:T(8,128)(2,1)} fusion(bf16[1024,1024]{1,0:T(8,128)(2,1)} %and_select_fusion, bf16[1024,256]{1,0:T(8,128)(2,1)S(1)} %bitcast.82, pred[1024]{0:T(1024)(128)(4,1)S(1)} %get-tuple-element.103, pred[]{:T(512)} %compare_reduce_fusion), kind=kLoop, calls=%fused_computation.18 | loop fusion | flops 524288 | bytes 1574400 | tf_op jit(solution)/shard_map/scatter | solution.py:230
  129.3 2.1 broadcast_select_fusion.2
  131.4 3.4 %gather_fusion.1 = bf16[256,1024]{1,0:T(8,128)(2,1)S(1)} fusion(bf16[1024,1024]{1,0:T(8,128)(2,1)} %get-tuple-element.88, s32[1024]{0:T(1024)S(1)} %pad_clamp_fusion), kind=kCustom, calls=%fused_computation.1 | custom fusion | bytes 1049600 | tf_op jit(solution)/shard_map/gather | solution.py:195
  134.8 0.1 broadcast_select_fusion
  135.0 1.0 pad_maximum_fusion.1
  136.0 0.0 copy-start
  136.0 69.2 %shard_map.48 = bf16[32,16,1024]{2,1,0:T(8,128)(2,1)} custom-call(bf16[32,16,1024]{2,1,0:T(8,128)(2,1)} %bitcast.79), custom_call_target="tpu_custom_call" | custom-call | tf_op jit(solution)/shard_map/pallas_call | solution.py:153
  205.2 1.3 fusion.45
  206.5 0.0 copy-done
  206.5 3.0 %scatter_fusion.1 = bf16[1024,1024]{1,0:T(8,128)(2,1)S(1)} fusion(bf16[1024,1024]{1,0:T(8,128)(2,1)S(1)} %copy-done, s32[256]{0:T(256)S(1)} %bitcast.92, bf16[256,1024]{1,0:T(8,128)(2,1)S(1)} %bitcast.85), kind=kCustom, calls=%fused_computation.3 | custom fusion | bytes 1573888 | tf_op jit(solution)/shard_map/scatter | solution.py:207
  209.5 0.2 fusion.6
  209.8 2.0 fusion.1
  211.8 29.2 %shard_map.49 = bf16[16,64,256]{2,1,0:T(8,128)(2,1)} custom-call(bf16[16,64,256]{2,1,0:T(8,128)(2,1)} %bitcast.89), custom_call_target="tpu_custom_call" | custom-call | tf_op jit(solution)/shard_map/pallas_call | solution.py:153
  241.0 0.3 convolution_convert_fusion
  241.3 0.0 copy-start.2
  241.3 3.4 %and_select_fusion.1 = bf16[1024,1024]{1,0:T(8,128)(2,1)} fusion(bf16[1024,1024]{1,0:T(8,128)(2,1)S(1)} %fusion.6, bf16[1024,256]{1,0:T(8,128)(2,1)} %bitcast.83, bf16[1024,256]{0,1:T(8,128)(2,1)S(1)} %convolution_convert_fusion, pred[1024]{0:T(1024)(128)(4,1)S(1)} %get-tuple-element.107, pred[1024]{0:T(1024)(128)(4,1)S(1)} %get-tuple-element.101), kind=kOutput, calls=%fused_computation.7 | convolution fusion | flops 542113792 | bytes 5244928 | tf_op jit(solution)/shard_map/dot_general | solution.py:226
  244.7 0.0 copy-done.2
  244.7 3.0 %fusion.3 = bf16[1024,1024]{1,0:T(8,128)(2,1)} fusion(bf16[1024,1024]{1,0:T(8,128)(2,1)} %and_select_fusion.1, bf16[1024,256]{1,0:T(8,128)(2,1)S(1)} %bitcast.84, pred[1024]{0:T(1024)(128)(4,1)S(1)} %get-tuple-element.102, pred[]{:T(512)} %compare_reduce_fusion), kind=kLoop, calls=%fused_computation.19 | loop fusion | flops 524288 | bytes 1574400 | tf_op jit(solution)/shard_map/scatter | solution.py:230
  247.7 2.0 fusion.4
  249.8 4.5 %reshape.688 = bf16[4,256,4,256]{3,2,1,0:T(4,128)(2,1)} reshape(bf16[1024,1024]{1,0:T(8,128)(2,1)} %fusion.4) | data formatting | bytes 4194304 | tf_op jit(solution)/shard_map/reshape | solution.py:237
  (11 shorter events, 0.1 us)
Async XLA Ops:
  2.9 1.2 copy-start.4
  82.2 39.7 %copy-start.3 = (bf16[2,256,256]{2,1,0:T(8,128)(2,1)S(1)}, bf16[2,256,256]{2,1,0:T(8,128)(2,1)}, u32[]{:S(2)}) copy-start(bf16[2,256,256]{2,1,0:T(8,128)(2,1)} %param.18) | copy-start | bytes 786436
  122.2 4.1 %copy-start.1 = (bf16[16,64,256]{2,1,0:T(8,128)(2,1)S(1)}, bf16[16,64,256]{2,1,0:T(8,128)(2,1)}, u32[]{:S(2)}) copy-start(bf16[16,64,256]{2,1,0:T(8,128)(2,1)} %shard_map.47) | copy-start | bytes 1572868
  136.0 70.5 %copy-start = (bf16[1024,1024]{1,0:T(8,128)(2,1)S(1)}, bf16[1024,1024]{1,0:T(8,128)(2,1)}, u32[]{:S(2)}) copy-start(bf16[1024,1024]{1,0:T(8,128)(2,1)} %get-tuple-element.88) | copy-start | bytes 6291460
  241.3 3.4 %copy-start.2 = (bf16[16,64,256]{2,1,0:T(8,128)(2,1)S(1)}, bf16[16,64,256]{2,1,0:T(8,128)(2,1)}, u32[]{:S(2)}) copy-start(bf16[16,64,256]{2,1,0:T(8,128)(2,1)} %shard_map.49) | copy-start | bytes 1572868

commit v4 on v3

--- a/solution.py
+++ b/solution.py
@@ -172,7 +172,99 @@
     return out.reshape(x.shape)
 
 
-def local(matrix, pivots, lower_inverse, upper_inverse):
+def group_kernel(stride, size, mode, x_ref, o_ref, buf, send, recv):
+    p = lax.axis_index("prow")
+    q = lax.axis_index("pcol")
+    me = lax.rem(p // stride, size)
+    base = p - me * stride
+
+    def dev(k):
+        return (base + k * stride, q)
+
+    barrier = pltpu.get_barrier_semaphore()
+
+    def greet(i, c):
+        pl.semaphore_signal(barrier, 1, device_id=dev(lax.rem(me + i, size)), device_id_type=MESH)
+        return c
+
+    lax.fori_loop(1, size, greet, 0)
+    pl.semaphore_wait(barrier, size - 1)
+
+    def copy(k, s):
+        src = x_ref.at[k] if mode == "rs" else buf.at[s]
+        return pltpu.make_async_remote_copy(
+            src_ref=src,
+            dst_ref=buf.at[s],
+            send_sem=send.at[k],
+            recv_sem=recv.at[s],
+            device_id=dev(k),
+            device_id_type=MESH,
+        )
+
+    if mode == "ag":
+        buf[me] = x_ref[...]
+
+    def start(i, c):
+        copy(lax.rem(me + i, size), me).start()
+        return c
+
+    lax.fori_loop(1, size, start, 0)
+    if mode == "rs":
+        buf[me] = x_ref[me]
+
+    def wait(i, c):
+        s = lax.rem(me + size - i, size)
+        copy(s, s).wait_recv()
+        copy(lax.rem(me + i, size), me).wait_send()
+        return c
+
+    lax.fori_loop(1, size, wait, 0)
+    if mode == "rs":
+        total = buf[0].astype(jnp.float32)
+        for s in range(1, size):
+            total = total + buf[s].astype(jnp.float32)
+        o_ref[...] = total.astype(o_ref.dtype)
+    else:
+        o_ref[...] = buf[...]
+
+
+def group_step(x, stride, size, mode, collective_id):
+    if mode == "rs":
+        chunks = x.reshape(size, x.shape[0] // size, x.shape[1])
+        out_shape = chunks.shape[1:]
+        buf_shape = chunks.shape
+    else:
+        chunks = x
+        out_shape = (size,) + x.shape
+        buf_shape = out_shape
+    out = pl.pallas_call(
+        functools.partial(group_kernel, stride, size, mode),
+        out_shape=jax.ShapeDtypeStruct(out_shape, x.dtype),
+        in_specs=[pl.BlockSpec(memory_space=pltpu.VMEM)],
+        out_specs=pl.BlockSpec(memory_space=pltpu.VMEM),
+        scratch_shapes=[
+            pltpu.VMEM(buf_shape, x.dtype),
+            pltpu.SemaphoreType.DMA((size,)),
+            pltpu.SemaphoreType.DMA((size,)),
+        ],
+        compiler_params=pltpu.CompilerParams(
+            collective_id=collective_id, has_side_effects=True
+        ),
+    )(chunks)
+    if mode == "ag":
+        out = out.reshape(size * x.shape[0], x.shape[1])
+    return out
+
+
+def prow_sum(x, x_devices):
+    y_devices = lax.axis_size("prow") // x_devices
+    part = group_step(x, 1, x_devices, "rs", 10)
+    part = group_step(part, x_devices, y_devices, "rs", 11)
+    part = group_step(part, x_devices, y_devices, "ag", 12)
+    return group_step(part, 1, x_devices, "ag", 13)
+
+
+def local(x_devices, matrix, pivots, lower_inverse, upper_inverse):
     row_count = lax.axis_size("prow")
     col_count = lax.axis_size("pcol")
     my_row = lax.axis_index("prow")
@@ -198,9 +290,7 @@
         is_top = my_row == top_holder
         top_local = current[top_first : top_first + block]
         top_part = jnp.where(is_top, top_local, jnp.zeros((), jnp.bfloat16))
-        both = axis_sum(
-            jnp.concatenate([picked, top_part], axis=0), "prow", "pcol", 2 * panel, block, top_holder
-        )
+        both = prow_sum(jnp.concatenate([picked, top_part], axis=0), x_devices)
         incoming = both[:block]
         old_top = both[block:]
         target = jnp.where(is_mine, local_index, local_rows)
@@ -238,6 +328,7 @@
 
 
 def solution(mesh):
+    x_devices = len({d.coords[0] for d in mesh.devices[:, 0]})
     in_specs = (P(None, "prow", None, "pcol"), P(), P(), P())
     out_specs = P(None, "prow", None, "pcol")
-    return jax.shard_map(local, mesh=mesh, in_specs=in_specs, out_specs=out_specs, check_vma=False)
+    return jax.shard_map(functools.partial(local, x_devices), mesh=mesh, in_specs=in_specs, out_specs=out_specs, check_vma=False)

time: 255 us -> 240 us (0.941)
  the two profiles are of different devices: /device:TPU:49 before, /device:TPU:1 now
where the time goes in v4:
time: 240 us; the launch traced here: 239 us
  Pallas kernels  192 us (80%)
  local copies, waits for them, and re-layouts  19.7 us (8%)
  other arithmetic  15.7 us (7%)
  matrix products  11.4 us (5%)
    pallas_call x8, Pallas kernels, group_step(): pl.pallas_call(functools.partial(group_kernel, stride, size, mode), out_s...  124 us
    pallas_call x2, Pallas kernels, axis_sum(): pl.pallas_call(functools.partial(sum_kernel, axis, other, n, summed, sour...  67.3 us
    dot_general x2, matrix products, local(): product = jnp.dot(lower, upper, preferred_element_type=jnp.float32)  6.78 us
    scatter x2, other arithmetic, local(): current.at[:, panel_first:panel_first + block]  5.99 us
    scatter x2, local copies, waits for them, and re-layouts, local(): current = current.at[target].set(old_top, mode='drop')  5.86 us

profile of v4, /device:TPU:1, one launch (start us, length us, event | category | flops | bytes accessed | tf_op | source)
XLA Modules:
  0.0 238.8 jit_solution(12295419857037565)
XLA Ops:
  0.0 0.8 and_select_fusion.5
  0.8 2.1 copy.8
  2.9 0.0 copy-start.4
  2.9 1.2 gather_fusion
  4.1 0.0 copy-done.4
  4.2 0.1 broadcast_select_fusion.1
  4.3 1.3 slice_select_fusion.4
  5.5 0.1 copy.9
  5.6 1.0 pad_maximum_fusion
  6.7 17.4 %shard_map.46 = bf16[128,1024]{1,0:T(8,128)(2,1)} custom-call(bf16[4,128,1024]{2,1,0:T(8,128)(2,1)} %bitcast.82), custom_call_target="tpu_custom_call" | custom-call | tf_op jit(solution)/shard_map/pallas_call | solution.py:240
  24.1 14.5 %shard_map.47.x_ref = bf16[16,1024]{1,0:T(8,128)(2,1)} custom-call(bf16[8,16,1024]{2,1,0:T(8,128)(2,1)} %bitcast.93), custom_call_target="tpu_custom_call" | custom-call | tf_op jit(solution)/shard_map/pallas_call | solution.py:240
  38.6 11.4 %shard_map.48 = bf16[8,16,1024]{2,1,0:T(8,128)(2,1)} custom-call(bf16[16,1024]{1,0:T(8,128)(2,1)} %shard_map.47.x_ref), custom_call_target="tpu_custom_call" | custom-call | tf_op jit(solution)/shard_map/pallas_call | solution.py:240
  50.0 20.5 %shard_map.49 = bf16[4,128,1024]{2,1,0:T(8,128)(2,1)} custom-call(bf16[128,1024]{1,0:T(8,128)(2,1)} %bitcast.94), custom_call_target="tpu_custom_call" | custom-call | tf_op jit(solution)/shard_map/pallas_call | solution.py:240
  70.5 1.3 fusion.46
  71.8 2.8 %scatter_fusion = bf16[1024,1024]{1,0:T(8,128)(2,1)S(1)} fusion(bf16[1024,1024]{1,0:T(8,128)(2,1)S(1)} %bitcast.77, s32[256]{0:T(256)S(1)} %bitcast.99, bf16[256,1024]{1,0:T(8,128)(2,1)S(1)} %bitcast.90), kind=kCustom, calls=%fused_computation.2 | custom fusion | bytes 1573888 | tf_op jit(solution)/shard_map/scatter | solution.py:297
  74.7 0.0 copy-start.3
  74.7 0.2 fusion.8
  74.9 2.0 fusion
  76.9 38.5 %shard_map.50 = bf16[16,64,256]{2,1,0:T(8,128)(2,1)} custom-call(bf16[16,64,256]{2,1,0:T(8,128)(2,1)} %bitcast.98), custom_call_target="tpu_custom_call" | custom-call | tf_op jit(solution)/shard_map/pallas_call | solution.py:153
  115.4 0.0 copy-done.3
  115.4 0.3 convolution_convert_fusion.1
  115.8 0.0 copy-start.1
  115.8 3.4 %and_select_fusion = bf16[1024,1024]{1,0:T(8,128)(2,1)} fusion(bf16[1024,1024]{1,0:T(8,128)(2,1)S(1)} %fusion.8, bf16[1024,256]{1,0:T(8,128)(2,1)} %bitcast.85, bf16[1024,256]{0,1:T(8,128)(2,1)S(1)} %convolution_convert_fusion.1, pred[1024]{0:T(1024)(128)(4,1)S(1)} %get-tuple-element.106, pred[1024]{0:T(1024)(128)(4,1)S(1)} %get-tuple-element.100), kind=kOutput, calls=%fused_computation.6 | convolution fusion | flops 542113792 | bytes 5244928 | tf_op jit(solution)/shard_map/dot_general | solution.py:316
  119.1 0.7 compare_reduce_fusion
  119.9 0.0 copy-done.1
  119.9 3.0 %fusion.2 = bf16[1024,1024]{1,0:T(8,128)(2,1)} fusion(bf16[1024,1024]{1,0:T(8,128)(2,1)} %and_select_fusion, bf16[1024,256]{1,0:T(8,128)(2,1)S(1)} %bitcast.86, pred[1024]{0:T(1024)(128)(4,1)S(1)} %get-tuple-element.103, pred[]{:T(512)} %compare_reduce_fusion), kind=kLoop, calls=%fused_computation.18 | loop fusion | flops 524288 | bytes 1574400 | tf_op jit(solution)/shard_map/scatter | solution.py:320
  122.8 2.1 broadcast_select_fusion.2
  124.9 3.4 %gather_fusion.1 = bf16[256,1024]{1,0:T(8,128)(2,1)S(1)} fusion(bf16[1024,1024]{1,0:T(8,128)(2,1)} %get-tuple-element.88, s32[1024]{0:T(1024)S(1)} %pad_clamp_fusion), kind=kCustom, calls=%fused_computation.1 | custom fusion | bytes 1049600 | tf_op jit(solution)/shard_map/gather | solution.py:287
  128.4 0.1 broadcast_select_fusion
  128.5 1.0 pad_maximum_fusion.1
  129.5 17.9 %shard_map.51 = bf16[128,1024]{1,0:T(8,128)(2,1)} custom-call(bf16[4,128,1024]{2,1,0:T(8,128)(2,1)} %bitcast.83), custom_call_target="tpu_custom_call" | custom-call | tf_op jit(solution)/shard_map/pallas_call | solution.py:240
  147.4 0.0 copy-start
  147.4 13.0 %shard_map.52.x_ref = bf16[16,1024]{1,0:T(8,128)(2,1)} custom-call(bf16[8,16,1024]{2,1,0:T(8,128)(2,1)} %bitcast.95), custom_call_target="tpu_custom_call" | custom-call | tf_op jit(solution)/shard_map/pallas_call | solution.py:240
  160.4 11.4 %shard_map.53 = bf16[8,16,1024]{2,1,0:T(8,128)(2,1)} custom-call(bf16[16,1024]{1,0:T(8,128)(2,1)} %shard_map.52.x_ref), custom_call_target="tpu_custom_call" | custom-call | tf_op jit(solution)/shard_map/pallas_call | solution.py:240
  171.8 18.2 %shard_map.54 = bf16[4,128,1024]{2,1,0:T(8,128)(2,1)} custom-call(bf16[128,1024]{1,0:T(8,128)(2,1)} %bitcast.96), custom_call_target="tpu_custom_call" | custom-call | tf_op jit(solution)/shard_map/pallas_call | solution.py:240
  190.1 1.3 fusion.45
  191.4 0.0 copy-done
  191.4 3.0 %scatter_fusion.1 = bf16[1024,1024]{1,0:T(8,128)(2,1)S(1)} fusion(bf16[1024,1024]{1,0:T(8,128)(2,1)S(1)} %copy-done, s32[256]{0:T(256)S(1)} %bitcast.100, bf16[256,1024]{1,0:T(8,128)(2,1)S(1)} %bitcast.89), kind=kCustom, calls=%fused_computation.3 | custom fusion | bytes 1573888 | tf_op jit(solution)/shard_map/scatter | solution.py:297
  194.4 0.2 fusion.6
  194.6 2.0 fusion.1
  196.6 28.8 %shard_map.55 = bf16[16,64,256]{2,1,0:T(8,128)(2,1)} custom-call(bf16[16,64,256]{2,1,0:T(8,128)(2,1)} %bitcast.97), custom_call_target="tpu_custom_call" | custom-call | tf_op jit(solution)/shard_map/pallas_call | solution.py:153
  225.5 0.3 convolution_convert_fusion
  225.8 0.0 copy-start.2
  225.8 3.4 %and_select_fusion.1 = bf16[1024,1024]{1,0:T(8,128)(2,1)} fusion(bf16[1024,1024]{1,0:T(8,128)(2,1)S(1)} %fusion.6, bf16[1024,256]{1,0:T(8,128)(2,1)} %bitcast.87, bf16[1024,256]{0,1:T(8,128)(2,1)S(1)} %convolution_convert_fusion, pred[1024]{0:T(1024)(128)(4,1)S(1)} %get-tuple-element.107, pred[1024]{0:T(1024)(128)(4,1)S(1)} %get-tuple-element.101), kind=kOutput, calls=%fused_computation.7 | convolution fusion | flops 542113792 | bytes 5244928 | tf_op jit(solution)/shard_map/dot_general | solution.py:316
  229.2 0.0 copy-done.2
  229.2 3.0 %fusion.3 = bf16[1024,1024]{1,0:T(8,128)(2,1)} fusion(bf16[1024,1024]{1,0:T(8,128)(2,1)} %and_select_fusion.1, bf16[1024,256]{1,0:T(8,128)(2,1)S(1)} %bitcast.88, pred[1024]{0:T(1024)(128)(4,1)S(1)} %get-tuple-element.102, pred[]{:T(512)} %compare_reduce_fusion), kind=kLoop, calls=%fused_computation.19 | loop fusion | flops 524288 | bytes 1574400 | tf_op jit(solution)/shard_map/scatter | solution.py:320
  232.2 2.0 fusion.4
  234.3 4.5 %reshape.704 = bf16[4,256,4,256]{3,2,1,0:T(4,128)(2,1)} reshape(bf16[1024,1024]{1,0:T(8,128)(2,1)} %fusion.4) | data formatting | bytes 4194304 | tf_op jit(solution)/shard_map/reshape | solution.py:327
  (11 shorter events, 0.1 us)
Async XLA Ops:
  2.9 1.2 copy-start.4
  74.7 40.7 %copy-start.3 = (bf16[2,256,256]{2,1,0:T(8,128)(2,1)S(1)}, bf16[2,256,256]{2,1,0:T(8,128)(2,1)}, u32[]{:S(2)}) copy-start(bf16[2,256,256]{2,1,0:T(8,128)(2,1)} %param.18) | copy-start | bytes 786436
  115.8 4.1 %copy-start.1 = (bf16[16,64,256]{2,1,0:T(8,128)(2,1)S(1)}, bf16[16,64,256]{2,1,0:T(8,128)(2,1)}, u32[]{:S(2)}) copy-start(bf16[16,64,256]{2,1,0:T(8,128)(2,1)} %shard_map.50) | copy-start | bytes 1572868
  147.4 44.0 %copy-start = (bf16[1024,1024]{1,0:T(8,128)(2,1)S(1)}, bf16[1024,1024]{1,0:T(8,128)(2,1)}, u32[]{:S(2)}) copy-start(bf16[1024,1024]{1,0:T(8,128)(2,1)} %get-tuple-element.88) | copy-start | bytes 6291460
  225.8 3.4 %copy-start.2 = (bf16[16,64,256]{2,1,0:T(8,128)(2,1)S(1)}, bf16[16,64,256]{2,1,0:T(8,128)(2,1)}, u32[]{:S(2)}) copy-start(bf16[16,64,256]{2,1,0:T(8,128)(2,1)} %shard_map.55) | copy-start | bytes 1572868

commit v5 on v4

--- a/solution.py
+++ b/solution.py
@@ -256,12 +256,97 @@
     return out
 
 
-def prow_sum(x, x_devices):
-    y_devices = lax.axis_size("prow") // x_devices
-    part = group_step(x, 1, x_devices, "rs", 10)
-    part = group_step(part, x_devices, y_devices, "rs", 11)
-    part = group_step(part, x_devices, y_devices, "ag", 12)
-    return group_step(part, 1, x_devices, "ag", 13)
+def prow_kernel(xd, yd, x_ref, o_ref, b1, a2, b2, b3, b4, sends, recvs):
+    p = lax.axis_index("prow")
+    q = lax.axis_index("pcol")
+    xi = lax.rem(p, xd)
+    yi = p // xd
+
+    def xdev(k):
+        return (yi * xd + k, q)
+
+    def ydev(k):
+        return (k * xd + xi, q)
+
+    barrier = pltpu.get_barrier_semaphore()
+
+    def greet_x(i, c):
+        pl.semaphore_signal(barrier, 1, device_id=xdev(lax.rem(xi + i, xd)), device_id_type=MESH)
+        return c
+
+    def greet_y(i, c):
+        pl.semaphore_signal(barrier, 1, device_id=ydev(lax.rem(yi + i, yd)), device_id_type=MESH)
+        return c
+
+    lax.fori_loop(1, xd, greet_x, 0)
+    lax.fori_loop(1, yd, greet_y, 0)
+    pl.semaphore_wait(barrier, xd + yd - 2)
+
+    def exchange(phase, src, dst, me, size, dev):
+        def copy(k, s):
+            return pltpu.make_async_remote_copy(
+                src_ref=src(k, s),
+                dst_ref=dst.at[s],
+                send_sem=sends.at[phase, k],
+                recv_sem=recvs.at[phase, s],
+                device_id=dev(k),
+                device_id_type=MESH,
+            )
+
+        def start(i, c):
+            copy(lax.rem(me + i, size), me).start()
+            return c
+
+        lax.fori_loop(1, size, start, 0)
+
+        def wait(i, c):
+            s = lax.rem(me + size - i, size)
+            copy(s, s).wait_recv()
+            copy(lax.rem(me + i, size), me).wait_send()
+            return c
+
+        lax.fori_loop(1, size, wait, 0)
+
+    def total(buf, size):
+        acc = buf[0].astype(jnp.float32)
+        for s in range(1, size):
+            acc = acc + buf[s].astype(jnp.float32)
+        return acc
+
+    exchange(0, lambda k, s: x_ref.at[k], b1, xi, xd, xdev)
+    b1[xi] = x_ref[xi]
+    a2[...] = total(b1, xd).astype(a2.dtype).reshape(a2.shape)
+    exchange(1, lambda k, s: a2.at[k], b2, yi, yd, ydev)
+    b2[yi] = a2[yi]
+    b3[yi] = total(b2, yd).astype(b3.dtype)
+    exchange(2, lambda k, s: b3.at[s], b3, yi, yd, ydev)
+    b4[xi] = b3[...].reshape(b4.shape[1:])
+    exchange(3, lambda k, s: b4.at[s], b4, xi, xd, xdev)
+    o_ref[...] = b4[...]
+
+
+def prow_sum(x, xd):
+    yd = lax.axis_size("prow") // xd
+    rows, cols = x.shape
+    chunks = x.reshape(xd, rows // xd, cols)
+    part = rows // xd // yd
+    out = pl.pallas_call(
+        functools.partial(prow_kernel, xd, yd),
+        out_shape=jax.ShapeDtypeStruct(chunks.shape, x.dtype),
+        in_specs=[pl.BlockSpec(memory_space=pltpu.VMEM)],
+        out_specs=pl.BlockSpec(memory_space=pltpu.VMEM),
+        scratch_shapes=[
+            pltpu.VMEM(chunks.shape, x.dtype),
+            pltpu.VMEM((yd, part, cols), x.dtype),
+            pltpu.VMEM((yd, part, cols), x.dtype),
+            pltpu.VMEM((yd, part, cols), x.dtype),
+            pltpu.VMEM(chunks.shape, x.dtype),
+            pltpu.SemaphoreType.DMA((4, max(xd, yd))),
+            pltpu.SemaphoreType.DMA((4, max(xd, yd))),
+        ],
+        compiler_params=pltpu.CompilerParams(collective_id=10, has_side_effects=True),
+    )(chunks)
+    return out.reshape(rows, cols)
 
 
 def local(x_devices, matrix, pivots, lower_inverse, upper_inverse):

time: 240 us -> 214 us (0.89)
  Pallas kernels: 192 us -> 167 us
    pallas_call x8 -> x2, Pallas kernels: 124 us -> 96.2 us  [prow_sum(): pl.pallas_call(functools.partial(prow_kernel, xd, yd), out_shape=jax.Shap...]
    pallas_call x2, Pallas kernels: 67.3 us -> 70.3 us  [axis_sum(): pl.pallas_call(functools.partial(sum_kernel, axis, other, n, summed, sour...]
where the time goes in v5:
time: 214 us
  Pallas kernels  167 us (78%)
  local copies, waits for them, and re-layouts  19.7 us (9%)
  other arithmetic  15.7 us (7%)
  matrix products  11.4 us (5%)
    pallas_call x2, Pallas kernels, prow_sum(): pl.pallas_call(functools.partial(prow_kernel, xd, yd), out_shape=jax.Shap...  96.2 us
    pallas_call x2, Pallas kernels, axis_sum(): pl.pallas_call(functools.partial(sum_kernel, axis, other, n, summed, sour...  70.3 us
    dot_general x2, matrix products, local(): product = jnp.dot(lower, upper, preferred_element_type=jnp.float32)  6.78 us
    scatter x2, other arithmetic, local(): current.at[:, panel_first:panel_first + block]  5.99 us
    scatter x2, local copies, waits for them, and re-layouts, local(): current = current.at[target].set(old_top, mode='drop')  5.86 us
    gather x2, local copies, waits for them, and re-layouts, local(): current[safe_index]  4.58 us
    reshape x1, local copies, waits for them, and re-layouts, local(): return current.reshape(matrix.shape)  4.49 us

profile of v5, /device:TPU:1, one launch (start us, length us, event | category | flops | bytes accessed | tf_op | source)
XLA Modules:
  0.0 213.6 jit_solution(807713081057644018)
XLA Ops:
  0.0 0.8 and_select_fusion.5
  0.8 2.1 copy.8
  2.9 0.0 copy-start.4
  2.9 1.2 gather_fusion
  4.1 0.0 copy-done.4
  4.2 0.1 broadcast_select_fusion.1
  4.3 1.3 slice_select_fusion.4
  5.5 0.1 copy.9
  5.6 1.0 pad_maximum_fusion
  6.7 47.0 %shard_map.46 = bf16[4,128,1024]{2,1,0:T(8,128)(2,1)} custom-call(bf16[4,128,1024]{2,1,0:T(8,128)(2,1)} %bitcast.78), custom_call_target="tpu_custom_call" | custom-call | tf_op jit(solution)/shard_map/pallas_call | solution.py:333
  53.6 1.3 fusion.46
  54.9 2.8 %scatter_fusion = bf16[1024,1024]{1,0:T(8,128)(2,1)S(1)} fusion(bf16[1024,1024]{1,0:T(8,128)(2,1)S(1)} %bitcast.73, s32[256]{0:T(256)S(1)} %bitcast.91, bf16[256,1024]{1,0:T(8,128)(2,1)S(1)} %bitcast.86), kind=kCustom, calls=%fused_computation.2 | custom fusion | bytes 1573888 | tf_op jit(solution)/shard_map/scatter | solution.py:382
  57.8 0.0 copy-start.3
  57.8 0.2 fusion.8
  58.0 2.0 fusion
  60.0 41.6 %shard_map.47 = bf16[16,64,256]{2,1,0:T(8,128)(2,1)} custom-call(bf16[16,64,256]{2,1,0:T(8,128)(2,1)} %bitcast.90), custom_call_target="tpu_custom_call" | custom-call | tf_op jit(solution)/shard_map/pallas_call | solution.py:153
  101.6 0.0 copy-done.3
  101.6 0.3 convolution_convert_fusion.1
  101.9 0.0 copy-start.1
  102.0 3.4 %and_select_fusion = bf16[1024,1024]{1,0:T(8,128)(2,1)} fusion(bf16[1024,1024]{1,0:T(8,128)(2,1)S(1)} %fusion.8, bf16[1024,256]{1,0:T(8,128)(2,1)} %bitcast.81, bf16[1024,256]{0,1:T(8,128)(2,1)S(1)} %convolution_convert_fusion.1, pred[1024]{0:T(1024)(128)(4,1)S(1)} %get-tuple-element.106, pred[1024]{0:T(1024)(128)(4,1)S(1)} %get-tuple-element.100), kind=kOutput, calls=%fused_computation.6 | convolution fusion | flops 542113792 | bytes 5244928 | tf_op jit(solution)/shard_map/dot_general | solution.py:401
  105.3 0.7 compare_reduce_fusion
  106.1 0.0 copy-done.1
  106.1 3.0 %fusion.2 = bf16[1024,1024]{1,0:T(8,128)(2,1)} fusion(bf16[1024,1024]{1,0:T(8,128)(2,1)} %and_select_fusion, bf16[1024,256]{1,0:T(8,128)(2,1)S(1)} %bitcast.82, pred[1024]{0:T(1024)(128)(4,1)S(1)} %get-tuple-element.103, pred[]{:T(512)} %compare_reduce_fusion), kind=kLoop, calls=%fused_computation.18 | loop fusion | flops 524288 | bytes 1574400 | tf_op jit(solution)/shard_map/scatter | solution.py:405
  109.0 2.1 broadcast_select_fusion.2
  111.1 3.4 %gather_fusion.1 = bf16[256,1024]{1,0:T(8,128)(2,1)S(1)} fusion(bf16[1024,1024]{1,0:T(8,128)(2,1)} %get-tuple-element.88, s32[1024]{0:T(1024)S(1)} %pad_clamp_fusion), kind=kCustom, calls=%fused_computation.1 | custom fusion | bytes 1049600 | tf_op jit(solution)/shard_map/gather | solution.py:372
  114.5 0.1 broadcast_select_fusion
  114.7 1.0 pad_maximum_fusion.1
  115.7 0.0 copy-start
  115.7 49.3 %shard_map.48 = bf16[4,128,1024]{2,1,0:T(8,128)(2,1)} custom-call(bf16[4,128,1024]{2,1,0:T(8,128)(2,1)} %bitcast.79), custom_call_target="tpu_custom_call" | custom-call | tf_op jit(solution)/shard_map/pallas_call | solution.py:333
  165.0 1.3 fusion.45
  166.3 0.0 copy-done
  166.3 3.0 %scatter_fusion.1 = bf16[1024,1024]{1,0:T(8,128)(2,1)S(1)} fusion(bf16[1024,1024]{1,0:T(8,128)(2,1)S(1)} %copy-done, s32[256]{0:T(256)S(1)} %bitcast.92, bf16[256,1024]{1,0:T(8,128)(2,1)S(1)} %bitcast.85), kind=kCustom, calls=%fused_computation.3 | custom fusion | bytes 1573888 | tf_op jit(solution)/shard_map/scatter | solution.py:382
  169.3 0.2 fusion.6
  169.5 2.0 fusion.1
  171.5 28.8 %shard_map.49 = bf16[16,64,256]{2,1,0:T(8,128)(2,1)} custom-call(bf16[16,64,256]{2,1,0:T(8,128)(2,1)} %bitcast.89), custom_call_target="tpu_custom_call" | custom-call | tf_op jit(solution)/shard_map/pallas_call | solution.py:153
  200.3 0.3 convolution_convert_fusion
  200.6 0.0 copy-start.2
  200.6 3.4 %and_select_fusion.1 = bf16[1024,1024]{1,0:T(8,128)(2,1)} fusion(bf16[1024,1024]{1,0:T(8,128)(2,1)S(1)} %fusion.6, bf16[1024,256]{1,0:T(8,128)(2,1)} %bitcast.83, bf16[1024,256]{0,1:T(8,128)(2,1)S(1)} %convolution_convert_fusion, pred[1024]{0:T(1024)(128)(4,1)S(1)} %get-tuple-element.107, pred[1024]{0:T(1024)(128)(4,1)S(1)} %get-tuple-element.101), kind=kOutput, calls=%fused_computation.7 | convolution fusion | flops 542113792 | bytes 5244928 | tf_op jit(solution)/shard_map/dot_general | solution.py:401
  204.0 0.0 copy-done.2
  204.0 3.0 %fusion.3 = bf16[1024,1024]{1,0:T(8,128)(2,1)} fusion(bf16[1024,1024]{1,0:T(8,128)(2,1)} %and_select_fusion.1, bf16[1024,256]{1,0:T(8,128)(2,1)S(1)} %bitcast.84, pred[1024]{0:T(1024)(128)(4,1)S(1)} %get-tuple-element.102, pred[]{:T(512)} %compare_reduce_fusion), kind=kLoop, calls=%fused_computation.19 | loop fusion | flops 524288 | bytes 1574400 | tf_op jit(solution)/shard_map/scatter | solution.py:405
  207.1 2.0 fusion.4
  209.1 4.5 %reshape.688 = bf16[4,256,4,256]{3,2,1,0:T(4,128)(2,1)} reshape(bf16[1024,1024]{1,0:T(8,128)(2,1)} %fusion.4) | data formatting | bytes 4194304 | tf_op jit(solution)/shard_map/reshape | solution.py:412
  (11 shorter events, 0.1 us)
Async XLA Ops:
  2.9 1.2 copy-start.4
  57.8 43.8 %copy-start.3 = (bf16[2,256,256]{2,1,0:T(8,128)(2,1)S(1)}, bf16[2,256,256]{2,1,0:T(8,128)(2,1)}, u32[]{:S(2)}) copy-start(bf16[2,256,256]{2,1,0:T(8,128)(2,1)} %param.18) | copy-start | bytes 786436
  101.9 4.1 %copy-start.1 = (bf16[16,64,256]{2,1,0:T(8,128)(2,1)S(1)}, bf16[16,64,256]{2,1,0:T(8,128)(2,1)}, u32[]{:S(2)}) copy-start(bf16[16,64,256]{2,1,0:T(8,128)(2,1)} %shard_map.47) | copy-start | bytes 1572868
  115.7 50.6 %copy-start = (bf16[1024,1024]{1,0:T(8,128)(2,1)S(1)}, bf16[1024,1024]{1,0:T(8,128)(2,1)}, u32[]{:S(2)}) copy-start(bf16[1024,1024]{1,0:T(8,128)(2,1)} %get-tuple-element.88) | copy-start | bytes 6291460
  200.6 3.4 %copy-start.2 = (bf16[16,64,256]{2,1,0:T(8,128)(2,1)S(1)}, bf16[16,64,256]{2,1,0:T(8,128)(2,1)}, u32[]{:S(2)}) copy-start(bf16[16,64,256]{2,1,0:T(8,128)(2,1)} %shard_map.49) | copy-start | bytes 1572868

commit v6 on v5

--- a/solution.py
+++ b/solution.py
@@ -349,7 +349,125 @@
     return out.reshape(rows, cols)
 
 
-def local(x_devices, matrix, pivots, lower_inverse, upper_inverse):
+def pcol_kernel(nz, source, x_ref, o_ref, g, p1send, p1recv, p2send, p2recv, p3send, p3recv):
+    q = lax.axis_index("pcol")
+    p = lax.axis_index("prow")
+    nc = lax.axis_size("pcol") // nz
+    z = q // nc
+    c = lax.rem(q, nc)
+    zs, cs = source // nc, source % nc
+
+    def dev(zz, cc):
+        return (p, zz * nc + cc)
+
+    barrier = pltpu.get_barrier_semaphore()
+    n = nz * nc
+
+    def greet(i, carry):
+        j = lax.rem(q + i, n)
+        pl.semaphore_signal(barrier, 1, device_id=(p, j), device_id_type=MESH)
+        return carry
+
+    lax.fori_loop(1, n, greet, 0)
+    pl.semaphore_wait(barrier, n - 1)
+
+    def spread(j):
+        return pltpu.make_async_remote_copy(
+            src_ref=x_ref.at[j],
+            dst_ref=g.at[j],
+            send_sem=p1send.at[j],
+            recv_sem=p1recv.at[0],
+            device_id=dev(j, cs),
+            device_id_type=MESH,
+        )
+
+    def ring(j, s):
+        return pltpu.make_async_remote_copy(
+            src_ref=g.at[s],
+            dst_ref=g.at[s],
+            send_sem=p2send.at[j],
+            recv_sem=p2recv.at[s],
+            device_id=dev(j, cs),
+            device_id_type=MESH,
+        )
+
+    def partner(zz):
+        return pltpu.make_async_remote_copy(
+            src_ref=g,
+            dst_ref=g,
+            send_sem=p3send.at[0],
+            recv_sem=p3recv.at[0],
+            device_id=dev(zz, 1 - cs),
+            device_id_type=MESH,
+        )
+
+    @pl.when(q == source)
+    def _():
+        def start(i, carry):
+            spread(lax.rem(zs + i, nz)).start()
+            return carry
+
+        lax.fori_loop(1, nz, start, 0)
+        g[zs] = x_ref[zs]
+
+        def sent(i, carry):
+            spread(lax.rem(zs + i, nz)).wait_send()
+            return carry
+
+        lax.fori_loop(1, nz, sent, 0)
+
+    @pl.when((c == cs) & (z != zs))
+    def _():
+        spread(z).wait_recv()
+
+    @pl.when(c == cs)
+    def _():
+        def start(i, carry):
+            ring(lax.rem(z + i, nz), z).start()
+            return carry
+
+        lax.fori_loop(1, nz, start, 0)
+
+        def wait(i, carry):
+            s = lax.rem(z + nz - i, nz)
+            ring(s, s).wait_recv()
+            ring(lax.rem(z + i, nz), z).wait_send()
+            return carry
+
+        lax.fori_loop(1, nz, wait, 0)
+        partner(z).start()
+        partner(z).wait_send()
+
+    @pl.when(c != cs)
+    def _():
+        partner(z).wait_recv()
+
+    o_ref[...] = g[...]
+
+
+def pcol_bcast(x, nz, source, collective_id):
+    rows, cols = x.shape
+    chunks = x.reshape(nz, rows // nz, cols)
+    out = pl.pallas_call(
+        functools.partial(pcol_kernel, nz, source),
+        out_shape=jax.ShapeDtypeStruct(chunks.shape, x.dtype),
+        in_specs=[pl.BlockSpec(memory_space=pltpu.VMEM)],
+        out_specs=pl.BlockSpec(memory_space=pltpu.VMEM),
+        scratch_shapes=[
+            pltpu.VMEM(chunks.shape, x.dtype),
+            pltpu.SemaphoreType.DMA((nz,)),
+            pltpu.SemaphoreType.DMA((1,)),
+            pltpu.SemaphoreType.DMA((nz,)),
+            pltpu.SemaphoreType.DMA((nz,)),
+            pltpu.SemaphoreType.DMA((1,)),
+            pltpu.SemaphoreType.DMA((1,)),
+        ],
+        compiler_params=pltpu.CompilerParams(collective_id=collective_id, has_side_effects=True),
+    )(chunks)
+    return out.reshape(rows, cols)
+
+
+def local(x_devices, z_chips, matrix, pivots, lower_inverse, upper_inverse):
     row_count = lax.axis_size("prow")
     col_count = lax.axis_size("pcol")
     my_row = lax.axis_index("prow")
@@ -392,7 +510,7 @@
         ).astype(jnp.bfloat16)
         is_panel = my_col == panel_holder
         factor = jnp.where(is_panel, factor, jnp.zeros((), jnp.bfloat16))
-        lower = axis_sum(factor, "pcol", "prow", 2 * panel + 1, 0, panel_holder)
+        lower = pcol_bcast(factor, z_chips, panel_holder, 20 + panel)
         upper = jnp.dot(
             lower_inverse[panel], incoming, preferred_element_type=jnp.float32
         ).astype(jnp.bfloat16)
@@ -414,6 +532,7 @@
 
 def solution(mesh):
     x_devices = len({d.coords[0] for d in mesh.devices[:, 0]})
+    z_chips = len({d.coords[2] for d in mesh.devices[0, :]})
     in_specs = (P(None, "prow", None, "pcol"), P(), P(), P())
     out_specs = P(None, "prow", None, "pcol")
-    return jax.shard_map(functools.partial(local, x_devices), mesh=mesh, in_specs=in_specs, out_specs=out_specs, check_vma=False)
+    return jax.shard_map(functools.partial(local, x_devices, z_chips), mesh=mesh, in_specs=in_specs, out_specs=out_specs, check_vma=False)

time: 214 us -> 203 us (0.949)
  Pallas kernels: 167 us -> 155 us
    pallas_call x2, Pallas kernels: 70.3 us -> 58.2 us  [pcol_bcast(): pl.pallas_call(functools.partial(pcol_kernel, nz, source), out_shape=jax....]
where the time goes in v6:
time: 203 us; the launch traced here: 202 us
  Pallas kernels  155 us (76%)
  local copies, waits for them, and re-layouts  19.7 us (10%)
  other arithmetic  15.7 us (8%)
  matrix products  11.4 us (6%)
    pallas_call x2, Pallas kernels, prow_sum(): pl.pallas_call(functools.partial(prow_kernel, xd, yd), out_shape=jax.Shap...  96.5 us
    pallas_call x2, Pallas kernels, pcol_bcast(): pl.pallas_call(functools.partial(pcol_kernel, nz, source), out_shape=jax....  58.2 us
    dot_general x2, matrix products, local(): product = jnp.dot(lower, upper, preferred_element_type=jnp.float32)  6.78 us
    scatter x2, other arithmetic, local(): current.at[:, panel_first:panel_first + block]  5.99 us
    scatter x2, local copies, waits for them, and re-layouts, local(): current = current.at[target].set(old_top, mode='drop')  5.86 us
    gather x2, local copies, waits for them, and re-layouts, local(): current[safe_index]  4.58 us
    reshape x1, local copies, waits for them, and re-layouts, local(): return current.reshape(matrix.shape)  4.49 us

profile of v6, /device:TPU:1, one launch (start us, length us, event | category | flops | bytes accessed | tf_op | source)
XLA Modules:
  0.0 201.7 jit_solution(15366632868612494014)
XLA Ops:
  0.0 0.8 and_select_fusion.5
  0.8 2.1 %copy.8 = bf16[128,8,4,256]{3,1,2,0:T(8,128)(2,1)S(1)} copy(bf16[128,8,4,256]{3,2,1,0:T(4,128)(2,1)} %bitcast.80) | data formatting | bytes 4194304
  2.9 0.0 copy-start.4
  2.9 1.2 gather_fusion
  4.1 0.0 copy-done.4
  4.2 0.1 broadcast_select_fusion.1
  4.3 1.3 slice_select_fusion.4
  5.5 0.1 copy.9
  5.6 1.0 pad_maximum_fusion
  6.7 47.0 %shard_map.46 = bf16[4,128,1024]{2,1,0:T(8,128)(2,1)} custom-call(bf16[4,128,1024]{2,1,0:T(8,128)(2,1)} %bitcast.78), custom_call_target="tpu_custom_call" | custom-call | tf_op jit(solution)/shard_map/pallas_call | solution.py:333
  53.6 1.3 fusion.46
  54.9 2.8 %scatter_fusion = bf16[1024,1024]{1,0:T(8,128)(2,1)S(1)} fusion(bf16[1024,1024]{1,0:T(8,128)(2,1)S(1)} %bitcast.73, s32[256]{0:T(256)S(1)} %bitcast.91, bf16[256,1024]{1,0:T(8,128)(2,1)S(1)} %bitcast.86), kind=kCustom, calls=%fused_computation.2 | custom fusion | bytes 1573888 | tf_op jit(solution)/shard_map/scatter | solution.py:500
  57.8 0.0 copy-start.3
  57.8 0.2 fusion.8
  58.0 2.0 fusion
  60.0 35.7 %shard_map.47 = bf16[8,128,256]{2,1,0:T(8,128)(2,1)} custom-call(bf16[8,128,256]{2,1,0:T(8,128)(2,1)} %bitcast.90), custom_call_target="tpu_custom_call" | custom-call | tf_op jit(solution)/shard_map/pallas_call | solution.py:451
  95.7 0.0 copy-done.3
  95.7 0.3 convolution_convert_fusion.1
  96.1 0.0 copy-start.1
  96.1 3.4 %and_select_fusion = bf16[1024,1024]{1,0:T(8,128)(2,1)} fusion(bf16[1024,1024]{1,0:T(8,128)(2,1)S(1)} %fusion.8, bf16[1024,256]{1,0:T(8,128)(2,1)} %bitcast.81, bf16[1024,256]{0,1:T(8,128)(2,1)S(1)} %convolution_convert_fusion.1, pred[1024]{0:T(1024)(128)(4,1)S(1)} %get-tuple-element.106, pred[1024]{0:T(1024)(128)(4,1)S(1)} %get-tuple-element.100), kind=kOutput, calls=%fused_computation.6 | convolution fusion | flops 542113792 | bytes 5244928 | tf_op jit(solution)/shard_map/dot_general | solution.py:519
  99.5 0.7 compare_reduce_fusion
  100.2 0.0 copy-done.1
  100.2 3.0 %fusion.2 = bf16[1024,1024]{1,0:T(8,128)(2,1)} fusion(bf16[1024,1024]{1,0:T(8,128)(2,1)} %and_select_fusion, bf16[1024,256]{1,0:T(8,128)(2,1)S(1)} %bitcast.82, pred[1024]{0:T(1024)(128)(4,1)S(1)} %get-tuple-element.103, pred[]{:T(512)} %compare_reduce_fusion), kind=kLoop, calls=%fused_computation.18 | loop fusion | flops 524288 | bytes 1574400 | tf_op jit(solution)/shard_map/scatter | solution.py:523
  103.2 2.1 %broadcast_select_fusion.2 = (bf16[256,1024]{1,0:T(8,128)(2,1)S(1)}, bf16[1024,1024]{1,0:T(8,128)(2,1)}) fusion(pred[]{:T(512)S(6)} %eq.72, bf16[1024,1024]{1,0:T(8,128)(2,1)} %fusion.2, bf16[1024,256]{0,1:T(8,128)(2,1)S(1)} %convolution_convert_fusion.1, pred[1024]{0:T(1024)(128)(4,1)S(1)} %get-tuple-element.109), kind=kLoop, calls=%fused_computation.32 | loop fusion | flops 524288 | bytes 2098177 | tf_op jit(solution)/shard_map/jit(_where)/select_n | solution.py:495
  105.3 3.4 %gather_fusion.1 = bf16[256,1024]{1,0:T(8,128)(2,1)S(1)} fusion(bf16[1024,1024]{1,0:T(8,128)(2,1)} %get-tuple-element.88, s32[1024]{0:T(1024)S(1)} %pad_clamp_fusion), kind=kCustom, calls=%fused_computation.1 | custom fusion | bytes 1049600 | tf_op jit(solution)/shard_map/gather | solution.py:490
  108.7 0.1 broadcast_select_fusion
  108.8 1.0 pad_maximum_fusion.1
  109.8 0.0 copy-start
  109.8 49.5 %shard_map.48 = bf16[4,128,1024]{2,1,0:T(8,128)(2,1)} custom-call(bf16[4,128,1024]{2,1,0:T(8,128)(2,1)} %bitcast.79), custom_call_target="tpu_custom_call" | custom-call | tf_op jit(solution)/shard_map/pallas_call | solution.py:333
  159.4 1.3 fusion.45
  160.6 0.0 copy-done
  160.7 3.0 %scatter_fusion.1 = bf16[1024,1024]{1,0:T(8,128)(2,1)S(1)} fusion(bf16[1024,1024]{1,0:T(8,128)(2,1)S(1)} %copy-done, s32[256]{0:T(256)S(1)} %bitcast.92, bf16[256,1024]{1,0:T(8,128)(2,1)S(1)} %bitcast.85), kind=kCustom, calls=%fused_computation.3 | custom fusion | bytes 1573888 | tf_op jit(solution)/shard_map/scatter | solution.py:500
  163.7 0.2 fusion.6
  163.9 2.0 %fusion.1 = bf16[1024,256]{1,0:T(8,128)(2,1)} fusion(bf16[1024,1024]{1,0:T(8,128)(2,1)S(1)} %fusion.6, pred[]{:T(512)S(6)} %eq.73, bf16[2,256,256]{2,1,0:T(8,128)(2,1)} %param.19), kind=kOutput, calls=%fused_computation.13 | convolution fusion | flops 134742016 | bytes 1179649 | tf_op jit(solution)/shard_map/dot_general | solution.py:508
  165.9 22.5 %shard_map.49 = bf16[8,128,256]{2,1,0:T(8,128)(2,1)} custom-call(bf16[8,128,256]{2,1,0:T(8,128)(2,1)} %bitcast.89), custom_call_target="tpu_custom_call" | custom-call | tf_op jit(solution)/shard_map/pallas_call | solution.py:451
  188.4 0.3 convolution_convert_fusion
  188.7 0.0 copy-start.2
  188.7 3.4 %and_select_fusion.1 = bf16[1024,1024]{1,0:T(8,128)(2,1)} fusion(bf16[1024,1024]{1,0:T(8,128)(2,1)S(1)} %fusion.6, bf16[1024,256]{1,0:T(8,128)(2,1)} %bitcast.83, bf16[1024,256]{0,1:T(8,128)(2,1)S(1)} %convolution_convert_fusion, pred[1024]{0:T(1024)(128)(4,1)S(1)} %get-tuple-element.107, pred[1024]{0:T(1024)(128)(4,1)S(1)} %get-tuple-element.101), kind=kOutput, calls=%fused_computation.7 | convolution fusion | flops 542113792 | bytes 5244928 | tf_op jit(solution)/shard_map/dot_general | solution.py:519
  192.1 0.0 copy-done.2
  192.1 3.0 %fusion.3 = bf16[1024,1024]{1,0:T(8,128)(2,1)} fusion(bf16[1024,1024]{1,0:T(8,128)(2,1)} %and_select_fusion.1, bf16[1024,256]{1,0:T(8,128)(2,1)S(1)} %bitcast.84, pred[1024]{0:T(1024)(128)(4,1)S(1)} %get-tuple-element.102, pred[]{:T(512)} %compare_reduce_fusion), kind=kLoop, calls=%fused_computation.19 | loop fusion | flops 524288 | bytes 1574400 | tf_op jit(solution)/shard_map/scatter | solution.py:523
  195.2 2.0 %fusion.4 = bf16[1024,1024]{1,0:T(8,128)(2,1)} fusion(bf16[1024,1024]{1,0:T(8,128)(2,1)} %fusion.3, bf16[1024,256]{0,1:T(8,128)(2,1)S(1)} %convolution_convert_fusion, pred[1024]{0:T(1024)(128)(4,1)S(1)} %get-tuple-element.108), kind=kLoop, calls=%fused_computation.21 | loop fusion | flops 262144 | bytes 1573888 | tf_op jit(solution)/shard_map/scatter | solution.py:527
  197.2 4.5 %reshape.688 = bf16[4,256,4,256]{3,2,1,0:T(4,128)(2,1)} reshape(bf16[1024,1024]{1,0:T(8,128)(2,1)} %fusion.4) | data formatting | bytes 4194304 | tf_op jit(solution)/shard_map/reshape | solution.py:530
  (11 shorter events, 0.1 us)
Async XLA Ops:
  2.9 1.2 copy-start.4
  57.8 38.0 %copy-start.3 = (bf16[2,256,256]{2,1,0:T(8,128)(2,1)S(1)}, bf16[2,256,256]{2,1,0:T(8,128)(2,1)}, u32[]{:S(2)}) copy-start(bf16[2,256,256]{2,1,0:T(8,128)(2,1)} %param.18) | copy-start | bytes 786436
  96.1 4.1 %copy-start.1 = (bf16[8,128,256]{2,1,0:T(8,128)(2,1)S(1)}, bf16[8,128,256]{2,1,0:T(8,128)(2,1)}, u32[]{:S(2)}) copy-start(bf16[8,128,256]{2,1,0:T(8,128)(2,1)} %shard_map.47) | copy-start | bytes 1572868
  109.8 50.8 %copy-start = (bf16[1024,1024]{1,0:T(8,128)(2,1)S(1)}, bf16[1024,1024]{1,0:T(8,128)(2,1)}, u32[]{:S(2)}) copy-start(bf16[1024,1024]{1,0:T(8,128)(2,1)} %get-tuple-element.88) | copy-start | bytes 6291460
  188.7 3.4 %copy-start.2 = (bf16[8,128,256]{2,1,0:T(8,128)(2,1)S(1)}, bf16[8,128,256]{2,1,0:T(8,128)(2,1)}, u32[]{:S(2)}) copy-start(bf16[8,128,256]{2,1,0:T(8,128)(2,1)} %shard_map.49) | copy-start | bytes 1572868

commit v7 on v6

--- a/solution.py
+++ b/solution.py
@@ -256,11 +256,12 @@
     return out
 
 
-def prow_kernel(xd, yd, x_ref, o_ref, b1, a2, b2, b3, b4, sends, recvs):
+def prow_kernel(xd, yd, top, t_ref, o_ref, b1, a2, b2, b3, b4, sends, recvs, tsend, trecv):
     p = lax.axis_index("prow")
     q = lax.axis_index("pcol")
     xi = lax.rem(p, xd)
     yi = p // xd
+    xt, yt = top % xd, top // xd
 
     def xdev(k):
         return (yi * xd + k, q)
@@ -286,7 +287,7 @@
         def copy(k, s):
             return pltpu.make_async_remote_copy(
                 src_ref=src(k, s),
-                dst_ref=dst.at[s],
+                dst_ref=dst(s),
                 send_sem=sends.at[phase, k],
                 recv_sem=recvs.at[phase, s],
                 device_id=dev(k),
@@ -307,46 +308,90 @@
 
         lax.fori_loop(1, size, wait, 0)
 
-    def total(buf, size):
-        acc = buf[0].astype(jnp.float32)
+    def total(parts, size):
+        acc = parts(0).astype(jnp.float32)
         for s in range(1, size):
-            acc = acc + buf[s].astype(jnp.float32)
+            acc = acc + parts(s).astype(jnp.float32)
         return acc
 
-    exchange(0, lambda k, s: x_ref.at[k], b1, xi, xd, xdev)
-    b1[xi] = x_ref[xi]
-    a2[...] = total(b1, xd).astype(a2.dtype).reshape(a2.shape)
-    exchange(1, lambda k, s: a2.at[k], b2, yi, yd, ydev)
+    def top_copy(k):
+        return pltpu.make_async_remote_copy(
+            src_ref=t_ref.at[k, 1],
+            dst_ref=b1.at[xt, 1],
+            send_sem=tsend.at[k],
+            recv_sem=trecv.at[0],
+            device_id=xdev(k),
+            device_id_type=MESH,
+        )
+
+    @pl.when(p == top)
+    def _():
+        def start(i, c):
+            top_copy(lax.rem(xi + i, xd)).start()
+            return c
+
+        lax.fori_loop(1, xd, start, 0)
+
+    exchange(0, lambda k, s: t_ref.at[k, 0], lambda s: b1.at[s, 0], xi, xd, xdev)
+    b1[xi, 0] = t_ref[xi, 0]
+    top_half = (yd // 2, b1.shape[2] * 2 // yd, b1.shape[3])
+    a2[: yd // 2] = total(lambda s: b1[s, 0], xd).astype(a2.dtype).reshape(top_half)
+
+    @pl.when(p == top)
+    def _():
+        def sent(i, c):
+            top_copy(lax.rem(xi + i, xd)).wait_send()
+            return c
+
+        lax.fori_loop(1, xd, sent, 0)
+        a3 = t_ref[xi, 1]
+        a2[yd // 2 :] = a3.reshape(top_half)
+
+    @pl.when((yi == yt) & (p != top))
+    def _():
+        top_copy(xi).wait_recv()
+        a2[yd // 2 :] = b1[xt, 1].reshape(top_half)
+
+    @pl.when(yi != yt)
+    def _():
+        a2[yd // 2 :] = jnp.zeros(top_half, a2.dtype)
+
+    exchange(1, lambda k, s: a2.at[k], lambda s: b2.at[s], yi, yd, ydev)
     b2[yi] = a2[yi]
-    b3[yi] = total(b2, yd).astype(b3.dtype)
-    exchange(2, lambda k, s: b3.at[s], b3, yi, yd, ydev)
+    b3[yi] = total(lambda s: b2[s], yd).astype(b3.dtype)
+    exchange(2, lambda k, s: b3.at[s], lambda s: b3.at[s], yi, yd, ydev)
     b4[xi] = b3[...].reshape(b4.shape[1:])
-    exchange(3, lambda k, s: b4.at[s], b4, xi, xd, xdev)
+    exchange(3, lambda k, s: b4.at[s], lambda s: b4.at[s], xi, xd, xdev)
     o_ref[...] = b4[...]
 
 
-def prow_sum(x, xd):
+def prow_sum(picked, top_part, xd, top):
     yd = lax.axis_size("prow") // xd
-    rows, cols = x.shape
-    chunks = x.reshape(xd, rows // xd, cols)
-    part = rows // xd // yd
+    rows, cols = picked.shape
+    chunks = jnp.stack(
+        [picked.reshape(xd, rows // xd, cols), top_part.reshape(xd, rows // xd, cols)], axis=1
+    )
+    part = 2 * rows // xd // yd
     out = pl.pallas_call(
-        functools.partial(prow_kernel, xd, yd),
-        out_shape=jax.ShapeDtypeStruct(chunks.shape, x.dtype),
+        functools.partial(prow_kernel, xd, yd, top),
+        out_shape=jax.ShapeDtypeStruct((xd, yd, part, cols), picked.dtype),
         in_specs=[pl.BlockSpec(memory_space=pltpu.VMEM)],
         out_specs=pl.BlockSpec(memory_space=pltpu.VMEM),
         scratch_shapes=[
-            pltpu.VMEM(chunks.shape, x.dtype),
-            pltpu.VMEM((yd, part, cols), x.dtype),
-            pltpu.VMEM((yd, part, cols), x.dtype),
-            pltpu.VMEM((yd, part, cols), x.dtype),
-            pltpu.VMEM(chunks.shape, x.dtype),
+            pltpu.VMEM(chunks.shape, picked.dtype),
+            pltpu.VMEM((yd, part, cols), picked.dtype),
+            pltpu.VMEM((yd, part, cols), picked.dtype),
+            pltpu.VMEM((yd, part, cols), picked.dtype),
+            pltpu.VMEM((xd, yd, part, cols), picked.dtype),
             pltpu.SemaphoreType.DMA((4, max(xd, yd))),
             pltpu.SemaphoreType.DMA((4, max(xd, yd))),
+            pltpu.SemaphoreType.DMA((xd,)),
+            pltpu.SemaphoreType.DMA((1,)),
         ],
-        compiler_params=pltpu.CompilerParams(collective_id=10, has_side_effects=True),
+        compiler_params=pltpu.CompilerParams(collective_id=10 + top, has_side_effects=True),
     )(chunks)
-    return out.reshape(rows, cols)
+    out = out.reshape(xd, 2, rows // xd, cols)
+    return out[:, 0].reshape(rows, cols), out[:, 1].reshape(rows, cols)
 
 
 def pcol_kernel(nz, source, x_ref, o_ref, g, p1send, p1recv, p2send, p2recv, p3send, p3recv):
@@ -493,9 +538,7 @@
         is_top = my_row == top_holder
         top_local = current[top_first : top_first + block]
         top_part = jnp.where(is_top, top_local, jnp.zeros((), jnp.bfloat16))
-        both = prow_sum(jnp.concatenate([picked, top_part], axis=0), x_devices)
-        incoming = both[:block]
-        old_top = both[block:]
+        incoming, old_top = prow_sum(picked, top_part, x_devices, top_holder)
         target = jnp.where(is_mine, local_index, local_rows)
         current = current.at[target].set(old_top, mode="drop")
         top_now = current[top_first : top_first + block]

time: 203 us -> 197 us (0.970)
  Pallas kernels: 155 us -> 146 us
    pallas_call x2, Pallas kernels: 96.5 us -> 89.4 us  [prow_sum(): pl.pallas_call(functools.partial(prow_kernel, xd, yd, top), out_shape=jax...]
    another operation x1 -> x3, other arithmetic: 0.72 us -> 3.89 us  [the longest x2 3.17 us: prow_sum(): jnp.stack([picked.reshape(xd, rows // xd, cols), top_part.reshape(xd, row...]
    concatenate x2 -> x0, other arithmetic: 2.07 us -> none  [local(): both = prow_sum(jnp.concatenate([picked, top_part], axis=0), x_devices)]
where the time goes in v7:
time: 197 us; the launch traced here: 196 us
  Pallas kernels  146 us (74%)
  local copies, waits for them, and re-layouts  20.2 us (10%)
  other arithmetic  17.6 us (9%)
  matrix products  11.4 us (6%)
    pallas_call x2, Pallas kernels, prow_sum(): pl.pallas_call(functools.partial(prow_kernel, xd, yd, top), out_shape=jax...  89.4 us
    pallas_call x2, Pallas kernels, pcol_bcast(): pl.pallas_call(functools.partial(pcol_kernel, nz, source), out_shape=jax....  56.9 us
    dot_general x2, matrix products, local(): product = jnp.dot(lower, upper, preferred_element_type=jnp.float32)  6.78 us
    scatter x2, other arithmetic, local(): current.at[:, panel_first:panel_first + block]  5.97 us
    scatter x2, local copies, waits for them, and re-layouts, local(): current = current.at[target].set(old_top, mode='drop')  5.86 us
    gather x2, local copies, waits for them, and re-layouts, local(): current[safe_index]  4.58 us
    reshape x1, local copies, waits for them, and re-layouts, local(): return current.reshape(matrix.shape)  4.49 us
    dot_general x2, matrix products, local(): jnp.dot(panel_cols, upper_inverse[panel], preferred_element_type=jnp.floa...  4 us

profile of v7, /device:TPU:1, one launch (start us, length us, event | category | flops | bytes accessed | tf_op | source)
XLA Modules:
  0.0 195.7 jit_solution(17587915470976522740)
XLA Ops:
  0.0 0.8 and_select_fusion.5
  0.8 2.1 %copy.8 = bf16[128,8,4,256]{3,1,2,0:T(8,128)(2,1)S(1)} copy(bf16[128,8,4,256]{3,2,1,0:T(4,128)(2,1)} %bitcast.78) | data formatting | bytes 4194304
  2.9 0.0 copy-start.4
  2.9 1.2 gather_fusion
  4.1 0.0 copy-done.4
  4.1 0.1 squeeze.23
  4.2 0.1 squeeze.27
  4.3 0.9 broadcast_select_fusion.2
  5.2 1.3 slice_select_fusion.4
  6.5 0.4 select_n.399
  6.9 2.1 %pad_maximum_fusion.t_ref = bf16[4,2,64,1024]{3,2,1,0:T(8,128)(2,1)} fusion(bf16[4,1,64,1024]{3,2,1,0:T(8,128)(2,1)S(1)} %select_n.399, bf16[4,1,64,1024]{3,2,1,0:T(8,128)(2,1)} %broadcast_select_fusion.2), kind=kLoop, calls=%fused_computation.14 | loop fusion | flops 524288 | bytes 2097152 | tf_op jit(solution)/shard_map/stack | solution.py:371
  9.0 45.6 %shard_map.46 = bf16[4,8,16,1024]{3,2,1,0:T(8,128)(2,1)} custom-call(bf16[4,2,64,1024]{3,2,1,0:T(8,128)(2,1)} %pad_maximum_fusion.t_ref), custom_call_target="tpu_custom_call" | custom-call | tf_op jit(solution)/shard_map/pallas_call | solution.py:375
  54.6 1.3 fusion.50
  55.9 2.8 %scatter_fusion = bf16[1024,1024]{1,0:T(8,128)(2,1)S(1)} fusion(bf16[1024,1024]{1,0:T(8,128)(2,1)S(1)} %bitcast.71, s32[256]{0:T(256)S(1)} %bitcast.90, bf16[256,1024]{1,0:T(8,128)(2,1)S(1)} %bitcast.86), kind=kCustom, calls=%fused_computation.2 | custom fusion | bytes 1573888 | tf_op jit(solution)/shard_map/scatter | solution.py:543
  58.7 0.0 copy-start.3
  58.7 0.2 fusion.8
  59.0 2.0 %fusion = bf16[1024,256]{1,0:T(8,128)(2,1)} fusion(bf16[1024,1024]{1,0:T(8,128)(2,1)S(1)} %fusion.8, pred[]{:T(512)S(6)} %eq.69, bf16[2,256,256]{2,1,0:T(8,128)(2,1)} %param.19), kind=kOutput, calls=%fused_computation.12 | convolution fusion | flops 134742016 | bytes 1179649 | tf_op jit(solution)/shard_map/dot_general | solution.py:551
  61.0 34.0 %shard_map.47 = bf16[8,128,256]{2,1,0:T(8,128)(2,1)} custom-call(bf16[8,128,256]{2,1,0:T(8,128)(2,1)} %bitcast.89), custom_call_target="tpu_custom_call" | custom-call | tf_op jit(solution)/shard_map/pallas_call | solution.py:496
  95.0 0.0 copy-done.3
  95.0 0.3 convolution_convert_fusion.1
  95.3 0.0 copy-start.1
  95.3 3.4 %and_select_fusion = bf16[1024,1024]{1,0:T(8,128)(2,1)} fusion(bf16[1024,1024]{1,0:T(8,128)(2,1)S(1)} %fusion.8, bf16[1024,256]{1,0:T(8,128)(2,1)} %bitcast.79, bf16[1024,256]{0,1:T(8,128)(2,1)S(1)} %convolution_convert_fusion.1, pred[1024]{0:T(1024)(128)(4,1)S(1)} %get-tuple-element.106, pred[1024]{0:T(1024)(128)(4,1)S(1)} %get-tuple-element.100), kind=kOutput, calls=%fused_computation.6 | convolution fusion | flops 542113792 | bytes 5244928 | tf_op jit(solution)/shard_map/dot_general | solution.py:562
  98.7 0.7 compare_reduce_fusion
  99.4 0.0 copy-done.1
  99.4 3.0 %fusion.2 = bf16[1024,1024]{1,0:T(8,128)(2,1)} fusion(bf16[1024,1024]{1,0:T(8,128)(2,1)} %and_select_fusion, bf16[1024,256]{1,0:T(8,128)(2,1)S(1)} %bitcast.80, pred[1024]{0:T(1024)(128)(4,1)S(1)} %get-tuple-element.105, pred[]{:T(512)} %compare_reduce_fusion), kind=kLoop, calls=%fused_computation.18 | loop fusion | flops 524288 | bytes 1574400 | tf_op jit(solution)/shard_map/scatter | solution.py:566
  102.4 2.1 %broadcast_select_fusion = (bf16[256,1024]{1,0:T(8,128)(2,1)S(1)}, bf16[1024,1024]{1,0:T(8,128)(2,1)}) fusion(pred[]{:T(512)S(6)} %eq.72, bf16[1024,1024]{1,0:T(8,128)(2,1)} %fusion.2, bf16[1024,256]{0,1:T(8,128)(2,1)S(1)} %convolution_convert_fusion.1, pred[1024]{0:T(1024)(128)(4,1)S(1)} %get-tuple-element.109), kind=kLoop, calls=%fused_computation.30 | loop fusion | flops 524288 | bytes 2098177 | tf_op jit(solution)/shard_map/jit(_where)/select_n | solution.py:540
  104.5 3.4 %gather_fusion.1 = bf16[256,1024]{1,0:T(8,128)(2,1)S(1)} fusion(bf16[1024,1024]{1,0:T(8,128)(2,1)} %get-tuple-element.90, s32[1024]{0:T(1024)S(1)} %pad_clamp_fusion), kind=kCustom, calls=%fused_computation.1 | custom fusion | bytes 1049600 | tf_op jit(solution)/shard_map/gather | solution.py:535
  107.9 0.1 broadcast_select_fusion.1
  108.0 1.1 pad_maximum_fusion.1.t_ref
  109.1 0.0 copy-start
  109.1 43.8 %shard_map.48 = bf16[4,8,16,1024]{3,2,1,0:T(8,128)(2,1)} custom-call(bf16[4,2,64,1024]{3,2,1,0:T(8,128)(2,1)} %pad_maximum_fusion.1.t_ref), custom_call_target="tpu_custom_call" | custom-call | tf_op jit(solution)/shard_map/pallas_call | solution.py:375
  152.9 1.3 fusion.49
  154.2 0.0 copy-done
  154.2 3.0 %scatter_fusion.1 = bf16[1024,1024]{1,0:T(8,128)(2,1)S(1)} fusion(bf16[1024,1024]{1,0:T(8,128)(2,1)S(1)} %copy-done, s32[256]{0:T(256)S(1)} %bitcast.91, bf16[256,1024]{1,0:T(8,128)(2,1)S(1)} %bitcast.85), kind=kCustom, calls=%fused_computation.3 | custom fusion | bytes 1573888 | tf_op jit(solution)/shard_map/scatter | solution.py:543
  157.3 0.2 fusion.6
  157.5 2.0 %fusion.1 = bf16[1024,256]{1,0:T(8,128)(2,1)} fusion(bf16[1024,1024]{1,0:T(8,128)(2,1)S(1)} %fusion.6, pred[]{:T(512)S(6)} %eq.73, bf16[2,256,256]{2,1,0:T(8,128)(2,1)} %param.19), kind=kOutput, calls=%fused_computation.13 | convolution fusion | flops 134742016 | bytes 1179649 | tf_op jit(solution)/shard_map/dot_general | solution.py:551
  159.5 22.9 %shard_map.49 = bf16[8,128,256]{2,1,0:T(8,128)(2,1)} custom-call(bf16[8,128,256]{2,1,0:T(8,128)(2,1)} %bitcast.88), custom_call_target="tpu_custom_call" | custom-call | tf_op jit(solution)/shard_map/pallas_call | solution.py:496
  182.4 0.3 convolution_convert_fusion
  182.7 0.0 copy-start.2
  182.8 3.4 %and_select_fusion.1 = bf16[1024,1024]{1,0:T(8,128)(2,1)} fusion(bf16[1024,1024]{1,0:T(8,128)(2,1)S(1)} %fusion.6, bf16[1024,256]{1,0:T(8,128)(2,1)} %bitcast.81, bf16[1024,256]{0,1:T(8,128)(2,1)S(1)} %convolution_convert_fusion, pred[1024]{0:T(1024)(128)(4,1)S(1)} %get-tuple-element.107, pred[1024]{0:T(1024)(128)(4,1)S(1)} %get-tuple-element.101), kind=kOutput, calls=%fused_computation.7 | convolution fusion | flops 542113792 | bytes 5244928 | tf_op jit(solution)/shard_map/dot_general | solution.py:562
  186.2 0.0 copy-done.2
  186.2 3.0 %fusion.3 = bf16[1024,1024]{1,0:T(8,128)(2,1)} fusion(bf16[1024,1024]{1,0:T(8,128)(2,1)} %and_select_fusion.1, bf16[1024,256]{1,0:T(8,128)(2,1)S(1)} %bitcast.82, pred[1024]{0:T(1024)(128)(4,1)S(1)} %get-tuple-element.104, pred[]{:T(512)} %compare_reduce_fusion), kind=kLoop, calls=%fused_computation.19 | loop fusion | flops 524288 | bytes 1574400 | tf_op jit(solution)/shard_map/scatter | solution.py:566
  189.2 2.0 %fusion.4 = bf16[1024,1024]{1,0:T(8,128)(2,1)} fusion(bf16[1024,1024]{1,0:T(8,128)(2,1)} %fusion.3, bf16[1024,256]{0,1:T(8,128)(2,1)S(1)} %convolution_convert_fusion, pred[1024]{0:T(1024)(128)(4,1)S(1)} %get-tuple-element.108), kind=kLoop, calls=%fused_computation.21 | loop fusion | flops 262144 | bytes 1573888 | tf_op jit(solution)/shard_map/scatter | solution.py:570
  191.2 4.5 %reshape.726 = bf16[4,256,4,256]{3,2,1,0:T(4,128)(2,1)} reshape(bf16[1024,1024]{1,0:T(8,128)(2,1)} %fusion.4) | data formatting | bytes 4194304 | tf_op jit(solution)/shard_map/reshape | solution.py:573
  (11 shorter events, 0.1 us)
Async XLA Ops:
  2.9 1.2 copy-start.4
  58.7 36.2 %copy-start.3 = (bf16[2,256,256]{2,1,0:T(8,128)(2,1)S(1)}, bf16[2,256,256]{2,1,0:T(8,128)(2,1)}, u32[]{:S(2)}) copy-start(bf16[2,256,256]{2,1,0:T(8,128)(2,1)} %param.18) | copy-start | bytes 786436
  95.3 4.1 %copy-start.1 = (bf16[8,128,256]{2,1,0:T(8,128)(2,1)S(1)}, bf16[8,128,256]{2,1,0:T(8,128)(2,1)}, u32[]{:S(2)}) copy-start(bf16[8,128,256]{2,1,0:T(8,128)(2,1)} %shard_map.47) | copy-start | bytes 1572868
  109.1 45.1 %copy-start = (bf16[1024,1024]{1,0:T(8,128)(2,1)S(1)}, bf16[1024,1024]{1,0:T(8,128)(2,1)}, u32[]{:S(2)}) copy-start(bf16[1024,1024]{1,0:T(8,128)(2,1)} %get-tuple-element.90) | copy-start | bytes 6291460
  182.7 3.4 %copy-start.2 = (bf16[8,128,256]{2,1,0:T(8,128)(2,1)S(1)}, bf16[8,128,256]{2,1,0:T(8,128)(2,1)}, u32[]{:S(2)}) copy-start(bf16[8,128,256]{2,1,0:T(8,128)(2,1)} %shard_map.49) | copy-start | bytes 1572868

commit v8 on v7

--- a/solution.py
+++ b/solution.py
@@ -561,14 +561,24 @@
         col_mask = global_cols >= start + block
         product = jnp.dot(lower, upper, preferred_element_type=jnp.float32)
         changed = (current.astype(jnp.float32) - product).astype(jnp.bfloat16)
-        current = jnp.where(row_mask[:, None] & col_mask[None, :], changed, current)
-        panel_now = current[:, panel_first : panel_first + block]
-        current = current.at[:, panel_first : panel_first + block].set(
-            jnp.where(is_panel & row_mask[:, None], lower, panel_now)
-        )
-        top_now = current[top_first : top_first + block]
-        current = current.at[top_first : top_first + block].set(
-            jnp.where(is_top & col_mask[None, :], upper, top_now)
+        below = row_mask[:, None]
+        right = col_mask[None, :]
+        in_panel = is_panel & (col_place // block == panel_first // block)[None, :]
+        in_top = is_top & (row_place // block == top_first // block)[:, None]
+        lower_wide = jnp.broadcast_to(
+            lower[:, None, :], (local_rows, blocks_across, block)
+        ).reshape(local_rows, local_cols)
+        upper_tall = jnp.broadcast_to(
+            upper[None], (blocks_down, block, local_cols)
+        ).reshape(local_rows, local_cols)
+        current = jnp.where(
+            below & right,
+            changed,
+            jnp.where(
+                in_panel & below,
+                lower_wide,
+                jnp.where(in_top & right, upper_tall, current),
+            ),
         )
     return current.reshape(matrix.shape)
 

time: 197 us -> 195 us (0.990)
  other arithmetic: 17.6 us -> 6.8 us
  local copies, waits for them, and re-layouts: 20.2 us -> 26.8 us
  matrix products: 11.4 us -> 14.2 us
    scatter x2 -> x0, other arithmetic: 5.97 us -> none  [local(): current.at[:, panel_first:panel_first + block]]
    unnamed x11 -> x23, local copies, waits for them, and re-layouts: 2.1 us -> 5.76 us
    dot_general x2, matrix products: 6.78 us -> 10 us  [local(): product = jnp.dot(lower, upper, preferred_element_type=jnp.float32)]
    broadcast_in_dim x0 -> x2, local copies, waits for them, and re-layouts: none -> 3.17 us  [local(): jnp.broadcast_to(lower[:, None, :], (local_rows, blocks_across, block))]
    gather x2, local copies, waits for them, and re-layouts: 4.58 us -> 2.34 us  [local(): current[safe_index]]
    select_n x2, other arithmetic: 3.34 us -> 1.3 us  [local(): top_part = jnp.where(is_top, top_local, jnp.zeros((), jnp.bfloat16))]
    scatter x3 -> x2, other arithmetic: 2.46 us -> 0.43 us  [local(): current.at[top_first:top_first + block]]
    convert_element_type x0 -> x2, local copies, waits for them, and re-layouts: none -> 2.02 us  [local(): upper = jnp.dot(lower_inverse[panel], incoming, preferred_element_type=jn...]
where the time goes in v8:
time: 195 us; the launch traced here: 194 us
  Pallas kernels  146 us (75%)
  local copies, waits for them, and re-layouts  26.8 us (14%)
  matrix products  14.2 us (7%)
  other arithmetic  6.8 us (3%)
    pallas_call x2, Pallas kernels, prow_sum(): pl.pallas_call(functools.partial(prow_kernel, xd, yd, top), out_shape=jax...  89.8 us
    pallas_call x2, Pallas kernels, pcol_bcast(): pl.pallas_call(functools.partial(pcol_kernel, nz, source), out_shape=jax....  56.3 us
    dot_general x2, matrix products, local(): product = jnp.dot(lower, upper, preferred_element_type=jnp.float32)  10 us
    scatter x2, local copies, waits for them, and re-layouts, local(): current = current.at[target].set(old_top, mode='drop')  5.86 us
    unnamed x23, local copies, waits for them, and re-layouts  5.76 us
    reshape x1, local copies, waits for them, and re-layouts, local(): return current.reshape(matrix.shape)  4.49 us

profile of v8, /device:TPU:1, one launch (start us, length us, event | category | flops | bytes accessed | tf_op | source)
XLA Modules:
  0.0 194.1 jit_solution(5562751250964302502)
XLA Ops:
  0.0 0.8 and_select_fusion.9
  0.8 2.1 %copy.9 = bf16[128,8,4,256]{3,1,2,0:T(8,128)(2,1)S(1)} copy(bf16[128,8,4,256]{3,2,1,0:T(4,128)(2,1)} %bitcast.90) | data formatting | bytes 4194304
  2.9 0.0 copy-start.8
  2.9 1.2 gather_fusion
  4.1 0.0 copy-done.8
  4.1 0.1 squeeze.23
  4.2 0.1 squeeze.27
  4.3 0.9 broadcast_select_fusion.1
  5.2 1.3 slice_select_fusion.3
  6.5 0.4 select_n.397
  6.9 2.1 %pad_maximum_fusion.t_ref = bf16[4,2,64,1024]{3,2,1,0:T(8,128)(2,1)} fusion(bf16[4,1,64,1024]{3,2,1,0:T(8,128)(2,1)S(1)} %select_n.397, bf16[4,1,64,1024]{3,2,1,0:T(8,128)(2,1)} %broadcast_select_fusion.1), kind=kLoop, calls=%fused_computation.18 | loop fusion | flops 524288 | bytes 2097152 | tf_op jit(solution)/shard_map/stack | solution.py:371
  9.0 45.6 %shard_map.46 = bf16[4,8,16,1024]{3,2,1,0:T(8,128)(2,1)} custom-call(bf16[4,2,64,1024]{3,2,1,0:T(8,128)(2,1)} %pad_maximum_fusion.t_ref), custom_call_target="tpu_custom_call" | custom-call | tf_op jit(solution)/shard_map/pallas_call | solution.py:375
  54.6 1.3 fusion.51
  55.9 0.0 copy-start.5
  55.9 0.0 copy-start.9
  55.9 2.8 %scatter_fusion = bf16[1024,1024]{1,0:T(8,128)(2,1)S(1)} fusion(bf16[1024,1024]{1,0:T(8,128)(2,1)S(1)} %bitcast.73, s32[256]{0:T(256)S(1)} %bitcast.98, bf16[256,1024]{1,0:T(8,128)(2,1)S(1)} %bitcast.94), kind=kCustom, calls=%fused_computation.2 | custom fusion | bytes 1573888 | tf_op jit(solution)/shard_map/scatter | solution.py:543
  58.8 0.0 copy-done.5
  58.8 0.2 fusion.5
  59.0 0.0 copy-start
  59.0 0.0 copy-done.9
  59.0 1.4 fusion
  60.4 34.0 %shard_map.47 = bf16[8,128,256]{2,1,0:T(8,128)(2,1)} custom-call(bf16[8,128,256]{2,1,0:T(8,128)(2,1)} %bitcast.96), custom_call_target="tpu_custom_call" | custom-call | tf_op jit(solution)/shard_map/pallas_call | solution.py:496
  94.4 1.6 broadcast_in_dim.78
  96.0 0.0 copy-done
  96.0 0.0 copy-start.6
  96.0 0.0 copy-start.7
  96.0 1.8 copy.10
  97.9 0.0 copy-start.1
  97.9 0.0 copy-done.6
  97.9 0.0 copy-done.7
  97.9 0.4 convolution_convert_fusion.2
  98.2 1.0 copy.7
  99.3 0.0 copy-done.1
  99.3 5.3 %and_select_fusion.4 = bf16[1024,1024]{1,0:T(8,128)(2,1)S(1)} fusion(bf16[1024,1024]{1,0:T(8,128)(2,1)} %bitcast.74, bf16[1024,1024]{1,0:T(8,128)(2,1)} %copy-done, pred[1024]{0:T(1024)(128)(4,1)S(1)} %get-tuple-element.57, pred[1024]{0:T(1024)(128)(4,1)S(1)} %get-tuple-element.54, pred[1024]{0:T(1024)(128)(4,1)S(1)} %get-tuple-element.56, ...), kind=kOutput, calls=%fused_computation.10 | convolution fusion | flops 546308096 | bytes 7868416 | tf_op jit(solution)/shard_map/dot_general | solution.py:562
  104.6 1.2 gather_fusion.1
  105.7 0.1 broadcast_select_fusion
  105.9 1.1 pad_maximum_fusion.1.t_ref
  107.0 44.2 %shard_map.48 = bf16[4,8,16,1024]{3,2,1,0:T(8,128)(2,1)} custom-call(bf16[4,2,64,1024]{3,2,1,0:T(8,128)(2,1)} %pad_maximum_fusion.1.t_ref), custom_call_target="tpu_custom_call" | custom-call | tf_op jit(solution)/shard_map/pallas_call | solution.py:375
  151.1 1.3 fusion.50
  152.4 0.0 copy-start.3
  152.5 3.0 %scatter_fusion.1 = bf16[1024,1024]{1,0:T(8,128)(2,1)S(1)} fusion(bf16[1024,1024]{1,0:T(8,128)(2,1)S(1)} %and_select_fusion.4, s32[256]{0:T(256)S(1)} %bitcast.99, bf16[256,1024]{1,0:T(8,128)(2,1)S(1)} %bitcast.93), kind=kCustom, calls=%fused_computation.3 | custom fusion | bytes 1573888 | tf_op jit(solution)/shard_map/scatter | solution.py:543
  155.5 0.0 copy-done.3
  155.5 0.2 fusion.3
  155.7 2.0 %fusion.1 = bf16[1024,256]{1,0:T(8,128)(2,1)} fusion(bf16[1024,1024]{1,0:T(8,128)(2,1)S(1)} %fusion.3, pred[]{:T(512)S(6)} %eq.100, bf16[2,256,256]{2,1,0:T(8,128)(2,1)} %param.11), kind=kOutput, calls=%fused_computation.17 | convolution fusion | flops 134742016 | bytes 1179649 | tf_op jit(solution)/shard_map/dot_general | solution.py:551
  157.7 22.3 %shard_map.49 = bf16[8,128,256]{2,1,0:T(8,128)(2,1)} custom-call(bf16[8,128,256]{2,1,0:T(8,128)(2,1)} %bitcast.97), custom_call_target="tpu_custom_call" | custom-call | tf_op jit(solution)/shard_map/pallas_call | solution.py:496
  180.0 1.6 broadcast_in_dim.82
  181.6 0.0 copy-start.4
  181.6 1.8 copy.11
  183.5 0.0 copy-start.2
  183.5 0.0 copy-done.4
  183.5 0.4 convolution_convert_fusion
  183.8 1.0 copy.8
  184.8 0.0 copy-done.2
  184.9 4.8 %and_select_fusion.5 = bf16[1024,1024]{1,0:T(8,128)(2,1)} fusion(bf16[1024,1024]{1,0:T(8,128)(2,1)} %bitcast.75, bf16[1024,1024]{1,0:T(8,128)(2,1)S(1)} %fusion.3, pred[1024]{0:T(1024)(128)(4,1)S(1)} %get-tuple-element.59, pred[1024]{0:T(1024)(128)(4,1)S(1)} %get-tuple-element.55, pred[1024]{0:T(1024)(128)(4,1)S(1)} %get-tuple-element.58, ...), kind=kOutput, calls=%fused_computation.11 | convolution fusion | flops 546308096 | bytes 7868416 | tf_op jit(solution)/shard_map/dot_general | solution.py:562
  189.6 4.5 %reshape.656 = bf16[4,256,4,256]{3,2,1,0:T(4,128)(2,1)} reshape(bf16[1024,1024]{1,0:T(8,128)(2,1)} %and_select_fusion.5) | data formatting | bytes 4194304 | tf_op jit(solution)/shard_map/reshape | solution.py:583
  (12 shorter events, 0.2 us)
Async XLA Ops:
  2.9 1.2 copy-start.8
  55.9 2.9 %copy-start.5 = (bf16[4,1,64,1024]{3,2,1,0:T(8,128)(2,1)}, bf16[4,1,64,1024]{3,2,1,0:T(8,128)(2,1)S(1)}, u32[]{:S(2)}) copy-start(bf16[4,1,64,1024]{3,2,1,0:T(8,128)(2,1)S(1)} %get-tuple-element.43) | copy-start | bytes 1572868
  55.9 3.1 %copy-start.9 = (bf16[2,256,256]{2,1,0:T(8,128)(2,1)S(1)}, bf16[2,256,256]{2,1,0:T(8,128)(2,1)}, u32[]{:S(2)}) copy-start(bf16[2,256,256]{2,1,0:T(8,128)(2,1)} %param.11) | copy-start | bytes 786436
  59.0 37.0 %copy-start = (bf16[1024,1024]{1,0:T(8,128)(2,1)}, bf16[1024,1024]{1,0:T(8,128)(2,1)S(1)}, u32[]{:S(2)}) copy-start(bf16[1024,1024]{1,0:T(8,128)(2,1)S(1)} %fusion.5) | copy-start | bytes 6291460
  96.0 1.8 copy-start.6
  96.0 1.8 copy-start.7
  97.9 1.4 copy-start.1
  152.4 3.1 %copy-start.3 = (bf16[4,1,64,1024]{3,2,1,0:T(8,128)(2,1)}, bf16[4,1,64,1024]{3,2,1,0:T(8,128)(2,1)S(1)}, u32[]{:S(2)}) copy-start(bf16[4,1,64,1024]{3,2,1,0:T(8,128)(2,1)S(1)} %get-tuple-element.41) | copy-start | bytes 1572868
  181.6 1.8 copy-start.4
  183.5 1.4 copy-start.2

commit v9 on v8

--- a/solution.py
+++ b/solution.py
@@ -356,9 +356,57 @@
     def _():
         a2[yd // 2 :] = jnp.zeros(top_half, a2.dtype)
 
-    exchange(1, lambda k, s: a2.at[k], lambda s: b2.at[s], yi, yd, ydev)
-    b2[yi] = a2[yi]
-    b3[yi] = total(lambda s: b2[s], yd).astype(b3.dtype)
+    def ycopy(k, s):
+        return pltpu.make_async_remote_copy(
+            src_ref=a2.at[k],
+            dst_ref=b2.at[s],
+            send_sem=sends.at[1, k],
+            recv_sem=recvs.at[1, s],
+            device_id=ydev(k),
+            device_id_type=MESH,
+        )
+
+    def ystart(i, c):
+        k = lax.rem(yi + i, yd)
+
+        @pl.when((k < yd // 2) | (yi == yt))
+        def _():
+            ycopy(k, yi).start()
+
+        return c
+
+    lax.fori_loop(1, yd, ystart, 0)
+
+    @pl.when(yi < yd // 2)
+    def _():
+        def wait(i, c):
+            s = lax.rem(yi + yd - i, yd)
+            ycopy(s, s).wait_recv()
+            return c
+
+        lax.fori_loop(1, yd, wait, 0)
+        b2[yi] = a2[yi]
+        b3[yi] = total(lambda s: b2[s], yd).astype(b3.dtype)
+
+    @pl.when((yi >= yd // 2) & (yi != yt))
+    def _():
+        ycopy(yt, yt).wait_recv()
+        b3[yi] = b2[yt]
+
+    @pl.when((yi >= yd // 2) & (yi == yt))
+    def _():
+        b3[yi] = a2[yi]
+
+    def ysent(i, c):
+        k = lax.rem(yi + i, yd)
+
+        @pl.when((k < yd // 2) | (yi == yt))
+        def _():
+            ycopy(k, yi).wait_send()
+
+        return c
+
+    lax.fori_loop(1, yd, ysent, 0)
     exchange(2, lambda k, s: b3.at[s], lambda s: b3.at[s], yi, yd, ydev)
     b4[xi] = b3[...].reshape(b4.shape[1:])
     exchange(3, lambda k, s: b4.at[s], lambda s: b4.at[s], xi, xd, xdev)

time: 195 us -> 196 us (level)
  no operation moved by 1% of the time
where the time goes in v9:
time: 196 us; the launch traced here: 195 us
  Pallas kernels  147 us (75%)
  local copies, waits for them, and re-layouts  26.8 us (14%)
  matrix products  14.1 us (7%)
  other arithmetic  6.8 us (3%)
    pallas_call x2, Pallas kernels, prow_sum(): pl.pallas_call(functools.partial(prow_kernel, xd, yd, top), out_shape=jax...  90.6 us
    pallas_call x2, Pallas kernels, pcol_bcast(): pl.pallas_call(functools.partial(pcol_kernel, nz, source), out_shape=jax....  56.3 us
    dot_general x2, matrix products, local(): product = jnp.dot(lower, upper, preferred_element_type=jnp.float32)  10 us
    scatter x2, local copies, waits for them, and re-layouts, local(): current = current.at[target].set(old_top, mode='drop')  5.86 us
    unnamed x23, local copies, waits for them, and re-layouts  5.76 us
    reshape x1, local copies, waits for them, and re-layouts, local(): return current.reshape(matrix.shape)  4.49 us

profile of v9, /device:TPU:1, one launch (start us, length us, event | category | flops | bytes accessed | tf_op | source)
XLA Modules:
  0.0 195.0 jit_solution(2972463873261490409)
XLA Ops:
  0.0 0.8 and_select_fusion.9
  0.8 2.1 %copy.9 = bf16[128,8,4,256]{3,1,2,0:T(8,128)(2,1)S(1)} copy(bf16[128,8,4,256]{3,2,1,0:T(4,128)(2,1)} %bitcast.90) | data formatting | bytes 4194304
  2.9 0.0 copy-start.8
  2.9 1.2 gather_fusion
  4.1 0.0 copy-done.8
  4.1 0.1 squeeze.23
  4.2 0.1 squeeze.27
  4.3 0.9 broadcast_select_fusion.1
  5.2 1.3 slice_select_fusion.3
  6.5 0.4 select_n.397
  6.9 2.1 %pad_maximum_fusion.t_ref = bf16[4,2,64,1024]{3,2,1,0:T(8,128)(2,1)} fusion(bf16[4,1,64,1024]{3,2,1,0:T(8,128)(2,1)S(1)} %select_n.397, bf16[4,1,64,1024]{3,2,1,0:T(8,128)(2,1)} %broadcast_select_fusion.1), kind=kLoop, calls=%fused_computation.18 | loop fusion | flops 524288 | bytes 2097152 | tf_op jit(solution)/shard_map/stack | solution.py:419
  9.0 46.1 %shard_map.46 = bf16[4,8,16,1024]{3,2,1,0:T(8,128)(2,1)} custom-call(bf16[4,2,64,1024]{3,2,1,0:T(8,128)(2,1)} %pad_maximum_fusion.t_ref), custom_call_target="tpu_custom_call" | custom-call | tf_op jit(solution)/shard_map/pallas_call | solution.py:423
  55.1 1.3 fusion.51
  56.4 0.0 copy-start.5
  56.4 0.0 copy-start.9
  56.5 2.8 %scatter_fusion = bf16[1024,1024]{1,0:T(8,128)(2,1)S(1)} fusion(bf16[1024,1024]{1,0:T(8,128)(2,1)S(1)} %bitcast.73, s32[256]{0:T(256)S(1)} %bitcast.98, bf16[256,1024]{1,0:T(8,128)(2,1)S(1)} %bitcast.94), kind=kCustom, calls=%fused_computation.2 | custom fusion | bytes 1573888 | tf_op jit(solution)/shard_map/scatter | solution.py:591
  59.3 0.0 copy-done.5
  59.3 0.2 fusion.5
  59.5 0.0 copy-start
  59.6 0.0 copy-done.9
  59.6 1.4 fusion
  61.0 34.8 %shard_map.47 = bf16[8,128,256]{2,1,0:T(8,128)(2,1)} custom-call(bf16[8,128,256]{2,1,0:T(8,128)(2,1)} %bitcast.96), custom_call_target="tpu_custom_call" | custom-call | tf_op jit(solution)/shard_map/pallas_call | solution.py:544
  95.8 1.6 broadcast_in_dim.78
  97.4 0.0 copy-done
  97.4 0.0 copy-start.6
  97.4 0.0 copy-start.7
  97.4 1.8 copy.10
  99.2 0.0 copy-start.1
  99.2 0.0 copy-done.6
  99.2 0.0 copy-done.7
  99.2 0.4 convolution_convert_fusion.2
  99.6 1.0 copy.7
  100.6 0.0 copy-done.1
  100.7 5.2 %and_select_fusion.4 = bf16[1024,1024]{1,0:T(8,128)(2,1)S(1)} fusion(bf16[1024,1024]{1,0:T(8,128)(2,1)} %bitcast.74, bf16[1024,1024]{1,0:T(8,128)(2,1)} %copy-done, pred[1024]{0:T(1024)(128)(4,1)S(1)} %get-tuple-element.57, pred[1024]{0:T(1024)(128)(4,1)S(1)} %get-tuple-element.54, pred[1024]{0:T(1024)(128)(4,1)S(1)} %get-tuple-element.56, ...), kind=kOutput, calls=%fused_computation.10 | convolution fusion | flops 546308096 | bytes 7868416 | tf_op jit(solution)/shard_map/dot_general | solution.py:610
  105.9 1.2 gather_fusion.1
  107.1 0.1 broadcast_select_fusion
  107.3 1.1 pad_maximum_fusion.1.t_ref
  108.3 44.5 %shard_map.48 = bf16[4,8,16,1024]{3,2,1,0:T(8,128)(2,1)} custom-call(bf16[4,2,64,1024]{3,2,1,0:T(8,128)(2,1)} %pad_maximum_fusion.1.t_ref), custom_call_target="tpu_custom_call" | custom-call | tf_op jit(solution)/shard_map/pallas_call | solution.py:423
  152.8 1.3 fusion.50
  154.1 0.0 copy-start.3
  154.1 3.0 %scatter_fusion.1 = bf16[1024,1024]{1,0:T(8,128)(2,1)S(1)} fusion(bf16[1024,1024]{1,0:T(8,128)(2,1)S(1)} %and_select_fusion.4, s32[256]{0:T(256)S(1)} %bitcast.99, bf16[256,1024]{1,0:T(8,128)(2,1)S(1)} %bitcast.93), kind=kCustom, calls=%fused_computation.3 | custom fusion | bytes 1573888 | tf_op jit(solution)/shard_map/scatter | solution.py:591
  157.2 0.0 copy-done.3
  157.2 0.2 fusion.3
  157.4 2.0 %fusion.1 = bf16[1024,256]{1,0:T(8,128)(2,1)} fusion(bf16[1024,1024]{1,0:T(8,128)(2,1)S(1)} %fusion.3, pred[]{:T(512)S(6)} %eq.100, bf16[2,256,256]{2,1,0:T(8,128)(2,1)} %param.11), kind=kOutput, calls=%fused_computation.17 | convolution fusion | flops 134742016 | bytes 1179649 | tf_op jit(solution)/shard_map/dot_general | solution.py:599
  159.4 21.5 %shard_map.49 = bf16[8,128,256]{2,1,0:T(8,128)(2,1)} custom-call(bf16[8,128,256]{2,1,0:T(8,128)(2,1)} %bitcast.97), custom_call_target="tpu_custom_call" | custom-call | tf_op jit(solution)/shard_map/pallas_call | solution.py:544
  180.9 1.6 broadcast_in_dim.82
  182.5 0.0 copy-start.4
  182.5 1.8 copy.11
  184.3 0.0 copy-start.2
  184.3 0.0 copy-done.4
  184.3 0.4 convolution_convert_fusion
  184.7 1.0 copy.8
  185.7 0.0 copy-done.2
  185.7 4.8 %and_select_fusion.5 = bf16[1024,1024]{1,0:T(8,128)(2,1)} fusion(bf16[1024,1024]{1,0:T(8,128)(2,1)} %bitcast.75, bf16[1024,1024]{1,0:T(8,128)(2,1)S(1)} %fusion.3, pred[1024]{0:T(1024)(128)(4,1)S(1)} %get-tuple-element.59, pred[1024]{0:T(1024)(128)(4,1)S(1)} %get-tuple-element.55, pred[1024]{0:T(1024)(128)(4,1)S(1)} %get-tuple-element.58, ...), kind=kOutput, calls=%fused_computation.11 | convolution fusion | flops 546308096 | bytes 7868416 | tf_op jit(solution)/shard_map/dot_general | solution.py:610
  190.5 4.5 %reshape.656 = bf16[4,256,4,256]{3,2,1,0:T(4,128)(2,1)} reshape(bf16[1024,1024]{1,0:T(8,128)(2,1)} %and_select_fusion.5) | data formatting | bytes 4194304 | tf_op jit(solution)/shard_map/reshape | solution.py:631
  (12 shorter events, 0.2 us)
Async XLA Ops:
  2.9 1.2 copy-start.8
  56.4 2.9 %copy-start.5 = (bf16[4,1,64,1024]{3,2,1,0:T(8,128)(2,1)}, bf16[4,1,64,1024]{3,2,1,0:T(8,128)(2,1)S(1)}, u32[]{:S(2)}) copy-start(bf16[4,1,64,1024]{3,2,1,0:T(8,128)(2,1)S(1)} %get-tuple-element.43) | copy-start | bytes 1572868
  56.4 3.1 %copy-start.9 = (bf16[2,256,256]{2,1,0:T(8,128)(2,1)S(1)}, bf16[2,256,256]{2,1,0:T(8,128)(2,1)}, u32[]{:S(2)}) copy-start(bf16[2,256,256]{2,1,0:T(8,128)(2,1)} %param.11) | copy-start | bytes 786436
  59.5 37.8 %copy-start = (bf16[1024,1024]{1,0:T(8,128)(2,1)}, bf16[1024,1024]{1,0:T(8,128)(2,1)S(1)}, u32[]{:S(2)}) copy-start(bf16[1024,1024]{1,0:T(8,128)(2,1)S(1)} %fusion.5) | copy-start | bytes 6291460
  97.4 1.8 copy-start.6
  97.4 1.8 copy-start.7
  99.2 1.4 copy-start.1
  154.1 3.1 %copy-start.3 = (bf16[4,1,64,1024]{3,2,1,0:T(8,128)(2,1)}, bf16[4,1,64,1024]{3,2,1,0:T(8,128)(2,1)S(1)}, u32[]{:S(2)}) copy-start(bf16[4,1,64,1024]{3,2,1,0:T(8,128)(2,1)S(1)} %get-tuple-element.41) | copy-start | bytes 1572868
  182.5 1.8 copy-start.4
  184.3 1.4 copy-start.2

commit v10 on v9

--- a/solution.py
+++ b/solution.py
@@ -256,7 +256,7 @@
     return out
 
 
-def prow_kernel(xd, yd, top, t_ref, o_ref, b1, a2, b2, b3, b4, sends, recvs, tsend, trecv):
+def prow_kernel(xd, yd, top, t_ref, o_ref, b1, a2, b2, b3, b4, sends, recvs, tsend, trecv, rsend, trecv2):
     p = lax.axis_index("prow")
     q = lax.axis_index("pcol")
     xi = lax.rem(p, xd)
@@ -409,7 +409,45 @@
     lax.fori_loop(1, yd, ysent, 0)
     exchange(2, lambda k, s: b3.at[s], lambda s: b3.at[s], yi, yd, ydev)
     b4[xi] = b3[...].reshape(b4.shape[1:])
-    exchange(3, lambda k, s: b4.at[s], lambda s: b4.at[s], xi, xd, xdev)
+    if xd == 4:
+        left, right = lax.rem(xi + 3, 4), lax.rem(xi + 1, 4)
+        h = yd // 2
+
+        def near(k, s):
+            return pltpu.make_async_remote_copy(
+                src_ref=b4.at[s],
+                dst_ref=b4.at[s],
+                send_sem=sends.at[3, k],
+                recv_sem=recvs.at[3, s],
+                device_id=xdev(k),
+                device_id_type=MESH,
+            )
+
+        def relay(k, s, lo, slot):
+            return pltpu.make_async_remote_copy(
+                src_ref=b4.at[s, pl.ds(lo, h)],
+                dst_ref=b4.at[s, pl.ds(lo, h)],
+                send_sem=rsend.at[slot],
+                recv_sem=trecv2.at[slot],
+                device_id=xdev(k),
+                device_id_type=MESH,
+            )
+
+        near(right, xi).start()
+        near(left, xi).start()
+        near(left, left).wait_recv()
+        relay(right, left, h, 1).start()
+        near(right, right).wait_recv()
+        relay(left, right, 0, 0).start()
+        far = lax.rem(xi + 2, 4)
+        relay(left, far, h, 1).wait_recv()
+        relay(right, far, 0, 0).wait_recv()
+        near(right, xi).wait_send()
+        near(left, xi).wait_send()
+        relay(right, left, h, 1).wait_send()
+        relay(left, right, 0, 0).wait_send()
+    else:
+        exchange(3, lambda k, s: b4.at[s], lambda s: b4.at[s], xi, xd, xdev)
     o_ref[...] = b4[...]
 
 
@@ -435,6 +473,8 @@
             pltpu.SemaphoreType.DMA((4, max(xd, yd))),
             pltpu.SemaphoreType.DMA((xd,)),
             pltpu.SemaphoreType.DMA((1,)),
+            pltpu.SemaphoreType.DMA((2,)),
+            pltpu.SemaphoreType.DMA((2,)),
         ],
         compiler_params=pltpu.CompilerParams(collective_id=10 + top, has_side_effects=True),
     )(chunks)

time: 196 us -> 196 us (level)
    pallas_call x2, Pallas kernels: 56.3 us -> 60.1 us  [pcol_bcast(): pl.pallas_call(functools.partial(pcol_kernel, nz, source), out_shape=jax....]
    pallas_call x2, Pallas kernels: 90.6 us -> 87 us  [prow_sum(): pl.pallas_call(functools.partial(prow_kernel, xd, yd, top), out_shape=jax...]
where the time goes in v10:
time: 196 us; the launch traced here: 195 us
  Pallas kernels  147 us (75%)
  local copies, waits for them, and re-layouts  26.8 us (14%)
  matrix products  14.1 us (7%)
  other arithmetic  6.8 us (3%)
    pallas_call x2, Pallas kernels, prow_sum(): pl.pallas_call(functools.partial(prow_kernel, xd, yd, top), out_shape=jax...  87 us
    pallas_call x2, Pallas kernels, pcol_bcast(): pl.pallas_call(functools.partial(pcol_kernel, nz, source), out_shape=jax....  60.1 us
    dot_general x2, matrix products, local(): product = jnp.dot(lower, upper, preferred_element_type=jnp.float32)  10 us
    scatter x2, local copies, waits for them, and re-layouts, local(): current = current.at[target].set(old_top, mode='drop')  5.86 us
    unnamed x23, local copies, waits for them, and re-layouts  5.76 us
    reshape x1, local copies, waits for them, and re-layouts, local(): return current.reshape(matrix.shape)  4.49 us

profile of v10, /device:TPU:1, one launch (start us, length us, event | category | flops | bytes accessed | tf_op | source)
XLA Modules:
  0.0 195.2 jit_solution(12586231124421203158)
XLA Ops:
  0.0 0.8 and_select_fusion.9
  0.8 2.1 %copy.9 = bf16[128,8,4,256]{3,1,2,0:T(8,128)(2,1)S(1)} copy(bf16[128,8,4,256]{3,2,1,0:T(4,128)(2,1)} %bitcast.90) | data formatting | bytes 4194304
  2.9 0.0 copy-start.8
  2.9 1.2 gather_fusion
  4.1 0.0 copy-done.8
  4.1 0.1 squeeze.23
  4.2 0.1 squeeze.27
  4.3 0.9 broadcast_select_fusion.1
  5.2 1.3 slice_select_fusion.3
  6.5 0.4 select_n.397
  6.9 2.1 %pad_maximum_fusion.t_ref = bf16[4,2,64,1024]{3,2,1,0:T(8,128)(2,1)} fusion(bf16[4,1,64,1024]{3,2,1,0:T(8,128)(2,1)S(1)} %select_n.397, bf16[4,1,64,1024]{3,2,1,0:T(8,128)(2,1)} %broadcast_select_fusion.1), kind=kLoop, calls=%fused_computation.18 | loop fusion | flops 524288 | bytes 2097152 | tf_op jit(solution)/shard_map/stack | solution.py:457
  9.0 44.9 %shard_map.46 = bf16[4,8,16,1024]{3,2,1,0:T(8,128)(2,1)} custom-call(bf16[4,2,64,1024]{3,2,1,0:T(8,128)(2,1)} %pad_maximum_fusion.t_ref), custom_call_target="tpu_custom_call" | custom-call | tf_op jit(solution)/shard_map/pallas_call | solution.py:461
  53.8 1.3 fusion.51
  55.2 0.0 copy-start.5
  55.2 0.0 copy-start.9
  55.2 2.8 %scatter_fusion = bf16[1024,1024]{1,0:T(8,128)(2,1)S(1)} fusion(bf16[1024,1024]{1,0:T(8,128)(2,1)S(1)} %bitcast.73, s32[256]{0:T(256)S(1)} %bitcast.98, bf16[256,1024]{1,0:T(8,128)(2,1)S(1)} %bitcast.94), kind=kCustom, calls=%fused_computation.2 | custom fusion | bytes 1573888 | tf_op jit(solution)/shard_map/scatter | solution.py:631
  58.0 0.0 copy-done.5
  58.0 0.2 fusion.5
  58.3 0.0 copy-start
  58.3 0.0 copy-done.9
  58.3 1.4 fusion
  59.7 35.4 %shard_map.47 = bf16[8,128,256]{2,1,0:T(8,128)(2,1)} custom-call(bf16[8,128,256]{2,1,0:T(8,128)(2,1)} %bitcast.96), custom_call_target="tpu_custom_call" | custom-call | tf_op jit(solution)/shard_map/pallas_call | solution.py:584
  95.1 1.6 broadcast_in_dim.78
  96.7 0.0 copy-done
  96.7 0.0 copy-start.6
  96.7 0.0 copy-start.7
  96.8 1.8 copy.10
  98.6 0.0 copy-start.1
  98.6 0.0 copy-done.6
  98.6 0.0 copy-done.7
  98.6 0.4 convolution_convert_fusion.2
  99.0 1.0 copy.7
  100.0 0.0 copy-done.1
  100.0 5.2 %and_select_fusion.4 = bf16[1024,1024]{1,0:T(8,128)(2,1)S(1)} fusion(bf16[1024,1024]{1,0:T(8,128)(2,1)} %bitcast.74, bf16[1024,1024]{1,0:T(8,128)(2,1)} %copy-done, pred[1024]{0:T(1024)(128)(4,1)S(1)} %get-tuple-element.57, pred[1024]{0:T(1024)(128)(4,1)S(1)} %get-tuple-element.54, pred[1024]{0:T(1024)(128)(4,1)S(1)} %get-tuple-element.56, ...), kind=kOutput, calls=%fused_computation.10 | convolution fusion | flops 546308096 | bytes 7868416 | tf_op jit(solution)/shard_map/dot_general | solution.py:650
  105.3 1.2 gather_fusion.1
  106.4 0.1 broadcast_select_fusion
  106.6 1.1 pad_maximum_fusion.1.t_ref
  107.7 42.1 %shard_map.48 = bf16[4,8,16,1024]{3,2,1,0:T(8,128)(2,1)} custom-call(bf16[4,2,64,1024]{3,2,1,0:T(8,128)(2,1)} %pad_maximum_fusion.1.t_ref), custom_call_target="tpu_custom_call" | custom-call | tf_op jit(solution)/shard_map/pallas_call | solution.py:461
  149.8 1.3 fusion.50
  151.1 0.0 copy-start.3
  151.1 3.0 %scatter_fusion.1 = bf16[1024,1024]{1,0:T(8,128)(2,1)S(1)} fusion(bf16[1024,1024]{1,0:T(8,128)(2,1)S(1)} %and_select_fusion.4, s32[256]{0:T(256)S(1)} %bitcast.99, bf16[256,1024]{1,0:T(8,128)(2,1)S(1)} %bitcast.93), kind=kCustom, calls=%fused_computation.3 | custom fusion | bytes 1573888 | tf_op jit(solution)/shard_map/scatter | solution.py:631
  154.2 0.0 copy-done.3
  154.2 0.2 fusion.3
  154.4 2.0 %fusion.1 = bf16[1024,256]{1,0:T(8,128)(2,1)} fusion(bf16[1024,1024]{1,0:T(8,128)(2,1)S(1)} %fusion.3, pred[]{:T(512)S(6)} %eq.100, bf16[2,256,256]{2,1,0:T(8,128)(2,1)} %param.11), kind=kOutput, calls=%fused_computation.17 | convolution fusion | flops 134742016 | bytes 1179649 | tf_op jit(solution)/shard_map/dot_general | solution.py:639
  156.4 24.7 %shard_map.49 = bf16[8,128,256]{2,1,0:T(8,128)(2,1)} custom-call(bf16[8,128,256]{2,1,0:T(8,128)(2,1)} %bitcast.97), custom_call_target="tpu_custom_call" | custom-call | tf_op jit(solution)/shard_map/pallas_call | solution.py:584
  181.1 1.6 broadcast_in_dim.82
  182.7 0.0 copy-start.4
  182.7 1.8 copy.11
  184.5 0.0 copy-start.2
  184.5 0.0 copy-done.4
  184.5 0.4 convolution_convert_fusion
  184.9 1.0 copy.8
  185.9 0.0 copy-done.2
  185.9 4.8 %and_select_fusion.5 = bf16[1024,1024]{1,0:T(8,128)(2,1)} fusion(bf16[1024,1024]{1,0:T(8,128)(2,1)} %bitcast.75, bf16[1024,1024]{1,0:T(8,128)(2,1)S(1)} %fusion.3, pred[1024]{0:T(1024)(128)(4,1)S(1)} %get-tuple-element.59, pred[1024]{0:T(1024)(128)(4,1)S(1)} %get-tuple-element.55, pred[1024]{0:T(1024)(128)(4,1)S(1)} %get-tuple-element.58, ...), kind=kOutput, calls=%fused_computation.11 | convolution fusion | flops 546308096 | bytes 7868416 | tf_op jit(solution)/shard_map/dot_general | solution.py:650
  190.7 4.5 %reshape.656 = bf16[4,256,4,256]{3,2,1,0:T(4,128)(2,1)} reshape(bf16[1024,1024]{1,0:T(8,128)(2,1)} %and_select_fusion.5) | data formatting | bytes 4194304 | tf_op jit(solution)/shard_map/reshape | solution.py:671
  (12 shorter events, 0.2 us)
Async XLA Ops:
  2.9 1.2 copy-start.8
  55.2 2.9 %copy-start.5 = (bf16[4,1,64,1024]{3,2,1,0:T(8,128)(2,1)}, bf16[4,1,64,1024]{3,2,1,0:T(8,128)(2,1)S(1)}, u32[]{:S(2)}) copy-start(bf16[4,1,64,1024]{3,2,1,0:T(8,128)(2,1)S(1)} %get-tuple-element.43) | copy-start | bytes 1572868
  55.2 3.1 %copy-start.9 = (bf16[2,256,256]{2,1,0:T(8,128)(2,1)S(1)}, bf16[2,256,256]{2,1,0:T(8,128)(2,1)}, u32[]{:S(2)}) copy-start(bf16[2,256,256]{2,1,0:T(8,128)(2,1)} %param.11) | copy-start | bytes 786436
  58.3 38.5 %copy-start = (bf16[1024,1024]{1,0:T(8,128)(2,1)}, bf16[1024,1024]{1,0:T(8,128)(2,1)S(1)}, u32[]{:S(2)}) copy-start(bf16[1024,1024]{1,0:T(8,128)(2,1)S(1)} %fusion.5) | copy-start | bytes 6291460
  96.7 1.8 copy-start.6
  96.7 1.8 copy-start.7
  98.6 1.4 copy-start.1
  151.1 3.1 %copy-start.3 = (bf16[4,1,64,1024]{3,2,1,0:T(8,128)(2,1)}, bf16[4,1,64,1024]{3,2,1,0:T(8,128)(2,1)S(1)}, u32[]{:S(2)}) copy-start(bf16[4,1,64,1024]{3,2,1,0:T(8,128)(2,1)S(1)} %get-tuple-element.41) | copy-start | bytes 1572868
  182.7 1.8 copy-start.4
  184.5 1.4 copy-start.2

commit v11 on v8

--- a/solution.py
+++ b/solution.py
@@ -416,83 +416,80 @@
     lax.fori_loop(1, n, greet, 0)
     pl.semaphore_wait(barrier, n - 1)
 
-    def spread(j):
-        return pltpu.make_async_remote_copy(
-            src_ref=x_ref.at[j],
-            dst_ref=g.at[j],
-            send_sem=p1send.at[j],
+    def spread(t):
+        zz, cc = t // nc, lax.rem(t, nc)
+        return pltpu.make_async_remote_copy(
+            src_ref=x_ref.at[cc, zz],
+            dst_ref=g.at[cc, zz],
+            send_sem=p1send.at[t],
             recv_sem=p1recv.at[0],
-            device_id=dev(j, cs),
+            device_id=dev(zz, cc),
             device_id_type=MESH,
         )
 
     def ring(j, s):
         return pltpu.make_async_remote_copy(
-            src_ref=g.at[s],
-            dst_ref=g.at[s],
+            src_ref=g.at[c, s],
+            dst_ref=g.at[c, s],
             send_sem=p2send.at[j],
             recv_sem=p2recv.at[s],
-            device_id=dev(j, cs),
-            device_id_type=MESH,
-        )
-
-    def partner(zz):
-        return pltpu.make_async_remote_copy(
-            src_ref=g,
-            dst_ref=g,
+            device_id=dev(j, c),
+            device_id_type=MESH,
+        )
+
+    def partner(cc, other):
+        return pltpu.make_async_remote_copy(
+            src_ref=g.at[cc],
+            dst_ref=g.at[cc],
             send_sem=p3send.at[0],
             recv_sem=p3recv.at[0],
-            device_id=dev(zz, 1 - cs),
+            device_id=dev(z, other),
             device_id_type=MESH,
         )
 
     @pl.when(q == source)
     def _():
         def start(i, carry):
-            spread(lax.rem(zs + i, nz)).start()
+            spread(lax.rem(q + i, n)).start()
             return carry
 
-        lax.fori_loop(1, nz, start, 0)
-        g[zs] = x_ref[zs]
+        lax.fori_loop(1, n, start, 0)
+        g[cs, zs] = x_ref[cs, zs]
 
         def sent(i, carry):
-            spread(lax.rem(zs + i, nz)).wait_send()
+            spread(lax.rem(q + i, n)).wait_send()
             return carry
 
-        lax.fori_loop(1, nz, sent, 0)
-
-    @pl.when((c == cs) & (z != zs))
+        lax.fori_loop(1, n, sent, 0)
+
+    @pl.when(q != source)
     def _():
-        spread(z).wait_recv()
-
-    @pl.when(c == cs)
-    def _():
-        def start(i, carry):
-            ring(lax.rem(z + i, nz), z).start()
-            return carry
-
-        lax.fori_loop(1, nz, start, 0)
-
-        def wait(i, carry):
-            s = lax.rem(z + nz - i, nz)
-            ring(s, s).wait_recv()
-            ring(lax.rem(z + i, nz), z).wait_send()
-            return carry
-
-        lax.fori_loop(1, nz, wait, 0)
-        partner(z).start()
-        partner(z).wait_send()
-
-    @pl.when(c != cs)
-    def _():
-        partner(z).wait_recv()
-
+        spread(q).wait_recv()
+
+    def start(i, carry):
+        ring(lax.rem(z + i, nz), z).start()
+        return carry
+
+    lax.fori_loop(1, nz, start, 0)
+
+    def wait(i, carry):
+        s = lax.rem(z + nz - i, nz)
+        ring(s, s).wait_recv()
+        ring(lax.rem(z + i, nz), z).wait_send()
+        return carry
+
+    lax.fori_loop(1, nz, wait, 0)
+    partner(c, 1 - c).start()
+    partner(1 - c, 1 - c).wait_recv()
+    partner(c, 1 - c).wait_send()
     o_ref[...] = g[...]
 
 
 def pcol_bcast(x, nz, source, collective_id):
     rows, cols = x.shape
-    chunks = x.reshape(nz, rows // nz, cols)
+    nc = lax.axis_size("pcol") // nz
+    chunks = x.reshape(nc, nz, rows // nz // nc, cols)
+    n = nz * nc
     out = pl.pallas_call(
         functools.partial(pcol_kernel, nz, source),
         out_shape=jax.ShapeDtypeStruct(chunks.shape, x.dtype),
@@ -500,7 +497,7 @@
         out_specs=pl.BlockSpec(memory_space=pltpu.VMEM),
         scratch_shapes=[
             pltpu.VMEM(chunks.shape, x.dtype),
-            pltpu.SemaphoreType.DMA((nz,)),
+            pltpu.SemaphoreType.DMA((n,)),
             pltpu.SemaphoreType.DMA((1,)),
             pltpu.SemaphoreType.DMA((nz,)),
             pltpu.SemaphoreType.DMA((nz,)),

time: 195 us -> 197 us (1.010)
  Pallas kernels: 146 us -> 148 us
where the time goes in v11:
time: 197 us; the launch traced here: 196 us
  Pallas kernels  148 us (75%)
  local copies, waits for them, and re-layouts  26.8 us (14%)
  matrix products  14.1 us (7%)
  other arithmetic  6.8 us (3%)
    pallas_call x2, Pallas kernels, prow_sum(): pl.pallas_call(functools.partial(prow_kernel, xd, yd, top), out_shape=jax...  89.8 us
    pallas_call x2, Pallas kernels, pcol_bcast(): pl.pallas_call(functools.partial(pcol_kernel, nz, source), out_shape=jax....  58.2 us
    dot_general x2, matrix products, local(): product = jnp.dot(lower, upper, preferred_element_type=jnp.float32)  10 us
    scatter x2, local copies, waits for them, and re-layouts, local(): current = current.at[target].set(old_top, mode='drop')  5.86 us
    unnamed x23, local copies, waits for them, and re-layouts  5.76 us
    reshape x1, local copies, waits for them, and re-layouts, local(): return current.reshape(matrix.shape)  4.49 us

profile of v11, /device:TPU:1, one launch (start us, length us, event | category | flops | bytes accessed | tf_op | source)
XLA Modules:
  0.0 196.1 jit_solution(2018774583480504779)
XLA Ops:
  0.0 0.8 and_select_fusion.9
  0.8 2.1 %copy.9 = bf16[128,8,4,256]{3,1,2,0:T(8,128)(2,1)S(1)} copy(bf16[128,8,4,256]{3,2,1,0:T(4,128)(2,1)} %bitcast.90) | data formatting | bytes 4194304
  2.9 0.0 copy-start.8
  2.9 1.2 gather_fusion
  4.1 0.0 copy-done.8
  4.1 0.1 squeeze.23
  4.2 0.1 squeeze.27
  4.3 0.9 broadcast_select_fusion.1
  5.2 1.3 slice_select_fusion.3
  6.5 0.4 select_n.397
  6.9 2.1 %pad_maximum_fusion.t_ref = bf16[4,2,64,1024]{3,2,1,0:T(8,128)(2,1)} fusion(bf16[4,1,64,1024]{3,2,1,0:T(8,128)(2,1)S(1)} %select_n.397, bf16[4,1,64,1024]{3,2,1,0:T(8,128)(2,1)} %broadcast_select_fusion.1), kind=kLoop, calls=%fused_computation.18 | loop fusion | flops 524288 | bytes 2097152 | tf_op jit(solution)/shard_map/stack | solution.py:371
  9.0 45.6 %shard_map.46 = bf16[4,8,16,1024]{3,2,1,0:T(8,128)(2,1)} custom-call(bf16[4,2,64,1024]{3,2,1,0:T(8,128)(2,1)} %pad_maximum_fusion.t_ref), custom_call_target="tpu_custom_call" | custom-call | tf_op jit(solution)/shard_map/pallas_call | solution.py:375
  54.6 1.3 fusion.51
  55.9 0.0 copy-start.5
  55.9 0.0 copy-start.9
  55.9 2.8 %scatter_fusion = bf16[1024,1024]{1,0:T(8,128)(2,1)S(1)} fusion(bf16[1024,1024]{1,0:T(8,128)(2,1)S(1)} %bitcast.73, s32[256]{0:T(256)S(1)} %bitcast.98, bf16[256,1024]{1,0:T(8,128)(2,1)S(1)} %bitcast.94), kind=kCustom, calls=%fused_computation.2 | custom fusion | bytes 1573888 | tf_op jit(solution)/shard_map/scatter | solution.py:540
  58.8 0.0 copy-done.5
  58.8 0.2 fusion.5
  59.0 0.0 copy-start
  59.0 0.0 copy-done.9
  59.0 1.4 fusion
  60.4 34.2 %shard_map.47 = bf16[2,8,64,256]{3,2,1,0:T(8,128)(2,1)} custom-call(bf16[2,8,64,256]{3,2,1,0:T(8,128)(2,1)} %bitcast.96), custom_call_target="tpu_custom_call" | custom-call | tf_op jit(solution)/shard_map/pallas_call | solution.py:493
  94.6 1.6 broadcast_in_dim.78
  96.2 0.0 copy-done
  96.2 0.0 copy-start.6
  96.2 0.0 copy-start.7
  96.3 1.8 copy.10
  98.1 0.0 copy-start.1
  98.1 0.0 copy-done.6
  98.1 0.0 copy-done.7
  98.1 0.4 convolution_convert_fusion.2
  98.4 1.0 copy.7
  99.5 0.0 copy-done.1
  99.5 5.2 %and_select_fusion.4 = bf16[1024,1024]{1,0:T(8,128)(2,1)S(1)} fusion(bf16[1024,1024]{1,0:T(8,128)(2,1)} %bitcast.74, bf16[1024,1024]{1,0:T(8,128)(2,1)} %copy-done, pred[1024]{0:T(1024)(128)(4,1)S(1)} %get-tuple-element.57, pred[1024]{0:T(1024)(128)(4,1)S(1)} %get-tuple-element.54, pred[1024]{0:T(1024)(128)(4,1)S(1)} %get-tuple-element.56, ...), kind=kOutput, calls=%fused_computation.10 | convolution fusion | flops 546308096 | bytes 7868416 | tf_op jit(solution)/shard_map/dot_general | solution.py:559
  104.8 1.2 gather_fusion.1
  105.9 0.1 broadcast_select_fusion
  106.1 1.1 pad_maximum_fusion.1.t_ref
  107.2 44.2 %shard_map.48 = bf16[4,8,16,1024]{3,2,1,0:T(8,128)(2,1)} custom-call(bf16[4,2,64,1024]{3,2,1,0:T(8,128)(2,1)} %pad_maximum_fusion.1.t_ref), custom_call_target="tpu_custom_call" | custom-call | tf_op jit(solution)/shard_map/pallas_call | solution.py:375
  151.3 1.3 fusion.50
  152.7 0.0 copy-start.3
  152.7 3.0 %scatter_fusion.1 = bf16[1024,1024]{1,0:T(8,128)(2,1)S(1)} fusion(bf16[1024,1024]{1,0:T(8,128)(2,1)S(1)} %and_select_fusion.4, s32[256]{0:T(256)S(1)} %bitcast.99, bf16[256,1024]{1,0:T(8,128)(2,1)S(1)} %bitcast.93), kind=kCustom, calls=%fused_computation.3 | custom fusion | bytes 1573888 | tf_op jit(solution)/shard_map/scatter | solution.py:540
  155.7 0.0 copy-done.3
  155.7 0.2 fusion.3
  155.9 2.0 %fusion.1 = bf16[1024,256]{1,0:T(8,128)(2,1)} fusion(bf16[1024,1024]{1,0:T(8,128)(2,1)S(1)} %fusion.3, pred[]{:T(512)S(6)} %eq.100, bf16[2,256,256]{2,1,0:T(8,128)(2,1)} %param.11), kind=kOutput, calls=%fused_computation.17 | convolution fusion | flops 134742016 | bytes 1179649 | tf_op jit(solution)/shard_map/dot_general | solution.py:548
  157.9 24.0 %shard_map.49 = bf16[2,8,64,256]{3,2,1,0:T(8,128)(2,1)} custom-call(bf16[2,8,64,256]{3,2,1,0:T(8,128)(2,1)} %bitcast.97), custom_call_target="tpu_custom_call" | custom-call | tf_op jit(solution)/shard_map/pallas_call | solution.py:493
  182.0 1.6 broadcast_in_dim.82
  183.6 0.0 copy-start.4
  183.6 1.8 copy.11
  185.4 0.0 copy-start.2
  185.4 0.0 copy-done.4
  185.4 0.4 convolution_convert_fusion
  185.8 1.0 copy.8
  186.8 0.0 copy-done.2
  186.8 4.8 %and_select_fusion.5 = bf16[1024,1024]{1,0:T(8,128)(2,1)} fusion(bf16[1024,1024]{1,0:T(8,128)(2,1)} %bitcast.75, bf16[1024,1024]{1,0:T(8,128)(2,1)S(1)} %fusion.3, pred[1024]{0:T(1024)(128)(4,1)S(1)} %get-tuple-element.59, pred[1024]{0:T(1024)(128)(4,1)S(1)} %get-tuple-element.55, pred[1024]{0:T(1024)(128)(4,1)S(1)} %get-tuple-element.58, ...), kind=kOutput, calls=%fused_computation.11 | convolution fusion | flops 546308096 | bytes 7868416 | tf_op jit(solution)/shard_map/dot_general | solution.py:559
  191.6 4.5 %reshape.656 = bf16[4,256,4,256]{3,2,1,0:T(4,128)(2,1)} reshape(bf16[1024,1024]{1,0:T(8,128)(2,1)} %and_select_fusion.5) | data formatting | bytes 4194304 | tf_op jit(solution)/shard_map/reshape | solution.py:580
  (12 shorter events, 0.2 us)
Async XLA Ops:
  2.9 1.2 copy-start.8
  55.9 2.9 %copy-start.5 = (bf16[4,1,64,1024]{3,2,1,0:T(8,128)(2,1)}, bf16[4,1,64,1024]{3,2,1,0:T(8,128)(2,1)S(1)}, u32[]{:S(2)}) copy-start(bf16[4,1,64,1024]{3,2,1,0:T(8,128)(2,1)S(1)} %get-tuple-element.43) | copy-start | bytes 1572868
  55.9 3.1 %copy-start.9 = (bf16[2,256,256]{2,1,0:T(8,128)(2,1)S(1)}, bf16[2,256,256]{2,1,0:T(8,128)(2,1)}, u32[]{:S(2)}) copy-start(bf16[2,256,256]{2,1,0:T(8,128)(2,1)} %param.11) | copy-start | bytes 786436
  59.0 37.2 %copy-start = (bf16[1024,1024]{1,0:T(8,128)(2,1)}, bf16[1024,1024]{1,0:T(8,128)(2,1)S(1)}, u32[]{:S(2)}) copy-start(bf16[1024,1024]{1,0:T(8,128)(2,1)S(1)} %fusion.5) | copy-start | bytes 6291460
  96.2 1.8 copy-start.6
  96.2 1.8 copy-start.7
  98.1 1.4 copy-start.1
  152.7 3.1 %copy-start.3 = (bf16[4,1,64,1024]{3,2,1,0:T(8,128)(2,1)}, bf16[4,1,64,1024]{3,2,1,0:T(8,128)(2,1)S(1)}, u32[]{:S(2)}) copy-start(bf16[4,1,64,1024]{3,2,1,0:T(8,128)(2,1)S(1)} %get-tuple-element.41) | copy-start | bytes 1572868
  183.6 1.8 copy-start.4
  185.4 1.4 copy-start.2

commit v12 on v8

--- a/solution.py
+++ b/solution.py
@@ -406,15 +406,22 @@
         return (p, zz * nc + cc)
 
     barrier = pltpu.get_barrier_semaphore()
-    n = nz * nc
-
-    def greet(i, carry):
-        j = lax.rem(q + i, n)
-        pl.semaphore_signal(barrier, 1, device_id=(p, j), device_id_type=MESH)
-        return carry
-
-    lax.fori_loop(1, n, greet, 0)
-    pl.semaphore_wait(barrier, n - 1)
+    pl.semaphore_signal(barrier, 1, device_id=dev(z, 1 - c), device_id_type=MESH)
+
+    @pl.when(c == cs)
+    def _():
+        def greet(i, carry):
+            pl.semaphore_signal(
+                barrier, 1, device_id=dev(lax.rem(z + i, nz), cs), device_id_type=MESH
+            )
+            return carry
+
+        lax.fori_loop(1, nz, greet, 0)
+        pl.semaphore_wait(barrier, nz)
+
+    @pl.when(c != cs)
+    def _():
+        pl.semaphore_wait(barrier, 1)
 
     def spread(j):
         return pltpu.make_async_remote_copy(

time: 195 us -> 195 us (level)
  no operation moved by 1% of the time
where the time goes in v12:
time: 195 us; the launch traced here: 194 us
  Pallas kernels  146 us (75%)
  local copies, waits for them, and re-layouts  26.8 us (14%)
  matrix products  14.2 us (7%)
  other arithmetic  6.8 us (3%)
    pallas_call x2, Pallas kernels, prow_sum(): pl.pallas_call(functools.partial(prow_kernel, xd, yd, top), out_shape=jax...  89.8 us
    pallas_call x2, Pallas kernels, pcol_bcast(): pl.pallas_call(functools.partial(pcol_kernel, nz, source), out_shape=jax....  56.3 us
    dot_general x2, matrix products, local(): product = jnp.dot(lower, upper, preferred_element_type=jnp.float32)  10 us
    scatter x2, local copies, waits for them, and re-layouts, local(): current = current.at[target].set(old_top, mode='drop')  5.86 us
    unnamed x23, local copies, waits for them, and re-layouts  5.76 us
    reshape x1, local copies, waits for them, and re-layouts, local(): return current.reshape(matrix.shape)  4.49 us

profile of v12, /device:TPU:1, one launch (start us, length us, event | category | flops | bytes accessed | tf_op | source)
XLA Modules:
  0.0 194.1 jit_solution(15969695301322978293)
XLA Ops:
  0.0 0.8 and_select_fusion.9
  0.8 2.1 %copy.9 = bf16[128,8,4,256]{3,1,2,0:T(8,128)(2,1)S(1)} copy(bf16[128,8,4,256]{3,2,1,0:T(4,128)(2,1)} %bitcast.90) | data formatting | bytes 4194304
  2.9 0.0 copy-start.8
  2.9 1.2 gather_fusion
  4.1 0.0 copy-done.8
  4.1 0.1 squeeze.23
  4.2 0.1 squeeze.27
  4.3 0.9 broadcast_select_fusion.1
  5.2 1.3 slice_select_fusion.3
  6.5 0.4 select_n.397
  6.9 2.1 %pad_maximum_fusion.t_ref = bf16[4,2,64,1024]{3,2,1,0:T(8,128)(2,1)} fusion(bf16[4,1,64,1024]{3,2,1,0:T(8,128)(2,1)S(1)} %select_n.397, bf16[4,1,64,1024]{3,2,1,0:T(8,128)(2,1)} %broadcast_select_fusion.1), kind=kLoop, calls=%fused_computation.18 | loop fusion | flops 524288 | bytes 2097152 | tf_op jit(solution)/shard_map/stack | solution.py:371
  9.0 45.6 %shard_map.46 = bf16[4,8,16,1024]{3,2,1,0:T(8,128)(2,1)} custom-call(bf16[4,2,64,1024]{3,2,1,0:T(8,128)(2,1)} %pad_maximum_fusion.t_ref), custom_call_target="tpu_custom_call" | custom-call | tf_op jit(solution)/shard_map/pallas_call | solution.py:375
  54.6 1.3 fusion.51
  55.9 0.0 copy-start.5
  55.9 0.0 copy-start.9
  55.9 2.8 %scatter_fusion = bf16[1024,1024]{1,0:T(8,128)(2,1)S(1)} fusion(bf16[1024,1024]{1,0:T(8,128)(2,1)S(1)} %bitcast.73, s32[256]{0:T(256)S(1)} %bitcast.98, bf16[256,1024]{1,0:T(8,128)(2,1)S(1)} %bitcast.94), kind=kCustom, calls=%fused_computation.2 | custom fusion | bytes 1573888 | tf_op jit(solution)/shard_map/scatter | solution.py:550
  58.8 0.0 copy-done.5
  58.8 0.2 fusion.5
  59.0 0.0 copy-start
  59.0 0.0 copy-done.9
  59.0 1.4 fusion
  60.4 34.0 %shard_map.47 = bf16[8,128,256]{2,1,0:T(8,128)(2,1)} custom-call(bf16[8,128,256]{2,1,0:T(8,128)(2,1)} %bitcast.96), custom_call_target="tpu_custom_call" | custom-call | tf_op jit(solution)/shard_map/pallas_call | solution.py:503
  94.4 1.6 broadcast_in_dim.78
  96.0 0.0 copy-done
  96.0 0.0 copy-start.6
  96.0 0.0 copy-start.7
  96.0 1.8 copy.10
  97.9 0.0 copy-start.1
  97.9 0.0 copy-done.6
  97.9 0.0 copy-done.7
  97.9 0.4 convolution_convert_fusion.2
  98.2 1.0 copy.7
  99.3 0.0 copy-done.1
  99.3 5.3 %and_select_fusion.4 = bf16[1024,1024]{1,0:T(8,128)(2,1)S(1)} fusion(bf16[1024,1024]{1,0:T(8,128)(2,1)} %bitcast.74, bf16[1024,1024]{1,0:T(8,128)(2,1)} %copy-done, pred[1024]{0:T(1024)(128)(4,1)S(1)} %get-tuple-element.57, pred[1024]{0:T(1024)(128)(4,1)S(1)} %get-tuple-element.54, pred[1024]{0:T(1024)(128)(4,1)S(1)} %get-tuple-element.56, ...), kind=kOutput, calls=%fused_computation.10 | convolution fusion | flops 546308096 | bytes 7868416 | tf_op jit(solution)/shard_map/dot_general | solution.py:569
  104.6 1.2 gather_fusion.1
  105.7 0.1 broadcast_select_fusion
  105.9 1.1 pad_maximum_fusion.1.t_ref
  107.0 44.2 %shard_map.48 = bf16[4,8,16,1024]{3,2,1,0:T(8,128)(2,1)} custom-call(bf16[4,2,64,1024]{3,2,1,0:T(8,128)(2,1)} %pad_maximum_fusion.1.t_ref), custom_call_target="tpu_custom_call" | custom-call | tf_op jit(solution)/shard_map/pallas_call | solution.py:375
  151.1 1.3 fusion.50
  152.4 0.0 copy-start.3
  152.5 3.0 %scatter_fusion.1 = bf16[1024,1024]{1,0:T(8,128)(2,1)S(1)} fusion(bf16[1024,1024]{1,0:T(8,128)(2,1)S(1)} %and_select_fusion.4, s32[256]{0:T(256)S(1)} %bitcast.99, bf16[256,1024]{1,0:T(8,128)(2,1)S(1)} %bitcast.93), kind=kCustom, calls=%fused_computation.3 | custom fusion | bytes 1573888 | tf_op jit(solution)/shard_map/scatter | solution.py:550
  155.5 0.0 copy-done.3
  155.5 0.2 fusion.3
  155.7 2.0 %fusion.1 = bf16[1024,256]{1,0:T(8,128)(2,1)} fusion(bf16[1024,1024]{1,0:T(8,128)(2,1)S(1)} %fusion.3, pred[]{:T(512)S(6)} %eq.100, bf16[2,256,256]{2,1,0:T(8,128)(2,1)} %param.11), kind=kOutput, calls=%fused_computation.17 | convolution fusion | flops 134742016 | bytes 1179649 | tf_op jit(solution)/shard_map/dot_general | solution.py:558
  157.7 22.3 %shard_map.49 = bf16[8,128,256]{2,1,0:T(8,128)(2,1)} custom-call(bf16[8,128,256]{2,1,0:T(8,128)(2,1)} %bitcast.97), custom_call_target="tpu_custom_call" | custom-call | tf_op jit(solution)/shard_map/pallas_call | solution.py:503
  180.0 1.6 broadcast_in_dim.82
  181.6 0.0 copy-start.4
  181.6 1.8 copy.11
  183.5 0.0 copy-start.2
  183.5 0.0 copy-done.4
  183.5 0.4 convolution_convert_fusion
  183.8 1.0 copy.8
  184.8 0.0 copy-done.2
  184.9 4.8 %and_select_fusion.5 = bf16[1024,1024]{1,0:T(8,128)(2,1)} fusion(bf16[1024,1024]{1,0:T(8,128)(2,1)} %bitcast.75, bf16[1024,1024]{1,0:T(8,128)(2,1)S(1)} %fusion.3, pred[1024]{0:T(1024)(128)(4,1)S(1)} %get-tuple-element.59, pred[1024]{0:T(1024)(128)(4,1)S(1)} %get-tuple-element.55, pred[1024]{0:T(1024)(128)(4,1)S(1)} %get-tuple-element.58, ...), kind=kOutput, calls=%fused_computation.11 | convolution fusion | flops 546308096 | bytes 7868416 | tf_op jit(solution)/shard_map/dot_general | solution.py:569
  189.6 4.5 %reshape.656 = bf16[4,256,4,256]{3,2,1,0:T(4,128)(2,1)} reshape(bf16[1024,1024]{1,0:T(8,128)(2,1)} %and_select_fusion.5) | data formatting | bytes 4194304 | tf_op jit(solution)/shard_map/reshape | solution.py:590
  (12 shorter events, 0.2 us)
Async XLA Ops:
  2.9 1.2 copy-start.8
  55.9 2.9 %copy-start.5 = (bf16[4,1,64,1024]{3,2,1,0:T(8,128)(2,1)}, bf16[4,1,64,1024]{3,2,1,0:T(8,128)(2,1)S(1)}, u32[]{:S(2)}) copy-start(bf16[4,1,64,1024]{3,2,1,0:T(8,128)(2,1)S(1)} %get-tuple-element.43) | copy-start | bytes 1572868
  55.9 3.1 %copy-start.9 = (bf16[2,256,256]{2,1,0:T(8,128)(2,1)S(1)}, bf16[2,256,256]{2,1,0:T(8,128)(2,1)}, u32[]{:S(2)}) copy-start(bf16[2,256,256]{2,1,0:T(8,128)(2,1)} %param.11) | copy-start | bytes 786436
  59.0 37.0 %copy-start = (bf16[1024,1024]{1,0:T(8,128)(2,1)}, bf16[1024,1024]{1,0:T(8,128)(2,1)S(1)}, u32[]{:S(2)}) copy-start(bf16[1024,1024]{1,0:T(8,128)(2,1)S(1)} %fusion.5) | copy-start | bytes 6291460
  96.0 1.8 copy-start.6
  96.0 1.8 copy-start.7
  97.9 1.4 copy-start.1
  152.4 3.1 %copy-start.3 = (bf16[4,1,64,1024]{3,2,1,0:T(8,128)(2,1)}, bf16[4,1,64,1024]{3,2,1,0:T(8,128)(2,1)S(1)}, u32[]{:S(2)}) copy-start(bf16[4,1,64,1024]{3,2,1,0:T(8,128)(2,1)S(1)} %get-tuple-element.41) | copy-start | bytes 1572868
  181.6 1.8 copy-start.4
  183.5 1.4 copy-start.2

commit v13 on v12

--- a/solution.py
+++ b/solution.py
@@ -462,12 +462,6 @@
         lax.fori_loop(1, nz, start, 0)
         g[zs] = x_ref[zs]
 
-        def sent(i, carry):
-            spread(lax.rem(zs + i, nz)).wait_send()
-            return carry
-
-        lax.fori_loop(1, nz, sent, 0)
-
     @pl.when((c == cs) & (z != zs))
     def _():
         spread(z).wait_recv()
@@ -493,6 +487,14 @@
     @pl.when(c != cs)
     def _():
         partner(z).wait_recv()
+
+    @pl.when(q == source)
+    def _():
+        def sent(i, carry):
+            spread(lax.rem(zs + i, nz)).wait_send()
+            return carry
+
+        lax.fori_loop(1, nz, sent, 0)
 
     o_ref[...] = g[...]
 

time: 195 us -> 195 us (level)
  no operation moved by 1% of the time
where the time goes in v13:
time: 195 us; the launch traced here: 194 us
  Pallas kernels  146 us (75%)
  local copies, waits for them, and re-layouts  26.8 us (14%)
  matrix products  14.2 us (7%)
  other arithmetic  6.8 us (3%)
    pallas_call x2, Pallas kernels, prow_sum(): pl.pallas_call(functools.partial(prow_kernel, xd, yd, top), out_shape=jax...  89.8 us
    pallas_call x2, Pallas kernels, pcol_bcast(): pl.pallas_call(functools.partial(pcol_kernel, nz, source), out_shape=jax....  56.5 us
    dot_general x2, matrix products, local(): product = jnp.dot(lower, upper, preferred_element_type=jnp.float32)  10 us
    scatter x2, local copies, waits for them, and re-layouts, local(): current = current.at[target].set(old_top, mode='drop')  5.86 us
    unnamed x23, local copies, waits for them, and re-layouts  5.76 us
    reshape x1, local copies, waits for them, and re-layouts, local(): return current.reshape(matrix.shape)  4.49 us

profile of v13, /device:TPU:1, one launch (start us, length us, event | category | flops | bytes accessed | tf_op | source)
XLA Modules:
  0.0 194.3 jit_solution(7500964660588332786)
XLA Ops:
  0.0 0.8 and_select_fusion.9
  0.8 2.1 %copy.9 = bf16[128,8,4,256]{3,1,2,0:T(8,128)(2,1)S(1)} copy(bf16[128,8,4,256]{3,2,1,0:T(4,128)(2,1)} %bitcast.90) | data formatting | bytes 4194304
  2.9 0.0 copy-start.8
  2.9 1.2 gather_fusion
  4.1 0.0 copy-done.8
  4.1 0.1 squeeze.23
  4.2 0.1 squeeze.27
  4.3 0.9 broadcast_select_fusion.1
  5.2 1.3 slice_select_fusion.3
  6.5 0.4 select_n.397
  6.9 2.1 %pad_maximum_fusion.t_ref = bf16[4,2,64,1024]{3,2,1,0:T(8,128)(2,1)} fusion(bf16[4,1,64,1024]{3,2,1,0:T(8,128)(2,1)S(1)} %select_n.397, bf16[4,1,64,1024]{3,2,1,0:T(8,128)(2,1)} %broadcast_select_fusion.1), kind=kLoop, calls=%fused_computation.18 | loop fusion | flops 524288 | bytes 2097152 | tf_op jit(solution)/shard_map/stack | solution.py:371
  9.0 45.6 %shard_map.46 = bf16[4,8,16,1024]{3,2,1,0:T(8,128)(2,1)} custom-call(bf16[4,2,64,1024]{3,2,1,0:T(8,128)(2,1)} %pad_maximum_fusion.t_ref), custom_call_target="tpu_custom_call" | custom-call | tf_op jit(solution)/shard_map/pallas_call | solution.py:375
  54.6 1.3 fusion.51
  55.9 0.0 copy-start.5
  55.9 0.0 copy-start.9
  55.9 2.8 %scatter_fusion = bf16[1024,1024]{1,0:T(8,128)(2,1)S(1)} fusion(bf16[1024,1024]{1,0:T(8,128)(2,1)S(1)} %bitcast.73, s32[256]{0:T(256)S(1)} %bitcast.98, bf16[256,1024]{1,0:T(8,128)(2,1)S(1)} %bitcast.94), kind=kCustom, calls=%fused_computation.2 | custom fusion | bytes 1573888 | tf_op jit(solution)/shard_map/scatter | solution.py:552
  58.8 0.0 copy-done.5
  58.8 0.2 fusion.5
  59.0 0.0 copy-start
  59.0 0.0 copy-done.9
  59.0 1.4 fusion
  60.4 34.0 %shard_map.47 = bf16[8,128,256]{2,1,0:T(8,128)(2,1)} custom-call(bf16[8,128,256]{2,1,0:T(8,128)(2,1)} %bitcast.96), custom_call_target="tpu_custom_call" | custom-call | tf_op jit(solution)/shard_map/pallas_call | solution.py:505
  94.4 1.6 broadcast_in_dim.78
  96.0 0.0 copy-done
  96.0 0.0 copy-start.6
  96.0 0.0 copy-start.7
  96.0 1.8 copy.10
  97.9 0.0 copy-start.1
  97.9 0.0 copy-done.6
  97.9 0.0 copy-done.7
  97.9 0.4 convolution_convert_fusion.2
  98.2 1.0 copy.7
  99.3 0.0 copy-done.1
  99.3 5.2 %and_select_fusion.4 = bf16[1024,1024]{1,0:T(8,128)(2,1)S(1)} fusion(bf16[1024,1024]{1,0:T(8,128)(2,1)} %bitcast.74, bf16[1024,1024]{1,0:T(8,128)(2,1)} %copy-done, pred[1024]{0:T(1024)(128)(4,1)S(1)} %get-tuple-element.57, pred[1024]{0:T(1024)(128)(4,1)S(1)} %get-tuple-element.54, pred[1024]{0:T(1024)(128)(4,1)S(1)} %get-tuple-element.56, ...), kind=kOutput, calls=%fused_computation.10 | convolution fusion | flops 546308096 | bytes 7868416 | tf_op jit(solution)/shard_map/dot_general | solution.py:571
  104.6 1.2 gather_fusion.1
  105.7 0.1 broadcast_select_fusion
  105.9 1.1 pad_maximum_fusion.1.t_ref
  107.0 44.2 %shard_map.48 = bf16[4,8,16,1024]{3,2,1,0:T(8,128)(2,1)} custom-call(bf16[4,2,64,1024]{3,2,1,0:T(8,128)(2,1)} %pad_maximum_fusion.1.t_ref), custom_call_target="tpu_custom_call" | custom-call | tf_op jit(solution)/shard_map/pallas_call | solution.py:375
  151.2 1.3 fusion.50
  152.5 0.0 copy-start.3
  152.5 3.0 %scatter_fusion.1 = bf16[1024,1024]{1,0:T(8,128)(2,1)S(1)} fusion(bf16[1024,1024]{1,0:T(8,128)(2,1)S(1)} %and_select_fusion.4, s32[256]{0:T(256)S(1)} %bitcast.99, bf16[256,1024]{1,0:T(8,128)(2,1)S(1)} %bitcast.93), kind=kCustom, calls=%fused_computation.3 | custom fusion | bytes 1573888 | tf_op jit(solution)/shard_map/scatter | solution.py:552
  155.5 0.0 copy-done.3
  155.5 0.2 fusion.3
  155.8 2.0 %fusion.1 = bf16[1024,256]{1,0:T(8,128)(2,1)} fusion(bf16[1024,1024]{1,0:T(8,128)(2,1)S(1)} %fusion.3, pred[]{:T(512)S(6)} %eq.100, bf16[2,256,256]{2,1,0:T(8,128)(2,1)} %param.11), kind=kOutput, calls=%fused_computation.17 | convolution fusion | flops 134742016 | bytes 1179649 | tf_op jit(solution)/shard_map/dot_general | solution.py:560
  157.8 22.5 %shard_map.49 = bf16[8,128,256]{2,1,0:T(8,128)(2,1)} custom-call(bf16[8,128,256]{2,1,0:T(8,128)(2,1)} %bitcast.97), custom_call_target="tpu_custom_call" | custom-call | tf_op jit(solution)/shard_map/pallas_call | solution.py:505
  180.2 1.6 broadcast_in_dim.82
  181.8 0.0 copy-start.4
  181.8 1.8 copy.11
  183.7 0.0 copy-start.2
  183.7 0.0 copy-done.4
  183.7 0.4 convolution_convert_fusion
  184.0 1.0 copy.8
  185.1 0.0 copy-done.2
  185.1 4.8 %and_select_fusion.5 = bf16[1024,1024]{1,0:T(8,128)(2,1)} fusion(bf16[1024,1024]{1,0:T(8,128)(2,1)} %bitcast.75, bf16[1024,1024]{1,0:T(8,128)(2,1)S(1)} %fusion.3, pred[1024]{0:T(1024)(128)(4,1)S(1)} %get-tuple-element.59, pred[1024]{0:T(1024)(128)(4,1)S(1)} %get-tuple-element.55, pred[1024]{0:T(1024)(128)(4,1)S(1)} %get-tuple-element.58, ...), kind=kOutput, calls=%fused_computation.11 | convolution fusion | flops 546308096 | bytes 7868416 | tf_op jit(solution)/shard_map/dot_general | solution.py:571
  189.9 4.5 %reshape.656 = bf16[4,256,4,256]{3,2,1,0:T(4,128)(2,1)} reshape(bf16[1024,1024]{1,0:T(8,128)(2,1)} %and_select_fusion.5) | data formatting | bytes 4194304 | tf_op jit(solution)/shard_map/reshape | solution.py:592
  (12 shorter events, 0.2 us)
Async XLA Ops:
  2.9 1.2 copy-start.8
  55.9 2.9 %copy-start.5 = (bf16[4,1,64,1024]{3,2,1,0:T(8,128)(2,1)}, bf16[4,1,64,1024]{3,2,1,0:T(8,128)(2,1)S(1)}, u32[]{:S(2)}) copy-start(bf16[4,1,64,1024]{3,2,1,0:T(8,128)(2,1)S(1)} %get-tuple-element.43) | copy-start | bytes 1572868
  55.9 3.1 %copy-start.9 = (bf16[2,256,256]{2,1,0:T(8,128)(2,1)S(1)}, bf16[2,256,256]{2,1,0:T(8,128)(2,1)}, u32[]{:S(2)}) copy-start(bf16[2,256,256]{2,1,0:T(8,128)(2,1)} %param.11) | copy-start | bytes 786436
  59.0 37.0 %copy-start = (bf16[1024,1024]{1,0:T(8,128)(2,1)}, bf16[1024,1024]{1,0:T(8,128)(2,1)S(1)}, u32[]{:S(2)}) copy-start(bf16[1024,1024]{1,0:T(8,128)(2,1)S(1)} %fusion.5) | copy-start | bytes 6291460
  96.0 1.8 copy-start.6
  96.0 1.8 copy-start.7
  97.9 1.4 copy-start.1
  152.5 3.1 %copy-start.3 = (bf16[4,1,64,1024]{3,2,1,0:T(8,128)(2,1)}, bf16[4,1,64,1024]{3,2,1,0:T(8,128)(2,1)S(1)}, u32[]{:S(2)}) copy-start(bf16[4,1,64,1024]{3,2,1,0:T(8,128)(2,1)S(1)} %get-tuple-element.41) | copy-start | bytes 1572868
  181.8 1.8 copy-start.4
  183.7 1.4 copy-start.2

commit v14 on v13

--- a/solution.py
+++ b/solution.py
@@ -519,6 +519,45 @@
         compiler_params=pltpu.CompilerParams(collective_id=collective_id, has_side_effects=True),
     )(chunks)
     return out.reshape(rows, cols)
+
+
+def update_kernel(a_ref, l_ref, u_ref, rf_ref, cf_ref, o_ref):
+    a = a_ref[...]
+    lower = l_ref[...]
+    upper = u_ref[...]
+    product = jnp.dot(lower, upper, preferred_element_type=jnp.float32)
+    changed = (a.astype(jnp.float32) - product).astype(a.dtype)
+    reps = a.shape[1] // lower.shape[1]
+    lower_wide = jnp.concatenate([lower] * reps, axis=1)
+    rf = rf_ref[...]
+    cf = cf_ref[...]
+    below = (rf & 1) == 1
+    in_top = (rf & 2) == 2
+    right = (cf & 1) == 1
+    in_panel = (cf & 2) == 2
+    o_ref[...] = jnp.where(
+        below & right,
+        changed,
+        jnp.where(in_panel & below, lower_wide, jnp.where(in_top & right, upper, a)),
+    )
+
+
+def trailing_update(a, lower, upper, row_flags, col_flags):
+    rows, cols = a.shape
+    block = upper.shape[0]
+    return pl.pallas_call(
+        update_kernel,
+        out_shape=jax.ShapeDtypeStruct(a.shape, a.dtype),
+        grid=(rows // block,),
+        in_specs=[
+            pl.BlockSpec((block, cols), lambda i: (i, 0)),
+            pl.BlockSpec((block, block), lambda i: (i, 0)),
+            pl.BlockSpec((block, cols), lambda i: (0, 0)),
+            pl.BlockSpec((block, 1), lambda i: (i, 0)),
+            pl.BlockSpec((1, cols), lambda i: (0, 0)),
+        ],
+        out_specs=pl.BlockSpec((block, cols), lambda i: (i, 0)),
+    )(a, lower, upper, row_flags, col_flags)
 
 
 def local(x_devices, z_chips, matrix, pivots, lower_inverse, upper_inverse):
@@ -568,26 +607,12 @@
         ).astype(jnp.bfloat16)
         row_mask = global_rows >= start + block
         col_mask = global_cols >= start + block
-        product = jnp.dot(lower, upper, preferred_element_type=jnp.float32)
-        changed = (current.astype(jnp.float32) - product).astype(jnp.bfloat16)
-        below = row_mask[:, None]
-        right = col_mask[None, :]
-        in_panel = is_panel & (col_place // block == panel_first // block)[None, :]
-        in_top = is_top & (row_place // block == top_first // block)[:, None]
-        lower_wide = jnp.broadcast_to(
-            lower[:, None, :], (local_rows, blocks_across, block)
-        ).reshape(local_rows, local_cols)
-        upper_tall = jnp.broadcast_to(
-            upper[None], (blocks_down, block, local_cols)
-        ).reshape(local_rows, local_cols)
-        current = jnp.where(
-            below & right,
-            changed,
-            jnp.where(
-                in_panel & below,
-                lower_wide,
-                jnp.where(in_top & right, upper_tall, current),
-            ),
+        below = row_mask.astype(jnp.int32)
+        right = col_mask.astype(jnp.int32)
+        in_panel = (is_panel & (col_place // block == panel_first // block)).astype(jnp.int32)
+        in_top = (is_top & (row_place // block == top_first // block)).astype(jnp.int32)
+        current = trailing_update(
+            current, lower, upper, (below + 2 * in_top)[:, None], (right + 2 * in_panel)[None, :]
         )
     return current.reshape(matrix.shape)
 

time: 195 us -> 195 us (level)
  Pallas kernels: 146 us -> 159 us
  matrix products: 14.2 us -> 6.49 us
  local copies, waits for them, and re-layouts: 26.8 us -> 20.2 us
    pallas_call x0 -> x2, Pallas kernels: none -> 12.7 us  [trailing_update(): pl.pallas_call(update_kernel, out_shape=jax.ShapeDtypeStruct(a.shape, a.d...]
    dot_general x2 -> x0, matrix products: 10 us -> none  [local(): product = jnp.dot(lower, upper, preferred_element_type=jnp.float32)]
    unnamed x23 -> x11, local copies, waits for them, and re-layouts: 5.76 us -> 2.11 us
    broadcast_in_dim x2 -> x0, local copies, waits for them, and re-layouts: 3.17 us -> none  [local(): jnp.broadcast_to(lower[:, None, :], (local_rows, blocks_across, block))]
    gather x2, local copies, waits for them, and re-layouts: 2.34 us -> 4.73 us  [local(): current[safe_index]]
    convert_element_type x2 -> x0, local copies, waits for them, and re-layouts: 2.02 us -> none  [local(): upper = jnp.dot(lower_inverse[panel], incoming, preferred_element_type=jn...]
where the time goes in v14:
time: 195 us; the launch traced here: 194 us
  Pallas kernels  159 us (82%)
  local copies, waits for them, and re-layouts  20.2 us (10%)
  other arithmetic  8.56 us (4%)
  matrix products  6.49 us (3%)
    pallas_call x2, Pallas kernels, prow_sum(): pl.pallas_call(functools.partial(prow_kernel, xd, yd, top), out_shape=jax...  89.2 us
    pallas_call x2, Pallas kernels, pcol_bcast(): pl.pallas_call(functools.partial(pcol_kernel, nz, source), out_shape=jax....  57 us
    pallas_call x2, Pallas kernels, trailing_update(): pl.pallas_call(update_kernel, out_shape=jax.ShapeDtypeStruct(a.shape, a.d...  12.7 us
    scatter x2, local copies, waits for them, and re-layouts, local(): current = current.at[target].set(old_top, mode='drop')  5.68 us
    gather x2, local copies, waits for them, and re-layouts, local(): current[safe_index]  4.73 us
    reshape x1, local copies, waits for them, and re-layouts, local(): return current.reshape(matrix.shape)  4.49 us
    dot_general x2, matrix products, local(): jnp.dot(panel_cols, upper_inverse[panel], preferred_element_type=jnp.floa...  4.3 us

profile of v14, /device:TPU:1, one launch (start us, length us, event | category | flops | bytes accessed | tf_op | source)
XLA Modules:
  0.0 194.3 jit_solution(6009177242632118210)
XLA Ops:
  0.0 0.8 and_select_fusion.7
  0.8 2.1 %copy.33 = bf16[128,8,4,256]{3,1,2,0:T(8,128)(2,1)S(1)} copy(bf16[128,8,4,256]{3,2,1,0:T(4,128)(2,1)} %bitcast.80) | data formatting | bytes 4194304
  2.9 0.0 copy-start.4
  2.9 1.2 gather_fusion
  4.1 0.0 copy-done.4
  4.1 0.1 squeeze.23
  4.2 0.1 squeeze.27
  4.3 0.9 broadcast_select_fusion.1
  5.2 1.3 slice_select_fusion.3
  6.5 0.4 select_n.380
  6.9 2.1 %pad_maximum_fusion.t_ref = bf16[4,2,64,1024]{3,2,1,0:T(8,128)(2,1)} fusion(bf16[4,1,64,1024]{3,2,1,0:T(8,128)(2,1)S(1)} %select_n.380, bf16[4,1,64,1024]{3,2,1,0:T(8,128)(2,1)} %broadcast_select_fusion.1), kind=kLoop, calls=%fused_computation.12 | loop fusion | flops 524288 | bytes 2097152 | tf_op jit(solution)/shard_map/stack | solution.py:371
  9.0 45.6 %shard_map.46 = bf16[4,8,16,1024]{3,2,1,0:T(8,128)(2,1)} custom-call(bf16[4,2,64,1024]{3,2,1,0:T(8,128)(2,1)} %pad_maximum_fusion.t_ref), custom_call_target="tpu_custom_call" | custom-call | tf_op jit(solution)/shard_map/pallas_call | solution.py:375
  54.6 1.3 fusion.44
  55.9 2.8 %scatter_fusion = bf16[1024,1024]{1,0:T(8,128)(2,1)S(1)} fusion(bf16[1024,1024]{1,0:T(8,128)(2,1)S(1)} %bitcast.73, s32[256]{0:T(256)S(1)} %bitcast.90, bf16[256,1024]{1,0:T(8,128)(2,1)S(1)} %bitcast.86), kind=kCustom, calls=%fused_computation.2 | custom fusion | bytes 1573888 | tf_op jit(solution)/shard_map/scatter | solution.py:591
  58.7 0.0 copy-start.3
  58.8 0.2 fusion.19.a_ref
  59.0 0.0 copy-start.2
  59.0 2.2 %fusion = bf16[1024,256]{1,0:T(8,128)(2,1)} fusion(bf16[1024,1024]{1,0:T(8,128)(2,1)S(1)} %fusion.19.a_ref, pred[]{:T(512)S(6)} %eq.103, bf16[2,256,256]{2,1,0:T(8,128)(2,1)} %param.11), kind=kOutput, calls=%fused_computation.8 | convolution fusion | flops 134742016 | bytes 1179649 | tf_op jit(solution)/shard_map/dot_general | solution.py:599
  61.2 34.0 %shard_map.47 = bf16[8,128,256]{2,1,0:T(8,128)(2,1)} custom-call(bf16[8,128,256]{2,1,0:T(8,128)(2,1)} %bitcast.89), custom_call_target="tpu_custom_call" | custom-call | tf_op jit(solution)/shard_map/pallas_call | solution.py:505
  95.2 0.0 copy-done.3
  95.2 1.1 fusion.2.u_ref
  96.3 1.2 select_add_fusion
  97.4 0.0 copy-done.2
  97.5 0.6 fusion.29
  98.1 6.3 %shard_map.48 = bf16[1024,1024]{1,0:T(8,128)(2,1)} custom-call(bf16[1024,1024]{1,0:T(8,128)(2,1)} %copy-done.2, bf16[1024,256]{1,0:T(8,128)(2,1)} %bitcast.81, bf16[256,1024]{1,0:T(8,128)(2,1)} %fusion.2.u_ref, s32[1024,1]{1,0:T(8,128)} %get-tuple-element.48.rf_ref, s32[1,1024]{1,0:T(1,128)} %get-tuple-element.54.cf_ref), custom_call_target="tpu_custom_call" | custom-call | tf_op jit(solution)/shard_map/pallas_call | solution.py:548
  104.4 0.0 copy-start
  104.4 3.6 %gather_fusion.1 = bf16[256,1024]{1,0:T(8,128)(2,1)S(1)} fusion(bf16[1024,1024]{1,0:T(8,128)(2,1)} %shard_map.48, s32[1024]{0:T(1024)S(1)} %pad_clamp_fusion), kind=kCustom, calls=%fused_computation.1 | custom fusion | bytes 1049600 | tf_op jit(solution)/shard_map/gather | solution.py:583
  108.0 0.1 broadcast_select_fusion
  108.1 0.0 copy-done
  108.2 1.1 pad_maximum_fusion.1.t_ref
  109.2 43.6 %shard_map.49 = bf16[4,8,16,1024]{3,2,1,0:T(8,128)(2,1)} custom-call(bf16[4,2,64,1024]{3,2,1,0:T(8,128)(2,1)} %pad_maximum_fusion.1.t_ref), custom_call_target="tpu_custom_call" | custom-call | tf_op jit(solution)/shard_map/pallas_call | solution.py:375
  152.8 1.3 fusion.43
  154.2 2.8 %scatter_fusion.1 = bf16[1024,1024]{1,0:T(8,128)(2,1)S(1)} fusion(bf16[1024,1024]{1,0:T(8,128)(2,1)S(1)} %copy-done, s32[256]{0:T(256)S(1)} %bitcast.91, bf16[256,1024]{1,0:T(8,128)(2,1)S(1)} %bitcast.85), kind=kCustom, calls=%fused_computation.3 | custom fusion | bytes 1573888 | tf_op jit(solution)/shard_map/scatter | solution.py:591
  157.0 0.2 fusion.17.a_ref
  157.2 0.0 copy-start.1
  157.2 2.1 %fusion.1 = bf16[1024,256]{1,0:T(8,128)(2,1)} fusion(bf16[1024,1024]{1,0:T(8,128)(2,1)S(1)} %fusion.17.a_ref, pred[]{:T(512)S(6)} %eq.109, bf16[2,256,256]{2,1,0:T(8,128)(2,1)} %param.11), kind=kOutput, calls=%fused_computation.9 | convolution fusion | flops 134742016 | bytes 1179649 | tf_op jit(solution)/shard_map/dot_general | solution.py:599
  159.4 23.0 %shard_map.50 = bf16[8,128,256]{2,1,0:T(8,128)(2,1)} custom-call(bf16[8,128,256]{2,1,0:T(8,128)(2,1)} %bitcast.88), custom_call_target="tpu_custom_call" | custom-call | tf_op jit(solution)/shard_map/pallas_call | solution.py:505
  182.4 1.1 fusion.3.u_ref
  183.5 0.0 copy-done.1
  183.5 6.4 %shard_map.51 = bf16[1024,1024]{1,0:T(8,128)(2,1)} custom-call(bf16[1024,1024]{1,0:T(8,128)(2,1)} %copy-done.1, bf16[1024,256]{1,0:T(8,128)(2,1)} %bitcast.82, bf16[256,1024]{1,0:T(8,128)(2,1)} %fusion.3.u_ref, s32[1024,1]{1,0:T(8,128)} %get-tuple-element.47.rf_ref, s32[1,1024]{1,0:T(1,128)} %get-tuple-element.55.cf_ref), custom_call_target="tpu_custom_call" | custom-call | tf_op jit(solution)/shard_map/pallas_call | solution.py:548
  189.8 4.5 %reshape.752 = bf16[4,256,4,256]{3,2,1,0:T(4,128)(2,1)} reshape(bf16[1024,1024]{1,0:T(8,128)(2,1)} %shard_map.51) | data formatting | bytes 4194304 | tf_op jit(solution)/shard_map/reshape | solution.py:617
  (8 shorter events, 0.1 us)
Async XLA Ops:
  2.9 1.2 copy-start.4
  58.7 36.4 %copy-start.3 = (bf16[2,256,256]{2,1,0:T(8,128)(2,1)S(1)}, bf16[2,256,256]{2,1,0:T(8,128)(2,1)}, u32[]{:S(2)}) copy-start(bf16[2,256,256]{2,1,0:T(8,128)(2,1)} %param.10) | copy-start | bytes 786436
  59.0 38.5 %copy-start.2 = (bf16[1024,1024]{1,0:T(8,128)(2,1)}, bf16[1024,1024]{1,0:T(8,128)(2,1)S(1)}, u32[]{:S(2)}) copy-start(bf16[1024,1024]{1,0:T(8,128)(2,1)S(1)} %fusion.19.a_ref) | copy-start | bytes 6291460
  104.4 3.7 %copy-start = (bf16[1024,1024]{1,0:T(8,128)(2,1)S(1)}, bf16[1024,1024]{1,0:T(8,128)(2,1)}, u32[]{:S(2)}) copy-start(bf16[1024,1024]{1,0:T(8,128)(2,1)} %shard_map.48) | copy-start | bytes 6291460
  157.2 26.3 %copy-start.1 = (bf16[1024,1024]{1,0:T(8,128)(2,1)}, bf16[1024,1024]{1,0:T(8,128)(2,1)S(1)}, u32[]{:S(2)}) copy-start(bf16[1024,1024]{1,0:T(8,128)(2,1)S(1)} %fusion.17.a_ref) | copy-start | bytes 6291460

commit v15 on v13

--- a/solution.py
+++ b/solution.py
@@ -519,6 +519,47 @@
         compiler_params=pltpu.CompilerParams(collective_id=collective_id, has_side_effects=True),
     )(chunks)
     return out.reshape(rows, cols)
+
+
+def update_kernel(rf_ref, cf_ref, a_ref, l_ref, u_ref, o_ref):
+    rb = rf_ref[pl.program_id(0)]
+    below = (rb & 1) == 1
+    in_top = (rb & 2) == 2
+    lower = l_ref[...]
+    block = lower.shape[1]
+    for c in range(a_ref.shape[1] // block):
+        cols = slice(c * block, (c + 1) * block)
+        cb = cf_ref[c]
+        right = (cb & 1) == 1
+        in_panel = (cb & 2) == 2
+        a = a_ref[:, cols]
+        upper = u_ref[:, cols]
+        product = jnp.dot(lower, upper, preferred_element_type=jnp.float32)
+        changed = (a.astype(jnp.float32) - product).astype(a.dtype)
+        o_ref[:, cols] = jnp.where(
+            below & right,
+            changed,
+            jnp.where(in_panel & below, lower, jnp.where(in_top & right, upper, a)),
+        )
+
+
+def trailing_update(a, lower, upper, row_flags, col_flags):
+    rows, cols = a.shape
+    block = upper.shape[0]
+    return pl.pallas_call(
+        update_kernel,
+        out_shape=jax.ShapeDtypeStruct(a.shape, a.dtype),
+        grid_spec=pltpu.PrefetchScalarGridSpec(
+            num_scalar_prefetch=2,
+            grid=(rows // block,),
+            in_specs=[
+                pl.BlockSpec((block, cols), lambda i, rf, cf: (i, 0)),
+                pl.BlockSpec((block, block), lambda i, rf, cf: (i, 0)),
+                pl.BlockSpec((block, cols), lambda i, rf, cf: (0, 0)),
+            ],
+            out_specs=pl.BlockSpec((block, cols), lambda i, rf, cf: (i, 0)),
+        ),
+    )(row_flags, col_flags, a, lower, upper)
 
 
 def local(x_devices, z_chips, matrix, pivots, lower_inverse, upper_inverse):
@@ -568,27 +609,13 @@
         ).astype(jnp.bfloat16)
         row_mask = global_rows >= start + block
         col_mask = global_cols >= start + block
-        product = jnp.dot(lower, upper, preferred_element_type=jnp.float32)
-        changed = (current.astype(jnp.float32) - product).astype(jnp.bfloat16)
-        below = row_mask[:, None]
-        right = col_mask[None, :]
-        in_panel = is_panel & (col_place // block == panel_first // block)[None, :]
-        in_top = is_top & (row_place // block == top_first // block)[:, None]
-        lower_wide = jnp.broadcast_to(
-            lower[:, None, :], (local_rows, blocks_across, block)
-        ).reshape(local_rows, local_cols)
-        upper_tall = jnp.broadcast_to(
-            upper[None], (blocks_down, block, local_cols)
-        ).reshape(local_rows, local_cols)
-        current = jnp.where(
-            below & right,
-            changed,
-            jnp.where(
-                in_panel & below,
-                lower_wide,
-                jnp.where(in_top & right, upper_tall, current),
-            ),
-        )
+        row_blocks = row_place[::block] // block
+        col_blocks = col_place[::block] // block
+        below = (row_blocks * row_count + my_row >= panel + 1).astype(jnp.int32)
+        right = (col_blocks * col_count + my_col >= panel + 1).astype(jnp.int32)
+        in_top = (is_top & (row_blocks == top_first // block)).astype(jnp.int32)
+        in_panel = (is_panel & (col_blocks == panel_first // block)).astype(jnp.int32)
+        current = trailing_update(current, lower, upper, below + 2 * in_top, right + 2 * in_panel)
     return current.reshape(matrix.shape)
 
 

time: 195 us -> 193 us (0.990)
  Pallas kernels: 146 us -> 157 us
  matrix products: 14.2 us -> 6.54 us
  local copies, waits for them, and re-layouts: 26.8 us -> 20.3 us
    pallas_call x0 -> x2, Pallas kernels: none -> 10.9 us  [trailing_update(): pl.pallas_call(update_kernel, out_shape=jax.ShapeDtypeStruct(a.shape, a.d...]
    dot_general x2 -> x0, matrix products: 10 us -> none  [local(): product = jnp.dot(lower, upper, preferred_element_type=jnp.float32)]
    unnamed x23 -> x11, local copies, waits for them, and re-layouts: 5.76 us -> 2.11 us
    broadcast_in_dim x2 -> x0, local copies, waits for them, and re-layouts: 3.17 us -> none  [local(): jnp.broadcast_to(lower[:, None, :], (local_rows, blocks_across, block))]
    gather x2, local copies, waits for them, and re-layouts: 2.34 us -> 4.73 us  [local(): current[safe_index]]
    convert_element_type x2 -> x0, local copies, waits for them, and re-layouts: 2.02 us -> none  [local(): upper = jnp.dot(lower_inverse[panel], incoming, preferred_element_type=jn...]
where the time goes in v15:
time: 193 us; the launch traced here: 192 us
  Pallas kernels  157 us (81%)
  local copies, waits for them, and re-layouts  20.3 us (11%)
  other arithmetic  7.94 us (4%)
  matrix products  6.54 us (3%)
    pallas_call x2, Pallas kernels, prow_sum(): pl.pallas_call(functools.partial(prow_kernel, xd, yd, top), out_shape=jax...  89 us
    pallas_call x2, Pallas kernels, pcol_bcast(): pl.pallas_call(functools.partial(pcol_kernel, nz, source), out_shape=jax....  57 us
    pallas_call x2, Pallas kernels, trailing_update(): pl.pallas_call(update_kernel, out_shape=jax.ShapeDtypeStruct(a.shape, a.d...  10.9 us
    scatter x2, local copies, waits for them, and re-layouts, local(): current = current.at[target].set(old_top, mode='drop')  5.68 us
    gather x2, local copies, waits for them, and re-layouts, local(): current[safe_index]  4.73 us
    reshape x1, local copies, waits for them, and re-layouts, local(): return current.reshape(matrix.shape)  4.49 us
    dot_general x2, matrix products, local(): jnp.dot(panel_cols, upper_inverse[panel], preferred_element_type=jnp.floa...  4.3 us

profile of v15, /device:TPU:1, one launch (start us, length us, event | category | flops | bytes accessed | tf_op | source)
XLA Modules:
  0.0 192.0 jit_solution(5803736821325841853)
XLA Ops:
  0.0 0.8 and_select_fusion.3
  0.8 2.1 %copy.25 = bf16[128,8,4,256]{3,1,2,0:T(8,128)(2,1)S(1)} copy(bf16[128,8,4,256]{3,2,1,0:T(4,128)(2,1)} %bitcast.80) | data formatting | bytes 4194304
  2.9 0.0 copy-start.4
  2.9 1.2 gather_fusion
  4.1 0.0 copy-done.4
  4.1 0.1 squeeze.23
  4.2 0.1 squeeze.27
  4.3 0.9 broadcast_select_fusion.1
  5.2 1.3 slice_select_fusion.3
  6.5 0.4 select_n.325
  6.9 2.1 %pad_maximum_fusion.t_ref = bf16[4,2,64,1024]{3,2,1,0:T(8,128)(2,1)} fusion(bf16[4,1,64,1024]{3,2,1,0:T(8,128)(2,1)S(1)} %select_n.325, bf16[4,1,64,1024]{3,2,1,0:T(8,128)(2,1)} %broadcast_select_fusion.1), kind=kLoop, calls=%fused_computation.12 | loop fusion | flops 524288 | bytes 2097152 | tf_op jit(solution)/shard_map/stack | solution.py:371
  9.0 45.6 %shard_map.46 = bf16[4,8,16,1024]{3,2,1,0:T(8,128)(2,1)} custom-call(bf16[4,2,64,1024]{3,2,1,0:T(8,128)(2,1)} %pad_maximum_fusion.t_ref), custom_call_target="tpu_custom_call" | custom-call | tf_op jit(solution)/shard_map/pallas_call | solution.py:375
  54.6 1.3 fusion.33
  55.9 2.8 %scatter_fusion = bf16[1024,1024]{1,0:T(8,128)(2,1)S(1)} fusion(bf16[1024,1024]{1,0:T(8,128)(2,1)S(1)} %bitcast.73, s32[256]{0:T(256)S(1)} %bitcast.90, bf16[256,1024]{1,0:T(8,128)(2,1)S(1)} %bitcast.84), kind=kCustom, calls=%fused_computation.2 | custom fusion | bytes 1573888 | tf_op jit(solution)/shard_map/scatter | solution.py:593
  58.7 0.0 copy-start.3
  58.7 0.2 fusion.7.a_ref
  59.0 0.0 copy-start.2
  59.0 2.2 %fusion = bf16[1024,256]{1,0:T(8,128)(2,1)} fusion(bf16[1024,1024]{1,0:T(8,128)(2,1)S(1)} %fusion.7.a_ref, pred[]{:T(512)S(6)} %eq.77, bf16[2,256,256]{2,1,0:T(8,128)(2,1)} %param.11), kind=kOutput, calls=%fused_computation.8 | convolution fusion | flops 134742016 | bytes 1179649 | tf_op jit(solution)/shard_map/dot_general | solution.py:601
  61.2 34.0 %shard_map.47 = bf16[8,128,256]{2,1,0:T(8,128)(2,1)} custom-call(bf16[8,128,256]{2,1,0:T(8,128)(2,1)} %bitcast.89), custom_call_target="tpu_custom_call" | custom-call | tf_op jit(solution)/shard_map/pallas_call | solution.py:505
  95.1 0.0 copy-done.3
  95.2 1.1 fusion.2.u_ref
  96.3 0.1 slice.99
  96.4 0.6 fusion.29
  97.0 0.6 fusion.28
  97.6 0.0 copy-done.2
  97.6 5.5 %shard_map.48 = bf16[1024,1024]{1,0:T(8,128)(2,1)} custom-call(s32[4]{0:T(128)} %get-tuple-element.49.rf_ref, s32[4]{0:T(128)} %get-tuple-element.41.cf_ref, bf16[1024,1024]{1,0:T(8,128)(2,1)} %copy-done.2, bf16[1024,256]{1,0:T(8,128)(2,1)} %bitcast.86, bf16[256,1024]{1,0:T(8,128)(2,1)} %fusion.2.u_ref), custom_call_target="tpu_custom_call" | custom-call | tf_op jit(solution)/shard_map/pallas_call | solution.py:549
  103.0 0.0 copy-start
  103.0 3.6 %gather_fusion.1 = bf16[256,1024]{1,0:T(8,128)(2,1)S(1)} fusion(bf16[1024,1024]{1,0:T(8,128)(2,1)} %shard_map.48, s32[1024]{0:T(1024)S(1)} %pad_clamp_fusion), kind=kCustom, calls=%fused_computation.1 | custom fusion | bytes 1049600 | tf_op jit(solution)/shard_map/gather | solution.py:585
  106.6 0.1 broadcast_select_fusion
  106.7 0.0 copy-done
  106.8 1.1 pad_maximum_fusion.1.t_ref
  107.8 43.4 %shard_map.49 = bf16[4,8,16,1024]{3,2,1,0:T(8,128)(2,1)} custom-call(bf16[4,2,64,1024]{3,2,1,0:T(8,128)(2,1)} %pad_maximum_fusion.1.t_ref), custom_call_target="tpu_custom_call" | custom-call | tf_op jit(solution)/shard_map/pallas_call | solution.py:375
  151.3 1.3 fusion.32
  152.6 2.8 %scatter_fusion.1 = bf16[1024,1024]{1,0:T(8,128)(2,1)S(1)} fusion(bf16[1024,1024]{1,0:T(8,128)(2,1)S(1)} %copy-done, s32[256]{0:T(256)S(1)} %bitcast.91, bf16[256,1024]{1,0:T(8,128)(2,1)S(1)} %bitcast.83), kind=kCustom, calls=%fused_computation.3 | custom fusion | bytes 1573888 | tf_op jit(solution)/shard_map/scatter | solution.py:593
  155.5 0.2 fusion.5.a_ref
  155.7 0.0 copy-start.1
  155.7 2.1 %fusion.1 = bf16[1024,256]{1,0:T(8,128)(2,1)} fusion(bf16[1024,1024]{1,0:T(8,128)(2,1)S(1)} %fusion.5.a_ref, pred[]{:T(512)S(6)} %eq.75, bf16[2,256,256]{2,1,0:T(8,128)(2,1)} %param.11), kind=kOutput, calls=%fused_computation.9 | convolution fusion | flops 134742016 | bytes 1179649 | tf_op jit(solution)/shard_map/dot_general | solution.py:601
  157.8 23.0 %shard_map.50 = bf16[8,128,256]{2,1,0:T(8,128)(2,1)} custom-call(bf16[8,128,256]{2,1,0:T(8,128)(2,1)} %bitcast.88), custom_call_target="tpu_custom_call" | custom-call | tf_op jit(solution)/shard_map/pallas_call | solution.py:505
  180.9 1.1 fusion.3.u_ref
  182.0 0.0 copy-done.1
  182.0 5.5 %shard_map.51 = bf16[1024,1024]{1,0:T(8,128)(2,1)} custom-call(s32[4]{0:T(128)} %get-tuple-element.51.rf_ref, s32[4]{0:T(128)} %get-tuple-element.50.cf_ref, bf16[1024,1024]{1,0:T(8,128)(2,1)} %copy-done.1, bf16[1024,256]{1,0:T(8,128)(2,1)} %bitcast.87, bf16[256,1024]{1,0:T(8,128)(2,1)} %fusion.3.u_ref), custom_call_target="tpu_custom_call" | custom-call | tf_op jit(solution)/shard_map/pallas_call | solution.py:549
  187.5 4.5 %reshape.562 = bf16[4,256,4,256]{3,2,1,0:T(4,128)(2,1)} reshape(bf16[1024,1024]{1,0:T(8,128)(2,1)} %shard_map.51) | data formatting | bytes 4194304 | tf_op jit(solution)/shard_map/reshape | solution.py:619
  (9 shorter events, 0.1 us)
Async XLA Ops:
  2.9 1.2 copy-start.4
  58.7 36.4 %copy-start.3 = (bf16[2,256,256]{2,1,0:T(8,128)(2,1)S(1)}, bf16[2,256,256]{2,1,0:T(8,128)(2,1)}, u32[]{:S(2)}) copy-start(bf16[2,256,256]{2,1,0:T(8,128)(2,1)} %param.10) | copy-start | bytes 786436
  59.0 38.6 %copy-start.2 = (bf16[1024,1024]{1,0:T(8,128)(2,1)}, bf16[1024,1024]{1,0:T(8,128)(2,1)S(1)}, u32[]{:S(2)}) copy-start(bf16[1024,1024]{1,0:T(8,128)(2,1)S(1)} %fusion.7.a_ref) | copy-start | bytes 6291460
  103.0 3.7 %copy-start = (bf16[1024,1024]{1,0:T(8,128)(2,1)S(1)}, bf16[1024,1024]{1,0:T(8,128)(2,1)}, u32[]{:S(2)}) copy-start(bf16[1024,1024]{1,0:T(8,128)(2,1)} %shard_map.48) | copy-start | bytes 6291460
  155.7 26.3 %copy-start.1 = (bf16[1024,1024]{1,0:T(8,128)(2,1)}, bf16[1024,1024]{1,0:T(8,128)(2,1)S(1)}, u32[]{:S(2)}) copy-start(bf16[1024,1024]{1,0:T(8,128)(2,1)S(1)} %fusion.5.a_ref) | copy-start | bytes 6291460

commit v16 on v15

--- a/solution.py
+++ b/solution.py
@@ -522,43 +522,37 @@
 
 
 def update_kernel(rf_ref, cf_ref, a_ref, l_ref, u_ref, o_ref):
-    rb = rf_ref[pl.program_id(0)]
-    below = (rb & 1) == 1
-    in_top = (rb & 2) == 2
-    lower = l_ref[...]
-    block = lower.shape[1]
-    for c in range(a_ref.shape[1] // block):
-        cols = slice(c * block, (c + 1) * block)
-        cb = cf_ref[c]
-        right = (cb & 1) == 1
-        in_panel = (cb & 2) == 2
-        a = a_ref[:, cols]
-        upper = u_ref[:, cols]
-        product = jnp.dot(lower, upper, preferred_element_type=jnp.float32)
-        changed = (a.astype(jnp.float32) - product).astype(a.dtype)
-        o_ref[:, cols] = jnp.where(
-            below & right,
-            changed,
-            jnp.where(in_panel & below, lower, jnp.where(in_top & right, upper, a)),
-        )
+    block = l_ref.shape[1]
+    for r in range(a_ref.shape[0] // block):
+        rows = slice(r * block, (r + 1) * block)
+        rb = rf_ref[r]
+        below = (rb & 1) == 1
+        in_top = (rb & 2) == 2
+        lower = l_ref[rows, :]
+        for c in range(a_ref.shape[1] // block):
+            cols = slice(c * block, (c + 1) * block)
+            cb = cf_ref[c]
+            right = (cb & 1) == 1
+            in_panel = (cb & 2) == 2
+            a = a_ref[rows, cols]
+            upper = u_ref[:, cols]
+            product = jnp.dot(lower, upper, preferred_element_type=jnp.float32)
+            changed = (a.astype(jnp.float32) - product).astype(a.dtype)
+            o_ref[rows, cols] = jnp.where(
+                below & right,
+                changed,
+                jnp.where(in_panel & below, lower, jnp.where(in_top & right, upper, a)),
+            )
 
 
 def trailing_update(a, lower, upper, row_flags, col_flags):
-    rows, cols = a.shape
-    block = upper.shape[0]
+    smem = pl.BlockSpec(memory_space=pltpu.SMEM)
+    vmem = pl.BlockSpec(memory_space=pltpu.VMEM)
     return pl.pallas_call(
         update_kernel,
         out_shape=jax.ShapeDtypeStruct(a.shape, a.dtype),
-        grid_spec=pltpu.PrefetchScalarGridSpec(
-            num_scalar_prefetch=2,
-            grid=(rows // block,),
-            in_specs=[
-                pl.BlockSpec((block, cols), lambda i, rf, cf: (i, 0)),
-                pl.BlockSpec((block, block), lambda i, rf, cf: (i, 0)),
-                pl.BlockSpec((block, cols), lambda i, rf, cf: (0, 0)),
-            ],
-            out_specs=pl.BlockSpec((block, cols), lambda i, rf, cf: (i, 0)),
-        ),
+        in_specs=[smem, smem, vmem, vmem, vmem],
+        out_specs=vmem,
     )(row_flags, col_flags, a, lower, upper)
 
 

time: 193 us -> 190 us (0.984)
  Pallas kernels: 157 us -> 154 us
    pallas_call x2, Pallas kernels: 10.9 us -> 8.35 us  [trailing_update(): pl.pallas_call(update_kernel, out_shape=jax.ShapeDtypeStruct(a.shape, a.d...]
where the time goes in v16:
time: 190 us; the launch traced here: 189 us
  Pallas kernels  154 us (81%)
  local copies, waits for them, and re-layouts  20.3 us (11%)
  other arithmetic  7.94 us (4%)
  matrix products  6.53 us (3%)
    pallas_call x2, Pallas kernels, prow_sum(): pl.pallas_call(functools.partial(prow_kernel, xd, yd, top), out_shape=jax...  89.1 us
    pallas_call x2, Pallas kernels, pcol_bcast(): pl.pallas_call(functools.partial(pcol_kernel, nz, source), out_shape=jax....  57 us
    pallas_call x2, Pallas kernels, trailing_update(): pl.pallas_call(update_kernel, out_shape=jax.ShapeDtypeStruct(a.shape, a.d...  8.35 us
    scatter x2, local copies, waits for them, and re-layouts, local(): current = current.at[target].set(old_top, mode='drop')  5.68 us
    gather x2, local copies, waits for them, and re-layouts, local(): current[safe_index]  4.74 us
    reshape x1, local copies, waits for them, and re-layouts, local(): return current.reshape(matrix.shape)  4.49 us
    dot_general x2, matrix products, local(): jnp.dot(panel_cols, upper_inverse[panel], preferred_element_type=jnp.floa...  4.3 us

profile of v16, /device:TPU:1, one launch (start us, length us, event | category | flops | bytes accessed | tf_op | source)
XLA Modules:
  0.0 189.5 jit_solution(1106811283642601634)
XLA Ops:
  0.0 0.8 and_select_fusion.3
  0.8 2.1 %copy.25 = bf16[128,8,4,256]{3,1,2,0:T(8,128)(2,1)S(1)} copy(bf16[128,8,4,256]{3,2,1,0:T(4,128)(2,1)} %bitcast.80) | data formatting | bytes 4194304
  2.9 0.0 copy-start.4
  2.9 1.2 gather_fusion
  4.1 0.0 copy-done.4
  4.1 0.1 squeeze.23
  4.2 0.1 squeeze.27
  4.3 0.9 broadcast_select_fusion.1
  5.2 1.3 slice_select_fusion.3
  6.5 0.4 select_n.325
  6.9 2.1 %pad_maximum_fusion.t_ref = bf16[4,2,64,1024]{3,2,1,0:T(8,128)(2,1)} fusion(bf16[4,1,64,1024]{3,2,1,0:T(8,128)(2,1)S(1)} %select_n.325, bf16[4,1,64,1024]{3,2,1,0:T(8,128)(2,1)} %broadcast_select_fusion.1), kind=kLoop, calls=%fused_computation.12 | loop fusion | flops 524288 | bytes 2097152 | tf_op jit(solution)/shard_map/stack | solution.py:371
  9.0 45.6 %shard_map.46 = bf16[4,8,16,1024]{3,2,1,0:T(8,128)(2,1)} custom-call(bf16[4,2,64,1024]{3,2,1,0:T(8,128)(2,1)} %pad_maximum_fusion.t_ref), custom_call_target="tpu_custom_call" | custom-call | tf_op jit(solution)/shard_map/pallas_call | solution.py:375
  54.6 1.3 fusion.33
  55.9 2.8 %scatter_fusion = bf16[1024,1024]{1,0:T(8,128)(2,1)S(1)} fusion(bf16[1024,1024]{1,0:T(8,128)(2,1)S(1)} %bitcast.73, s32[256]{0:T(256)S(1)} %bitcast.90, bf16[256,1024]{1,0:T(8,128)(2,1)S(1)} %bitcast.84), kind=kCustom, calls=%fused_computation.2 | custom fusion | bytes 1573888 | tf_op jit(solution)/shard_map/scatter | solution.py:587
  58.7 0.0 copy-start.3
  58.7 0.2 fusion.7.a_ref
  59.0 0.0 copy-start.2
  59.0 2.2 %fusion = bf16[1024,256]{1,0:T(8,128)(2,1)} fusion(bf16[1024,1024]{1,0:T(8,128)(2,1)S(1)} %fusion.7.a_ref, pred[]{:T(512)S(6)} %eq.77, bf16[2,256,256]{2,1,0:T(8,128)(2,1)} %param.11), kind=kOutput, calls=%fused_computation.8 | convolution fusion | flops 134742016 | bytes 1179649 | tf_op jit(solution)/shard_map/dot_general | solution.py:595
  61.2 34.0 %shard_map.47 = bf16[8,128,256]{2,1,0:T(8,128)(2,1)} custom-call(bf16[8,128,256]{2,1,0:T(8,128)(2,1)} %bitcast.89), custom_call_target="tpu_custom_call" | custom-call | tf_op jit(solution)/shard_map/pallas_call | solution.py:505
  95.1 0.0 copy-done.3
  95.2 1.1 fusion.2.u_ref
  96.3 0.1 slice.99
  96.4 0.6 fusion.29
  97.0 0.6 fusion.28
  97.6 0.0 copy-done.2
  97.6 4.2 %shard_map.48 = bf16[1024,1024]{1,0:T(8,128)(2,1)} custom-call(s32[4]{0:T(128)} %get-tuple-element.49.rf_ref, s32[4]{0:T(128)} %get-tuple-element.41.cf_ref, bf16[1024,1024]{1,0:T(8,128)(2,1)} %copy-done.2, bf16[1024,256]{1,0:T(8,128)(2,1)} %bitcast.86, bf16[256,1024]{1,0:T(8,128)(2,1)} %fusion.2.u_ref), custom_call_target="tpu_custom_call" | custom-call | tf_op jit(solution)/shard_map/pallas_call | solution.py:551
  101.7 0.0 copy-start
  101.7 3.6 %gather_fusion.1 = bf16[256,1024]{1,0:T(8,128)(2,1)S(1)} fusion(bf16[1024,1024]{1,0:T(8,128)(2,1)} %shard_map.48, s32[1024]{0:T(1024)S(1)} %pad_clamp_fusion), kind=kCustom, calls=%fused_computation.1 | custom fusion | bytes 1049600 | tf_op jit(solution)/shard_map/gather | solution.py:579
  105.3 0.1 broadcast_select_fusion
  105.4 0.0 copy-done
  105.5 1.1 pad_maximum_fusion.1.t_ref
  106.6 43.5 %shard_map.49 = bf16[4,8,16,1024]{3,2,1,0:T(8,128)(2,1)} custom-call(bf16[4,2,64,1024]{3,2,1,0:T(8,128)(2,1)} %pad_maximum_fusion.1.t_ref), custom_call_target="tpu_custom_call" | custom-call | tf_op jit(solution)/shard_map/pallas_call | solution.py:375
  150.1 1.3 fusion.32
  151.4 2.8 %scatter_fusion.1 = bf16[1024,1024]{1,0:T(8,128)(2,1)S(1)} fusion(bf16[1024,1024]{1,0:T(8,128)(2,1)S(1)} %copy-done, s32[256]{0:T(256)S(1)} %bitcast.91, bf16[256,1024]{1,0:T(8,128)(2,1)S(1)} %bitcast.83), kind=kCustom, calls=%fused_computation.3 | custom fusion | bytes 1573888 | tf_op jit(solution)/shard_map/scatter | solution.py:587
  154.2 0.2 fusion.5.a_ref
  154.5 0.0 copy-start.1
  154.5 2.1 %fusion.1 = bf16[1024,256]{1,0:T(8,128)(2,1)} fusion(bf16[1024,1024]{1,0:T(8,128)(2,1)S(1)} %fusion.5.a_ref, pred[]{:T(512)S(6)} %eq.75, bf16[2,256,256]{2,1,0:T(8,128)(2,1)} %param.11), kind=kOutput, calls=%fused_computation.9 | convolution fusion | flops 134742016 | bytes 1179649 | tf_op jit(solution)/shard_map/dot_general | solution.py:595
  156.6 23.1 %shard_map.50 = bf16[8,128,256]{2,1,0:T(8,128)(2,1)} custom-call(bf16[8,128,256]{2,1,0:T(8,128)(2,1)} %bitcast.88), custom_call_target="tpu_custom_call" | custom-call | tf_op jit(solution)/shard_map/pallas_call | solution.py:505
  179.7 1.1 fusion.3.u_ref
  180.8 0.0 copy-done.1
  180.8 4.2 %shard_map.51 = bf16[1024,1024]{1,0:T(8,128)(2,1)} custom-call(s32[4]{0:T(128)} %get-tuple-element.51.rf_ref, s32[4]{0:T(128)} %get-tuple-element.50.cf_ref, bf16[1024,1024]{1,0:T(8,128)(2,1)} %copy-done.1, bf16[1024,256]{1,0:T(8,128)(2,1)} %bitcast.87, bf16[256,1024]{1,0:T(8,128)(2,1)} %fusion.3.u_ref), custom_call_target="tpu_custom_call" | custom-call | tf_op jit(solution)/shard_map/pallas_call | solution.py:551
  185.0 4.5 %reshape.562 = bf16[4,256,4,256]{3,2,1,0:T(4,128)(2,1)} reshape(bf16[1024,1024]{1,0:T(8,128)(2,1)} %shard_map.51) | data formatting | bytes 4194304 | tf_op jit(solution)/shard_map/reshape | solution.py:613
  (9 shorter events, 0.1 us)
Async XLA Ops:
  2.9 1.2 copy-start.4
  58.7 36.4 %copy-start.3 = (bf16[2,256,256]{2,1,0:T(8,128)(2,1)S(1)}, bf16[2,256,256]{2,1,0:T(8,128)(2,1)}, u32[]{:S(2)}) copy-start(bf16[2,256,256]{2,1,0:T(8,128)(2,1)} %param.10) | copy-start | bytes 786436
  59.0 38.6 %copy-start.2 = (bf16[1024,1024]{1,0:T(8,128)(2,1)}, bf16[1024,1024]{1,0:T(8,128)(2,1)S(1)}, u32[]{:S(2)}) copy-start(bf16[1024,1024]{1,0:T(8,128)(2,1)S(1)} %fusion.7.a_ref) | copy-start | bytes 6291460
  101.7 3.7 %copy-start = (bf16[1024,1024]{1,0:T(8,128)(2,1)S(1)}, bf16[1024,1024]{1,0:T(8,128)(2,1)}, u32[]{:S(2)}) copy-start(bf16[1024,1024]{1,0:T(8,128)(2,1)} %shard_map.48) | copy-start | bytes 6291460
  154.5 26.3 %copy-start.1 = (bf16[1024,1024]{1,0:T(8,128)(2,1)}, bf16[1024,1024]{1,0:T(8,128)(2,1)S(1)}, u32[]{:S(2)}) copy-start(bf16[1024,1024]{1,0:T(8,128)(2,1)S(1)} %fusion.5.a_ref) | copy-start | bytes 6291460

commit v17 on v16

--- a/solution.py
+++ b/solution.py
@@ -521,7 +521,7 @@
     return out.reshape(rows, cols)
 
 
-def update_kernel(rf_ref, cf_ref, a_ref, l_ref, u_ref, o_ref):
+def update_kernel(four, rf_ref, cf_ref, a_ref, l_ref, u_ref, o_ref):
     block = l_ref.shape[1]
     for r in range(a_ref.shape[0] // block):
         rows = slice(r * block, (r + 1) * block)
@@ -538,19 +538,23 @@
             upper = u_ref[:, cols]
             product = jnp.dot(lower, upper, preferred_element_type=jnp.float32)
             changed = (a.astype(jnp.float32) - product).astype(a.dtype)
-            o_ref[rows, cols] = jnp.where(
+            result = jnp.where(
                 below & right,
                 changed,
                 jnp.where(in_panel & below, lower, jnp.where(in_top & right, upper, a)),
             )
-
-
-def trailing_update(a, lower, upper, row_flags, col_flags):
+            if four:
+                o_ref[r, :, c, :] = result
+            else:
+                o_ref[rows, cols] = result
+
+
+def trailing_update(a, lower, upper, row_flags, col_flags, out_shape=None):
     smem = pl.BlockSpec(memory_space=pltpu.SMEM)
     vmem = pl.BlockSpec(memory_space=pltpu.VMEM)
     return pl.pallas_call(
-        update_kernel,
-        out_shape=jax.ShapeDtypeStruct(a.shape, a.dtype),
+        functools.partial(update_kernel, out_shape is not None),
+        out_shape=jax.ShapeDtypeStruct(out_shape or a.shape, a.dtype),
         in_specs=[smem, smem, vmem, vmem, vmem],
         out_specs=vmem,
     )(row_flags, col_flags, a, lower, upper)
@@ -609,7 +613,11 @@
         right = (col_blocks * col_count + my_col >= panel + 1).astype(jnp.int32)
         in_top = (is_top & (row_blocks == top_first // block)).astype(jnp.int32)
         in_panel = (is_panel & (col_blocks == panel_first // block)).astype(jnp.int32)
-        current = trailing_update(current, lower, upper, below + 2 * in_top, right + 2 * in_panel)
+        last = panel == pivots.shape[0] - 1
+        current = trailing_update(
+            current, lower, upper, below + 2 * in_top, right + 2 * in_panel,
+            matrix.shape if last else None,
+        )
     return current.reshape(matrix.shape)
 
 

time: 190 us -> 189 us (level)
  local copies, waits for them, and re-layouts: 20.3 us -> 16 us
  Pallas kernels: 154 us -> 157 us
    reshape x1 -> x0, local copies, waits for them, and re-layouts: 4.49 us -> none  [local(): return current.reshape(matrix.shape)]
    pallas_call x2, Pallas kernels: 8.35 us -> 11 us  [trailing_update(): pl.pallas_call(functools.partial(update_kernel, out_shape is not None), o...]
where the time goes in v17:
time: 189 us; the launch traced here: 188 us
  Pallas kernels  157 us (83%)
  local copies, waits for them, and re-layouts  16 us (8%)
  other arithmetic  7.94 us (4%)
  matrix products  6.57 us (3%)
    pallas_call x2, Pallas kernels, prow_sum(): pl.pallas_call(functools.partial(prow_kernel, xd, yd, top), out_shape=jax...  89.2 us
    pallas_call x2, Pallas kernels, pcol_bcast(): pl.pallas_call(functools.partial(pcol_kernel, nz, source), out_shape=jax....  56.9 us
    pallas_call x2, Pallas kernels, trailing_update(): pl.pallas_call(functools.partial(update_kernel, out_shape is not None), o...  11 us
    scatter x2, local copies, waits for them, and re-layouts, local(): current = current.at[target].set(old_top, mode='drop')  5.86 us
    gather x2, local copies, waits for them, and re-layouts, local(): current[safe_index]  4.74 us
    dot_general x2, matrix products, local(): jnp.dot(panel_cols, upper_inverse[panel], preferred_element_type=jnp.floa...  4.34 us

profile of v17, /device:TPU:1, one launch (start us, length us, event | category | flops | bytes accessed | tf_op | source)
XLA Modules:
  0.0 187.9 jit_solution(17371267567538078429)
XLA Ops:
  0.0 0.8 and_select_fusion.3
  0.8 2.1 %copy.25 = bf16[128,8,4,256]{3,1,2,0:T(8,128)(2,1)S(1)} copy(bf16[128,8,4,256]{3,2,1,0:T(4,128)(2,1)} %bitcast.80) | data formatting | bytes 4194304
  2.9 0.0 copy-start.4
  2.9 1.2 gather_fusion
  4.1 0.0 copy-done.4
  4.1 0.1 squeeze.23
  4.2 0.1 squeeze.27
  4.3 0.9 broadcast_select_fusion.1
  5.2 1.3 slice_select_fusion.3
  6.5 0.4 select_n.325
  6.9 2.1 %pad_maximum_fusion.t_ref = bf16[4,2,64,1024]{3,2,1,0:T(8,128)(2,1)} fusion(bf16[4,1,64,1024]{3,2,1,0:T(8,128)(2,1)S(1)} %select_n.325, bf16[4,1,64,1024]{3,2,1,0:T(8,128)(2,1)} %broadcast_select_fusion.1), kind=kLoop, calls=%fused_computation.12 | loop fusion | flops 524288 | bytes 2097152 | tf_op jit(solution)/shard_map/stack | solution.py:371
  9.0 45.6 %shard_map.46 = bf16[4,8,16,1024]{3,2,1,0:T(8,128)(2,1)} custom-call(bf16[4,2,64,1024]{3,2,1,0:T(8,128)(2,1)} %pad_maximum_fusion.t_ref), custom_call_target="tpu_custom_call" | custom-call | tf_op jit(solution)/shard_map/pallas_call | solution.py:375
  54.6 1.3 fusion.33
  55.9 2.8 %scatter_fusion = bf16[1024,1024]{1,0:T(8,128)(2,1)S(1)} fusion(bf16[1024,1024]{1,0:T(8,128)(2,1)S(1)} %bitcast.73, s32[256]{0:T(256)S(1)} %bitcast.90, bf16[256,1024]{1,0:T(8,128)(2,1)S(1)} %bitcast.84), kind=kCustom, calls=%fused_computation.2 | custom fusion | bytes 1573888 | tf_op jit(solution)/shard_map/scatter | solution.py:591
  58.7 0.0 copy-start.3
  58.7 0.2 fusion.7.a_ref
  59.0 0.0 copy-start.2
  59.0 2.2 %fusion = bf16[1024,256]{1,0:T(8,128)(2,1)} fusion(bf16[1024,1024]{1,0:T(8,128)(2,1)S(1)} %fusion.7.a_ref, pred[]{:T(512)S(6)} %eq.77, bf16[2,256,256]{2,1,0:T(8,128)(2,1)} %param.11), kind=kOutput, calls=%fused_computation.8 | convolution fusion | flops 134742016 | bytes 1179649 | tf_op jit(solution)/shard_map/dot_general | solution.py:599
  61.2 33.9 %shard_map.47 = bf16[8,128,256]{2,1,0:T(8,128)(2,1)} custom-call(bf16[8,128,256]{2,1,0:T(8,128)(2,1)} %bitcast.89), custom_call_target="tpu_custom_call" | custom-call | tf_op jit(solution)/shard_map/pallas_call | solution.py:505
  95.1 0.0 copy-done.3
  95.1 1.1 fusion.2.u_ref
  96.3 0.1 slice.99
  96.4 0.6 fusion.29
  97.0 0.6 fusion.28
  97.5 0.0 copy-done.2
  97.5 4.2 %shard_map.48 = bf16[1024,1024]{1,0:T(8,128)(2,1)} custom-call(s32[4]{0:T(128)} %get-tuple-element.49.rf_ref, s32[4]{0:T(128)} %get-tuple-element.41.cf_ref, bf16[1024,1024]{1,0:T(8,128)(2,1)} %copy-done.2, bf16[1024,256]{1,0:T(8,128)(2,1)} %bitcast.86, bf16[256,1024]{1,0:T(8,128)(2,1)} %fusion.2.u_ref), custom_call_target="tpu_custom_call" | custom-call | tf_op jit(solution)/shard_map/pallas_call | solution.py:555
  101.7 0.0 copy-start
  101.7 3.6 %gather_fusion.1 = bf16[256,1024]{1,0:T(8,128)(2,1)S(1)} fusion(bf16[1024,1024]{1,0:T(8,128)(2,1)} %shard_map.48, s32[1024]{0:T(1024)S(1)} %pad_clamp_fusion), kind=kCustom, calls=%fused_computation.1 | custom fusion | bytes 1049600 | tf_op jit(solution)/shard_map/gather | solution.py:583
  105.3 0.1 broadcast_select_fusion
  105.4 0.0 copy-done
  105.5 1.1 pad_maximum_fusion.1.t_ref
  106.5 43.6 %shard_map.49 = bf16[4,8,16,1024]{3,2,1,0:T(8,128)(2,1)} custom-call(bf16[4,2,64,1024]{3,2,1,0:T(8,128)(2,1)} %pad_maximum_fusion.1.t_ref), custom_call_target="tpu_custom_call" | custom-call | tf_op jit(solution)/shard_map/pallas_call | solution.py:375
  150.2 1.3 fusion.32
  151.5 3.0 %scatter_fusion.1 = bf16[1024,1024]{1,0:T(8,128)(2,1)S(1)} fusion(bf16[1024,1024]{1,0:T(8,128)(2,1)S(1)} %copy-done, s32[256]{0:T(256)S(1)} %bitcast.91, bf16[256,1024]{1,0:T(8,128)(2,1)S(1)} %bitcast.83), kind=kCustom, calls=%fused_computation.3 | custom fusion | bytes 1573888 | tf_op jit(solution)/shard_map/scatter | solution.py:591
  154.5 0.2 fusion.5.a_ref
  154.8 0.0 copy-start.1
  154.8 2.1 %fusion.1 = bf16[1024,256]{1,0:T(8,128)(2,1)} fusion(bf16[1024,1024]{1,0:T(8,128)(2,1)S(1)} %fusion.5.a_ref, pred[]{:T(512)S(6)} %eq.75, bf16[2,256,256]{2,1,0:T(8,128)(2,1)} %param.11), kind=kOutput, calls=%fused_computation.9 | convolution fusion | flops 134742016 | bytes 1179649 | tf_op jit(solution)/shard_map/dot_general | solution.py:599
  156.9 23.0 %shard_map.50 = bf16[8,128,256]{2,1,0:T(8,128)(2,1)} custom-call(bf16[8,128,256]{2,1,0:T(8,128)(2,1)} %bitcast.88), custom_call_target="tpu_custom_call" | custom-call | tf_op jit(solution)/shard_map/pallas_call | solution.py:505
  179.9 1.1 fusion.3.u_ref
  181.0 0.0 copy-done.1
  181.0 6.8 %shard_map.51 = bf16[4,256,4,256]{3,2,1,0:T(4,128)(2,1)} custom-call(s32[4]{0:T(128)} %get-tuple-element.51.rf_ref, s32[4]{0:T(128)} %get-tuple-element.50.cf_ref, bf16[1024,1024]{1,0:T(8,128)(2,1)} %copy-done.1, bf16[1024,256]{1,0:T(8,128)(2,1)} %bitcast.87, bf16[256,1024]{1,0:T(8,128)(2,1)} %fusion.3.u_ref), custom_call_target="tpu_custom_call" | custom-call | tf_op jit(solution)/shard_map/pallas_call | solution.py:555
  (9 shorter events, 0.1 us)
Async XLA Ops:
  2.9 1.2 copy-start.4
  58.7 36.4 %copy-start.3 = (bf16[2,256,256]{2,1,0:T(8,128)(2,1)S(1)}, bf16[2,256,256]{2,1,0:T(8,128)(2,1)}, u32[]{:S(2)}) copy-start(bf16[2,256,256]{2,1,0:T(8,128)(2,1)} %param.10) | copy-start | bytes 786436
  59.0 38.6 %copy-start.2 = (bf16[1024,1024]{1,0:T(8,128)(2,1)}, bf16[1024,1024]{1,0:T(8,128)(2,1)S(1)}, u32[]{:S(2)}) copy-start(bf16[1024,1024]{1,0:T(8,128)(2,1)S(1)} %fusion.7.a_ref) | copy-start | bytes 6291460
  101.7 3.7 %copy-start = (bf16[1024,1024]{1,0:T(8,128)(2,1)S(1)}, bf16[1024,1024]{1,0:T(8,128)(2,1)}, u32[]{:S(2)}) copy-start(bf16[1024,1024]{1,0:T(8,128)(2,1)} %shard_map.48) | copy-start | bytes 6291460
  154.8 26.3 %copy-start.1 = (bf16[1024,1024]{1,0:T(8,128)(2,1)}, bf16[1024,1024]{1,0:T(8,128)(2,1)S(1)}, u32[]{:S(2)}) copy-start(bf16[1024,1024]{1,0:T(8,128)(2,1)S(1)} %fusion.5.a_ref) | copy-start | bytes 6291460

commit v18 on v17

--- a/solution.py
+++ b/solution.py
@@ -529,6 +529,7 @@
         below = (rb & 1) == 1
         in_top = (rb & 2) == 2
         lower = l_ref[rows, :]
+        results = []
         for c in range(a_ref.shape[1] // block):
             cols = slice(c * block, (c + 1) * block)
             cb = cf_ref[c]
@@ -544,9 +545,11 @@
                 jnp.where(in_panel & below, lower, jnp.where(in_top & right, upper, a)),
             )
             if four:
-                o_ref[r, :, c, :] = result
+                results.append(result)
             else:
                 o_ref[rows, cols] = result
+        if four:
+            o_ref[r] = jnp.stack(results, axis=1)
 
 
 def trailing_update(a, lower, upper, row_flags, col_flags, out_shape=None):

time: 189 us -> 190 us (level)
  no operation moved by 1% of the time
where the time goes in v18:
time: 190 us; the launch traced here: 189 us
  Pallas kernels  158 us (83%)
  local copies, waits for them, and re-layouts  16 us (8%)
  other arithmetic  7.94 us (4%)
  matrix products  6.57 us (3%)
    pallas_call x2, Pallas kernels, prow_sum(): pl.pallas_call(functools.partial(prow_kernel, xd, yd, top), out_shape=jax...  89.2 us
    pallas_call x2, Pallas kernels, pcol_bcast(): pl.pallas_call(functools.partial(pcol_kernel, nz, source), out_shape=jax....  56.9 us
    pallas_call x2, Pallas kernels, trailing_update(): pl.pallas_call(functools.partial(update_kernel, out_shape is not None), o...  12 us
    scatter x2, local copies, waits for them, and re-layouts, local(): current = current.at[target].set(old_top, mode='drop')  5.86 us
    gather x2, local copies, waits for them, and re-layouts, local(): current[safe_index]  4.74 us
    dot_general x2, matrix products, local(): jnp.dot(panel_cols, upper_inverse[panel], preferred_element_type=jnp.floa...  4.34 us

profile of v18, /device:TPU:1, one launch (start us, length us, event | category | flops | bytes accessed | tf_op | source)
XLA Modules:
  0.0 188.9 jit_solution(14724826986404693305)
XLA Ops:
  0.0 0.8 and_select_fusion.3
  0.8 2.1 %copy.25 = bf16[128,8,4,256]{3,1,2,0:T(8,128)(2,1)S(1)} copy(bf16[128,8,4,256]{3,2,1,0:T(4,128)(2,1)} %bitcast.80) | data formatting | bytes 4194304
  2.9 0.0 copy-start.4
  2.9 1.2 gather_fusion
  4.1 0.0 copy-done.4
  4.1 0.1 squeeze.23
  4.2 0.1 squeeze.27
  4.3 0.9 broadcast_select_fusion.1
  5.2 1.3 slice_select_fusion.3
  6.5 0.4 select_n.325
  6.9 2.1 %pad_maximum_fusion.t_ref = bf16[4,2,64,1024]{3,2,1,0:T(8,128)(2,1)} fusion(bf16[4,1,64,1024]{3,2,1,0:T(8,128)(2,1)S(1)} %select_n.325, bf16[4,1,64,1024]{3,2,1,0:T(8,128)(2,1)} %broadcast_select_fusion.1), kind=kLoop, calls=%fused_computation.12 | loop fusion | flops 524288 | bytes 2097152 | tf_op jit(solution)/shard_map/stack | solution.py:371
  9.0 45.6 %shard_map.46 = bf16[4,8,16,1024]{3,2,1,0:T(8,128)(2,1)} custom-call(bf16[4,2,64,1024]{3,2,1,0:T(8,128)(2,1)} %pad_maximum_fusion.t_ref), custom_call_target="tpu_custom_call" | custom-call | tf_op jit(solution)/shard_map/pallas_call | solution.py:375
  54.6 1.3 fusion.33
  55.9 2.8 %scatter_fusion = bf16[1024,1024]{1,0:T(8,128)(2,1)S(1)} fusion(bf16[1024,1024]{1,0:T(8,128)(2,1)S(1)} %bitcast.73, s32[256]{0:T(256)S(1)} %bitcast.90, bf16[256,1024]{1,0:T(8,128)(2,1)S(1)} %bitcast.84), kind=kCustom, calls=%fused_computation.2 | custom fusion | bytes 1573888 | tf_op jit(solution)/shard_map/scatter | solution.py:594
  58.7 0.0 copy-start.3
  58.7 0.2 fusion.7.a_ref
  59.0 0.0 copy-start.2
  59.0 2.2 %fusion = bf16[1024,256]{1,0:T(8,128)(2,1)} fusion(bf16[1024,1024]{1,0:T(8,128)(2,1)S(1)} %fusion.7.a_ref, pred[]{:T(512)S(6)} %eq.77, bf16[2,256,256]{2,1,0:T(8,128)(2,1)} %param.11), kind=kOutput, calls=%fused_computation.8 | convolution fusion | flops 134742016 | bytes 1179649 | tf_op jit(solution)/shard_map/dot_general | solution.py:602
  61.2 33.9 %shard_map.47 = bf16[8,128,256]{2,1,0:T(8,128)(2,1)} custom-call(bf16[8,128,256]{2,1,0:T(8,128)(2,1)} %bitcast.89), custom_call_target="tpu_custom_call" | custom-call | tf_op jit(solution)/shard_map/pallas_call | solution.py:505
  95.1 0.0 copy-done.3
  95.1 1.1 fusion.2.u_ref
  96.3 0.1 slice.99
  96.4 0.6 fusion.29
  97.0 0.6 fusion.28
  97.5 0.0 copy-done.2
  97.5 4.2 %shard_map.48 = bf16[1024,1024]{1,0:T(8,128)(2,1)} custom-call(s32[4]{0:T(128)} %get-tuple-element.49.rf_ref, s32[4]{0:T(128)} %get-tuple-element.41.cf_ref, bf16[1024,1024]{1,0:T(8,128)(2,1)} %copy-done.2, bf16[1024,256]{1,0:T(8,128)(2,1)} %bitcast.86, bf16[256,1024]{1,0:T(8,128)(2,1)} %fusion.2.u_ref), custom_call_target="tpu_custom_call" | custom-call | tf_op jit(solution)/shard_map/pallas_call | solution.py:558
  101.7 0.0 copy-start
  101.7 3.6 %gather_fusion.1 = bf16[256,1024]{1,0:T(8,128)(2,1)S(1)} fusion(bf16[1024,1024]{1,0:T(8,128)(2,1)} %shard_map.48, s32[1024]{0:T(1024)S(1)} %pad_clamp_fusion), kind=kCustom, calls=%fused_computation.1 | custom fusion | bytes 1049600 | tf_op jit(solution)/shard_map/gather | solution.py:586
  105.3 0.1 broadcast_select_fusion
  105.4 0.0 copy-done
  105.5 1.1 pad_maximum_fusion.1.t_ref
  106.5 43.6 %shard_map.49 = bf16[4,8,16,1024]{3,2,1,0:T(8,128)(2,1)} custom-call(bf16[4,2,64,1024]{3,2,1,0:T(8,128)(2,1)} %pad_maximum_fusion.1.t_ref), custom_call_target="tpu_custom_call" | custom-call | tf_op jit(solution)/shard_map/pallas_call | solution.py:375
  150.2 1.3 fusion.32
  151.5 3.0 %scatter_fusion.1 = bf16[1024,1024]{1,0:T(8,128)(2,1)S(1)} fusion(bf16[1024,1024]{1,0:T(8,128)(2,1)S(1)} %copy-done, s32[256]{0:T(256)S(1)} %bitcast.91, bf16[256,1024]{1,0:T(8,128)(2,1)S(1)} %bitcast.83), kind=kCustom, calls=%fused_computation.3 | custom fusion | bytes 1573888 | tf_op jit(solution)/shard_map/scatter | solution.py:594
  154.5 0.2 fusion.5.a_ref
  154.8 0.0 copy-start.1
  154.8 2.1 %fusion.1 = bf16[1024,256]{1,0:T(8,128)(2,1)} fusion(bf16[1024,1024]{1,0:T(8,128)(2,1)S(1)} %fusion.5.a_ref, pred[]{:T(512)S(6)} %eq.75, bf16[2,256,256]{2,1,0:T(8,128)(2,1)} %param.11), kind=kOutput, calls=%fused_computation.9 | convolution fusion | flops 134742016 | bytes 1179649 | tf_op jit(solution)/shard_map/dot_general | solution.py:602
  156.9 23.0 %shard_map.50 = bf16[8,128,256]{2,1,0:T(8,128)(2,1)} custom-call(bf16[8,128,256]{2,1,0:T(8,128)(2,1)} %bitcast.88), custom_call_target="tpu_custom_call" | custom-call | tf_op jit(solution)/shard_map/pallas_call | solution.py:505
  179.9 1.1 fusion.3.u_ref
  181.0 0.0 copy-done.1
  181.0 7.9 %shard_map.51 = bf16[4,256,4,256]{3,2,1,0:T(4,128)(2,1)} custom-call(s32[4]{0:T(128)} %get-tuple-element.51.rf_ref, s32[4]{0:T(128)} %get-tuple-element.50.cf_ref, bf16[1024,1024]{1,0:T(8,128)(2,1)} %copy-done.1, bf16[1024,256]{1,0:T(8,128)(2,1)} %bitcast.87, bf16[256,1024]{1,0:T(8,128)(2,1)} %fusion.3.u_ref), custom_call_target="tpu_custom_call" | custom-call | tf_op jit(solution)/shard_map/pallas_call | solution.py:558
  (9 shorter events, 0.1 us)
Async XLA Ops:
  2.9 1.2 copy-start.4
  58.7 36.4 %copy-start.3 = (bf16[2,256,256]{2,1,0:T(8,128)(2,1)S(1)}, bf16[2,256,256]{2,1,0:T(8,128)(2,1)}, u32[]{:S(2)}) copy-start(bf16[2,256,256]{2,1,0:T(8,128)(2,1)} %param.10) | copy-start | bytes 786436
  59.0 38.6 %copy-start.2 = (bf16[1024,1024]{1,0:T(8,128)(2,1)}, bf16[1024,1024]{1,0:T(8,128)(2,1)S(1)}, u32[]{:S(2)}) copy-start(bf16[1024,1024]{1,0:T(8,128)(2,1)S(1)} %fusion.7.a_ref) | copy-start | bytes 6291460
  101.7 3.7 %copy-start = (bf16[1024,1024]{1,0:T(8,128)(2,1)S(1)}, bf16[1024,1024]{1,0:T(8,128)(2,1)}, u32[]{:S(2)}) copy-start(bf16[1024,1024]{1,0:T(8,128)(2,1)} %shard_map.48) | copy-start | bytes 6291460
  154.8 26.3 %copy-start.1 = (bf16[1024,1024]{1,0:T(8,128)(2,1)}, bf16[1024,1024]{1,0:T(8,128)(2,1)S(1)}, u32[]{:S(2)}) copy-start(bf16[1024,1024]{1,0:T(8,128)(2,1)S(1)} %fusion.5.a_ref) | copy-start | bytes 6291460
